TPU v7x, 32 devices: a whole 2x2x4 slice. The times are simulated.
32 devices in a mesh: groups: 2 (over x), row: 16 (over z, y, core).
Axes of the slice: x: 2, y: 2, z: 4, core: 2. Of those that a mesh axis runs over, the one named last changes fastest.
Arguments:
- factor_panel: bfloat16 [32768, 2048], P(('groups', 'row')), parts along dimension 0, may hold values from -0.25 to 0.25
- pivots: float32 [4096], P('groups'), parts along dimension 0, may hold values from 1 to 1.25
- right_sides: float32 [32768, 256], P(('groups', 'row')), parts along dimension 0, may hold values from -6 to 6
- block_home: int32 [32], replicated, may hold values from 0 to 31, each once
Outputs:
- remainder: float32 [32768, 256], P('groups', 'row'), parts along dimension 0
- psf_variance: float32 [512], P(('groups', 'row')), parts along dimension 0
There are 2 independent parts, one for each index of `groups`. A program takes and returns all parts, laid end to end along the dimension named above; an argument that names none is the same for every part. Nothing has to cross between parts.
Inputs may be any that keep to these rules, and one draw needn't show every extreme that they name: block_home[g] is the stored position of global block g; position p is slot p % 2 of row device p // 2; every position holds exactly one block.
All inputs are finite; a program needn't handle non-finite values.
Results may differ from a plain program's by a relative error of at most 0.0042.
Values may be sent and summed in bfloat16 or wider, within the bound.
No kernel may reach another device: no remote copies, remote signals or barrier semaphores. Data moves between devices by JAX's collectives and lax.ppermute only.
A program may use at most 128 MiB of HBM per device.

v0:
```python
import jax
import jax.numpy as jnp
from jax import lax
from jax.sharding import PartitionSpec as P

BLOCK = 512
STEPS = 4
PANEL = 2048


def spread(value, axis, source):
    kept = jnp.where(lax.axis_index(axis) == source, value, 0).astype(value.dtype)
    return lax.psum(kept, axis)


def on_device(factor_panel, pivots, right_sides, block_home):
    slot_count = factor_panel.shape[0] // BLOCK
    columns_all = right_sides.shape[1]
    row_count = lax.axis_size("row")
    row_index = lax.axis_index("row")
    block_total = block_home.shape[0]
    positions = row_index * slot_count + jnp.arange(slot_count, dtype=jnp.int32)
    global_ids = jnp.sum(
        jnp.where(
            block_home[None, :] == positions[:, None],
            jnp.arange(block_total, dtype=jnp.int32)[None, :],
            0,
        ),
        axis=1,
    )
    partial_value = right_sides.reshape(slot_count, BLOCK, columns_all)
    factor_blocks = factor_panel.reshape(slot_count, BLOCK, PANEL)
    my_columns = columns_all // row_count
    solutions = []
    for k in range(STEPS):
        slot = block_home[k] % slot_count
        rows = lax.dynamic_index_in_dim(partial_value, slot, 0, keepdims=False)
        diag_slot = block_home[k] % slot_count
        held = lax.dynamic_index_in_dim(factor_blocks, diag_slot, 0, keepdims=False)
        diag_rows = held[:, k * BLOCK : (k + 1) * BLOCK].astype(jnp.float32)
        diag_block = jnp.tril(diag_rows, -1) + jnp.diag(pivots[k * BLOCK : (k + 1) * BLOCK])
        solution = jax.scipy.linalg.solve_triangular(diag_block, rows, lower=True).astype(
            jnp.bfloat16
        )
        solution = spread(solution, "row", block_home[k] // slot_count)
        active = (global_ids > k).astype(jnp.float32)
        product = jnp.einsum(
            "sij,jc->sic",
            factor_blocks[:, :, k * BLOCK : (k + 1) * BLOCK],
            solution,
            preferred_element_type=jnp.float32,
        )
        partial_value = partial_value - active[:, None, None] * product
        partial_value = jnp.where(
            (global_ids == k)[:, None, None], solution.astype(jnp.float32)[None], partial_value
        )
        solutions.append(solution)
    stored = lax.all_to_all(
        partial_value.reshape(slot_count * BLOCK, columns_all),
        "row",
        split_axis=1,
        concat_axis=0,
        tiled=True,
    )
    ordered = jnp.take(stored.reshape(block_total, BLOCK, my_columns), block_home, axis=0)
    remainder = ordered.reshape(block_total * BLOCK, my_columns)
    solved = remainder[: STEPS * BLOCK]
    psf_variance = jnp.mean(solved * solved, axis=0)
    return (remainder, psf_variance)


def solution(mesh):
    in_specs = (P(("groups", "row"), None), P("groups"), P(("groups", "row"), None), P())
    out_specs = (P("groups", "row"), P(("groups", "row")))
    return jax.shard_map(
        on_device, mesh=mesh, in_specs=in_specs, out_specs=out_specs, check_vma=False
    )
```

profile of v0, /device:TPU:0, one launch (start us, length us, event | category | flops | bytes accessed | tf_op | source)
XLA Modules:
  0.0 518.6 jit_solution(8942205453289188810)
XLA Ops:
  17.5 4.3 dynamic-slice_bitcast_fusion.3
  21.9 2.0 fusion.19
  23.9 12.0 %while.8 = (s32[]{:T(128)}, f32[512,512]{1,0:T(8,128)}, s32[4,2]{0,1:T(2,128)S(1)}, f32[4,128,128]{2,1,0:T(8,128)S(1)}, s32[]{:T(128)}) while((s32[]{:T(128)}, f32[512,512]{1,0:T(8,128)}, s32[4,2]{0,1:T(2,128)S(1)}, f32[4,128,128]{2,1,0:T(8,128)S(1)}, s32[]{:T(128)}) %tuple.86), condition=%wide.while_cond, body=%wide.while_body.sunk | while | flops 2 | bytes 131181 | solution.py:42
  24.6 2.3 bitcast_dynamic-update-slice_fusion.8
  27.6 2.3 bitcast_dynamic-update-slice_fusion.8
  30.6 2.3 bitcast_dynamic-update-slice_fusion.8
  33.6 2.2 bitcast_dynamic-update-slice_fusion.8
  36.6 40.1 %custom-call.6 = f32[4,128,128]{1,2,0:T(8,128)S(1)} custom-call(f32[4,128,128]{2,1,0:T(8,128)} %copy-done.2), custom_call_target="InvertDiagBlocksLowerTriangular" | custom-call | tf_op jit(solution)/shard_map/jit(_solve_triangular)/triangular_solve | solution.py:42
  84.9 7.6 %while.9 = (s32[]{:T(128)}, f32[512,512]{1,0:T(8,128)S(1)}, s32[4,2]{0,1:T(2,128)S(1)}, f32[4,128,128]{2,1,0:T(8,128)S(1)}, s32[]{:T(128)}) while((s32[]{:T(128)}, f32[512,512]{1,0:T(8,128)S(1)}, s32[4,2]{0,1:T(2,128)S(1)}, f32[4,128,128]{2,1,0:T(8,128)S(1)}, s32[]{:T(128)}) %tuple.106), condition=%wide.while_cond.clone, body=%wide.while_body.clone.sunk | while | flops 2 | bytes 131181 | solution.py:42
  93.2 40.2 %custom-call.7 = f32[4,128,128]{1,2,0:T(8,128)S(1)} custom-call(f32[4,128,128]{2,1,0:T(8,128)} %copy-done.3), custom_call_target="InvertDiagBlocksLowerTriangular" | custom-call | tf_op jit(solution)/shard_map/jit(_solve_triangular)/triangular_solve | solution.py:42
  133.4 42.2 %all-reduce.5.cloned.1.call-done = bf16[512,256]{1,0:T(8,128)(2,1)} async-done(((bf16[512,256]{1,0:T(8,128)(2,1)}), bf16[512,256]{1,0:T(8,128)(2,1)}) %all-reduce.5.cloned.1.call-update) | async-done | bytes 262160 | tf_op jit(solution)/shard_map/psum | solution.py:13
  175.6 1.9 copy.55
  177.5 1.9 fusion.11
  185.7 11.1 %while.10 = (s32[]{:T(128)}, f32[512,512]{1,0:T(8,128)}, s32[4,2]{0,1:T(2,128)S(1)}, f32[4,128,128]{2,1,0:T(8,128)S(1)}, s32[]{:T(128)}) while((s32[]{:T(128)}, f32[512,512]{1,0:T(8,128)}, s32[4,2]{0,1:T(2,128)S(1)}, f32[4,128,128]{2,1,0:T(8,128)S(1)}, s32[]{:T(128)}) %tuple.107), condition=%wide.while_cond.clone.1, body=%wide.while_body.clone.1.sunk | while | flops 2 | bytes 131181 | solution.py:42
  186.3 2.2 bitcast_dynamic-update-slice_fusion.10
  189.1 2.2 bitcast_dynamic-update-slice_fusion.10
  191.9 2.2 bitcast_dynamic-update-slice_fusion.10
  194.7 2.1 bitcast_dynamic-update-slice_fusion.10
  197.4 39.3 %custom-call.8 = f32[4,128,128]{1,2,0:T(8,128)S(1)} custom-call(f32[4,128,128]{2,1,0:T(8,128)S(1)} %get-tuple-element.31), custom_call_target="InvertDiagBlocksLowerTriangular" | custom-call | tf_op jit(solution)/shard_map/jit(_solve_triangular)/triangular_solve | solution.py:42
  236.8 39.7 %all-reduce.7.cloned.1.call-done = bf16[512,256]{1,0:T(8,128)(2,1)} async-done(((bf16[512,256]{1,0:T(8,128)(2,1)}), bf16[512,256]{1,0:T(8,128)(2,1)}) %all-reduce.7.cloned.1.call-update) | async-done | bytes 262160 | tf_op jit(solution)/shard_map/psum | solution.py:13
  276.4 1.9 copy.59
  278.3 1.9 fusion.8
  286.3 8.3 %while.11 = (s32[]{:T(128)}, f32[512,512]{1,0:T(8,128)S(1)}, s32[4,2]{0,1:T(2,128)S(1)}, f32[4,128,128]{2,1,0:T(8,128)S(1)}, s32[]{:T(128)}) while((s32[]{:T(128)}, f32[512,512]{1,0:T(8,128)S(1)}, s32[4,2]{0,1:T(2,128)S(1)}, f32[4,128,128]{2,1,0:T(8,128)S(1)}, s32[]{:T(128)}) %tuple.108), condition=%wide.while_cond.clone.2, body=%wide.while_body.clone.2.sunk | while | flops 2 | bytes 131181 | solution.py:42
  295.3 39.3 %custom-call.9 = f32[4,128,128]{1,2,0:T(8,128)S(1)} custom-call(f32[4,128,128]{2,1,0:T(8,128)S(1)} %get-tuple-element.32), custom_call_target="InvertDiagBlocksLowerTriangular" | custom-call | tf_op jit(solution)/shard_map/jit(_solve_triangular)/triangular_solve | solution.py:42
  334.6 42.4 %all-reduce.9.cloned.1.call-done = bf16[512,256]{1,0:T(8,128)(2,1)} async-done(((bf16[512,256]{1,0:T(8,128)(2,1)}), bf16[512,256]{1,0:T(8,128)(2,1)}) %all-reduce.9.cloned.1.call-update) | async-done | bytes 262160 | tf_op jit(solution)/shard_map/psum | solution.py:13
  377.0 1.9 copy.62
  378.9 1.9 fusion.5
  384.1 90.4 %all-reduce.11.cloned.1.call-done = bf16[512,256]{1,0:T(8,128)(2,1)} async-done(((bf16[512,256]{1,0:T(8,128)(2,1)}), bf16[512,256]{1,0:T(8,128)(2,1)}) %all-reduce.11.cloned.1.call-update) | async-done | bytes 262160 | tf_op jit(solution)/shard_map/psum | solution.py:13
  475.6 1.8 fusion.2
  478.2 1.9 all_to_all.12
  480.1 5.2 %all-to-all-start = ((f32[1024,16,16]{0,2,1:T(8,128)}), f32[1024,16,16]{0,2,1:T(8,128)S(1)}, u32[]{:S(2)}, u32[]{:S(2)}) async-start(f32[1024,16,16]{0,2,1:T(8,128)} %all_to_all.12), calls=%async_computation | async-start | bytes 2097152 | tf_op jit(solution)/shard_map/all_to_all | solution.py:58
  485.4 22.7 %all-to-all-done = f32[1024,16,16]{0,2,1:T(8,128)S(1)} async-done(((f32[1024,16,16]{0,2,1:T(8,128)}), f32[1024,16,16]{0,2,1:T(8,128)S(1)}, u32[]{:S(2)}, u32[]{:S(2)}) %all-to-all-start) | async-done | bytes 1048608 | tf_op jit(solution)/shard_map/all_to_all | solution.py:58
  (125 shorter events, 53.1 us)
Async XLA Ops:
  7.2 168.4 %all-reduce.5.cloned.1.call-start = ((), (), s32[]{:S(2)}) async-start(), calls=%async_computation.1 | async-start | bytes 524288 | tf_op jit(solution)/shard_map/psum | solution.py:13
  21.8 54.9 %copy-start.1 = (f32[1024,256]{1,0:T(8,128)S(1)}, f32[1024,256]{1,0:T(8,128)}, u32[]{:S(2)}) copy-start(f32[1024,256]{1,0:T(8,128)} %param.8) | copy-start | bytes 3145732
  23.8 60.8 %copy-start.4 = (s32[32]{0:T(128)S(1)}, s32[32]{0:T(128)}, u32[]{:S(2)}) copy-start(s32[32]{0:T(128)} %param.9) | copy-start | bytes 388
  35.9 0.7 copy-start.2
  82.5 194.0 %all-reduce.7.cloned.1.call-start = ((), (), s32[]{:S(2)}) async-start(), calls=%async_computation.2 | async-start | bytes 524288 | tf_op jit(solution)/shard_map/psum | solution.py:13
  92.5 0.7 copy-start.3
  93.2 84.3 %copy-start = (f32[512,512]{1,0:T(8,128)}, f32[512,512]{1,0:T(8,128)S(1)}, u32[]{:S(2)}) copy-start(f32[512,512]{1,0:T(8,128)S(1)} %get-tuple-element.280) | copy-start | bytes 3145732
  185.4 191.6 %all-reduce.9.cloned.1.call-start = ((), (), s32[]{:S(2)}) async-start(), calls=%async_computation.3 | async-start | bytes 524288 | tf_op jit(solution)/shard_map/psum | solution.py:13
  286.2 188.3 %all-reduce.11.cloned.1.call-start = ((), (), s32[]{:S(2)}) async-start(), calls=%async_computation.4 | async-start | bytes 524288 | tf_op jit(solution)/shard_map/psum | solution.py:13
  480.1 28.1 %all-to-all-start = ((f32[1024,16,16]{0,2,1:T(8,128)}), f32[1024,16,16]{0,2,1:T(8,128)S(1)}, u32[]{:S(2)}, u32[]{:S(2)}) async-start(f32[1024,16,16]{0,2,1:T(8,128)} %all_to_all.12), calls=%async_computation | async-start | bytes 2097152 | tf_op jit(solution)/shard_map/all_to_all | solution.py:58
Sparse Core Ops, SparseCore 0:
  82.6 92.9 all-reduce.4
  185.5 90.8 all-reduce.6
  286.3 90.6 all-reduce.8
  384.2 90.2 all-reduce.10
where the time goes:
time: 521 us; the launch traced here: 519 us
  waiting for transfers between devices  237 us (45%)
  other arithmetic  166 us (32%)
  local copies, waits for them, and re-layouts  60.7 us (12%)
  between operations  24.4 us (5%)
  matrix products  24.3 us (5%)
  starting transfers between devices  5.53 us (1%)
    psum x4, waiting for transfers between devices, spread(): return lax.psum(kept, axis)  215 us
    another operation x6, other arithmetic, on_device(): jax.scipy.linalg.solve_triangular(diag_block, rows, lower=True)  161 us
    another operation x53, local copies, waits for them, and re-layouts, on_device(): jax.scipy.linalg.solve_triangular(diag_block, rows, lower=True)  38.8 us
    all_to_all x1, waiting for transfers between devices, on_device(): lax.all_to_all(partial_value.reshape(slot_count * BLOCK, columns_all), 'r...  22.7 us
    another operation x28, matrix products, on_device(): jax.scipy.linalg.solve_triangular(diag_block, rows, lower=True)  16.7 us
  transfers between devices with their start and end apart: 5, of which 5 were waited for; matrix products, arithmetic and copies ran while one was open for 28% of the time, Pallas kernels for 0%

commit v1 on v0

v1 whole, which is shorter than its diff:
```python
import functools

import jax
import jax.numpy as jnp
from jax import lax
from jax.experimental import pallas as pl
from jax.experimental.pallas import tpu as pltpu
from jax.sharding import PartitionSpec as P

BLOCK = 512
HALF = 256
STEPS = 4
PANEL = 2048
BF = jnp.bfloat16
F32 = jnp.float32
VMEM_LIMIT = 24 * 1024 * 1024


def mm(a, b):
    return jnp.dot(a, b, preferred_element_type=F32)


def mm_nt(a, b):
    return lax.dot_general(a, b, (((1,), (1,)), ((), ())), preferred_element_type=F32)


def parts(value):
    high = value.astype(BF)
    return high, (value - high.astype(F32)).astype(BF)


def mm3(a_high, a_low, b):
    b_high, b_low = parts(b)
    return mm(a_high, b_high) + (mm(a_high, b_low) + mm(a_low, b_high))


def invert(tiles, pivot_rows):
    shape = tiles[0].shape
    row = lax.broadcasted_iota(jnp.int32, shape, 0)
    col = lax.broadcasted_iota(jnp.int32, shape, 1)
    apart = row ^ col
    lower = row > col
    inverses = []
    for tile, pivot in zip(tiles, pivot_rows):
        across = 1.0 / pivot
        diag = jnp.where(row == col, across, 0.0)
        down = jnp.sum(diag, axis=1, keepdims=True)
        first = jnp.where((apart == 1) & lower, tile.astype(F32), 0.0)
        inverses.append(diag - down * first * across)
    halves = [parts(value) for value in inverses]
    bit = 1
    while (2 << bit) <= shape[0]:
        mask = (lax.shift_right_logical(apart, bit) == 1) & lower
        for at, tile in enumerate(tiles):
            high, low = halves[at]
            link = jnp.where(mask, tile.astype(F32), 0.0).astype(BF)
            inner = mm(link, high) + mm(link, low)
            inverses[at] = inverses[at] - mm3(high, low, inner)
            halves[at] = parts(inverses[at])
        bit += 1
    return halves


def solve(tile_cross, inv, rows):
    (a_high, a_low), (b_high, b_low) = inv
    top = mm3(a_high, a_low, rows[:HALF])
    top_high, top_low = parts(top)
    rest = rows[HALF:] - (mm(tile_cross, top_high) + mm(tile_cross, top_low))
    return top.astype(BF), mm3(b_high, b_low, rest).astype(BF)


def put_halves(core, top, bottom, keep_ref, send_ref):
    first = core == 0
    keep_ref[...] = jnp.where(first, top, bottom)
    send_ref[...] = jnp.where(first, bottom, top)


def first_kernel(slots, home, factor, pivots, rows, inv_high, inv_low, keep, send):
    me = lax.axis_index("row")
    core = me % 2

    def one_slot(slot, carry):
        spot = me * slots + slot
        which = jnp.int32(-1)
        for k in range(STEPS):
            which = jnp.where(home[k] == spot, k, which)

        @pl.when(which >= 0)
        def _():
            r0 = pl.multiple_of(slot * BLOCK, BLOCK)
            c0 = pl.multiple_of(which * BLOCK, BLOCK)
            tiles = [
                factor[pl.ds(r0 + h * HALF, HALF), pl.ds(c0 + h * HALF, HALF)]
                for h in range(2)
            ]
            pivot_rows = [pivots[:, pl.ds(c0 + h * HALF, HALF)] for h in range(2)]
            for h, (high, low) in enumerate(invert(tiles, pivot_rows)):
                inv_high[slot, h] = high
                inv_low[slot, h] = low

        return carry

    lax.fori_loop(0, slots, one_slot, 0)
    finish(0, slots, home, factor, rows, inv_high, inv_low, [], keep, send)


def finish(k, slots, home, factor, rows, inv_high, inv_low, solved, keep, send):
    me = lax.axis_index("row")
    core = me % 2
    mine = home[k] // slots == me

    @pl.when(mine)
    def _():
        slot = home[k] % slots
        r0 = pl.multiple_of(slot * BLOCK, BLOCK)
        value = rows[pl.ds(r0, BLOCK), :]
        for j, pair in enumerate(solved):
            for turn, half in enumerate(pair):
                at = core if turn == 0 else 1 - core
                c0 = pl.multiple_of(j * BLOCK + at * HALF, HALF)
                value = value - mm(factor[pl.ds(r0, BLOCK), pl.ds(c0, HALF)], half[...])
        cross = factor[pl.ds(r0 + HALF, HALF), pl.ds(k * BLOCK, HALF)]
        inv = [(inv_high[slot, h], inv_low[slot, h]) for h in range(2)]
        top, bottom = solve(cross, inv, value)
        put_halves(core, top, bottom, keep, send)

    @pl.when(jnp.logical_not(mine))
    def _():
        keep[...] = jnp.zeros_like(keep)
        send[...] = jnp.zeros_like(send)


def step_kernel(k, slots, home, factor, rows, inv_high, inv_low, *refs):
    solved = [(refs[2 * j], refs[2 * j + 1]) for j in range(k)]
    keep, send = refs[2 * k :]
    finish(k, slots, home, factor, rows, inv_high, inv_low, solved, keep, send)


def last_kernel(slots, home, factor, rows, *refs):
    me = lax.axis_index("row")
    core = me % 2
    solved = [(refs[2 * j], refs[2 * j + 1]) for j in range(STEPS)]
    out = refs[2 * STEPS]
    eye_shape = (HALF, HALF)
    eye = (
        lax.broadcasted_iota(jnp.int32, eye_shape, 0)
        == lax.broadcasted_iota(jnp.int32, eye_shape, 1)
    ).astype(F32).astype(BF)
    columns = rows.shape[1]

    def chunk(at, carry):
        r0 = pl.multiple_of(at * HALF, HALF)
        value = rows[pl.ds(r0, HALF), :]
        for j, pair in enumerate(solved):
            for turn, half in enumerate(pair):
                where = core if turn == 0 else 1 - core
                c0 = pl.multiple_of(j * BLOCK + where * HALF, HALF)
                value = value - mm(factor[pl.ds(r0, HALF), pl.ds(c0, HALF)], half[...])
        value = value.astype(BF)
        for c in range(0, columns, HALF):
            out[c : c + HALF, pl.ds(r0, HALF)] = mm_nt(eye, value[:, c : c + HALF]).astype(BF)
        return carry

    lax.fori_loop(0, rows.shape[0] // HALF, chunk, 0)


def order_kernel(slots, width, home, arrived, *refs):
    me = lax.axis_index("row")
    core = me % 2
    solved = [(refs[2 * j], refs[2 * j + 1]) for j in range(STEPS)]
    out, variance = refs[2 * STEPS :]
    columns = solved[0][0].shape[1]
    pick = (
        lax.broadcasted_iota(jnp.int32, (width, columns), 1)
        == lax.broadcasted_iota(jnp.int32, (width, columns), 0) + me * width
    ).astype(F32).astype(BF)
    total = jnp.zeros((width, 1), F32)
    for j, pair in enumerate(solved):
        for turn, half in enumerate(pair):
            where = core if turn == 0 else 1 - core
            c0 = pl.multiple_of(j * BLOCK + where * HALF, HALF)
            value = mm_nt(pick, half[...])
            out[:, pl.ds(c0, HALF)] = value
            total = total + jnp.sum(value * value, axis=1, keepdims=True)
    variance[...] = jnp.broadcast_to(total * (1.0 / (STEPS * BLOCK)), variance.shape)
    blocks = out.shape[1] // BLOCK

    def place(g, carry):
        spot = home[g]
        r0 = pl.multiple_of((spot // slots) * width, width)
        c0 = pl.multiple_of((spot % slots) * BLOCK, BLOCK)
        o0 = pl.multiple_of(g * BLOCK, BLOCK)
        out[:, pl.ds(o0, BLOCK)] = arrived[pl.ds(r0, width), pl.ds(c0, BLOCK)].astype(F32)
        return carry

    lax.fori_loop(STEPS, blocks, place, 0)


def call(kernel, count, outs, flops=0, moved=0):
    vmem = pl.BlockSpec(memory_space=pltpu.VMEM)
    return pl.pallas_call(
        kernel,
        grid_spec=pltpu.PrefetchScalarGridSpec(
            num_scalar_prefetch=1,
            in_specs=[vmem] * count,
            out_specs=[vmem] * len(outs),
        ),
        out_shape=outs,
        compiler_params=pltpu.CompilerParams(vmem_limit_bytes=VMEM_LIMIT),
        cost_estimate=pl.CostEstimate(flops=flops, bytes_accessed=moved, transcendentals=0),
    )


def hop(value, count, mask):
    return lax.ppermute(value, "row", [(i, i ^ mask) for i in range(count)])


def spread(keep, send, count):
    mine = keep + hop(send, count, 1)
    if count >= 8:
        mine = mine + hop(mine, count, 2) + hop(mine, count, 4) + hop(mine, count, 6)
        mask = 8
    else:
        mask = 2
    while mask < count:
        mine = mine + hop(mine, count, mask)
        mask *= 2
    return mine, hop(mine, count, 1)


def on_device(factor_panel, pivots, right_sides, block_home):
    slots = factor_panel.shape[0] // BLOCK
    columns = right_sides.shape[1]
    count = lax.axis_size("row")
    width = columns // count
    blocks = block_home.shape[0]
    half = jax.ShapeDtypeStruct((HALF, columns), BF)
    inverse = jax.ShapeDtypeStruct((slots, 2, HALF, HALF), BF)
    inv_high, inv_low, keep, send = call(
        functools.partial(first_kernel, slots), 3, [inverse, inverse, half, half]
    )(block_home, factor_panel, pivots.reshape(1, PANEL), right_sides)
    solved = list(spread(keep, send, count))
    for k in range(1, STEPS):
        keep, send = call(functools.partial(step_kernel, k, slots), 4 + 2 * k, [half, half])(
            block_home, factor_panel, right_sides, inv_high, inv_low, *solved
        )
        solved += spread(keep, send, count)
    (turned,) = call(
        functools.partial(last_kernel, slots),
        2 + 2 * STEPS,
        [jax.ShapeDtypeStruct((columns, slots * BLOCK), BF)],
    )(block_home, factor_panel, right_sides, *solved)
    arrived = lax.all_to_all(turned, "row", split_axis=0, concat_axis=0, tiled=True)
    out, variance = call(
        functools.partial(order_kernel, slots, width),
        1 + 2 * STEPS,
        [
            jax.ShapeDtypeStruct((width, blocks * BLOCK), F32),
            jax.ShapeDtypeStruct((width, 128), F32),
        ],
    )(block_home, arrived, *solved)
    return out.T, variance[:, 0]


def solution(mesh):
    in_specs = (P(("groups", "row"), None), P("groups"), P(("groups", "row"), None), P())
    out_specs = (P("groups", "row"), P(("groups", "row")))
    return jax.shard_map(
        on_device, mesh=mesh, in_specs=in_specs, out_specs=out_specs, check_vma=False
    )
```

time: 521 us -> 124 us (0.24)
  waiting for transfers between devices: 237 us -> 62.8 us
  other arithmetic: 166 us -> 0.39 us
  local copies, waits for them, and re-layouts: 60.7 us -> 5.38 us
  matrix products: 24.3 us -> 0 us
  between operations: 24.4 us -> 0.78 us
  starting transfers between devices: 5.53 us -> 28.7 us
  blocking collectives: 0 us -> 18.4 us
  Pallas kernels: 0 us -> 7.98 us
    psum x4 -> x0, waiting for transfers between devices: 215 us -> none  [spread(): return lax.psum(kept, axis)]
    another operation x6 -> x0, other arithmetic: 161 us -> none  [on_device(): jax.scipy.linalg.solve_triangular(diag_block, rows, lower=True)]
    ppermute x0 -> x24, waiting for transfers between devices: none -> 62.8 us  [hop(): return lax.ppermute(value, 'row', [(i, i ^ mask) for i in range(count)])]
    another operation x53 -> x0, local copies, waits for them, and re-layouts: 38.8 us -> none  [on_device(): jax.scipy.linalg.solve_triangular(diag_block, rows, lower=True)]
    ppermute x0 -> x24, starting transfers between devices: none -> 28.7 us  [hop(): return lax.ppermute(value, 'row', [(i, i ^ mask) for i in range(count)])]
    all_to_all x1 -> x0, waiting for transfers between devices: 22.7 us -> none  [on_device(): lax.all_to_all(partial_value.reshape(slot_count * BLOCK, columns_all), 'r...]
    all_to_all x0 -> x1, blocking collectives: none -> 18.4 us  [on_device(): lax.all_to_all(turned, 'row', split_axis=0, concat_axis=0, tiled=True)]
    another operation x28 -> x0, matrix products: 16.7 us -> none  [on_device(): jax.scipy.linalg.solve_triangular(diag_block, rows, lower=True)]
  transfers between devices with their start and end apart: 5 -> 24, of which waited for: 5 -> 19; matrix products, arithmetic and copies ran while one was open for 28% -> 0% of each run, Pallas kernels for 0% -> 0%
where the time goes in v1:
time: 124 us
  waiting for transfers between devices  62.8 us (51%)
  starting transfers between devices  28.7 us (23%)
  blocking collectives  18.4 us (15%)
  Pallas kernels  7.98 us (6%)
  local copies, waits for them, and re-layouts  5.38 us (4%)
    ppermute x24, waiting for transfers between devices, hop(): return lax.ppermute(value, 'row', [(i, i ^ mask) for i in range(count)])  62.8 us
    ppermute x24, starting transfers between devices, hop(): return lax.ppermute(value, 'row', [(i, i ^ mask) for i in range(count)])  28.7 us
    all_to_all x1, blocking collectives, on_device(): lax.all_to_all(turned, 'row', split_axis=0, concat_axis=0, tiled=True)  18.4 us
    unnamed x10, local copies, waits for them, and re-layouts  4.76 us
    pallas_call x1, Pallas kernels, on_device(): call(functools.partial(last_kernel, slots), 2 + 2 * STEPS, [jax.ShapeDtyp...  3.25 us
  transfers between devices with their start and end apart: 24, of which 19 were waited for; matrix products, arithmetic and copies ran while one was open for 0% of the time, Pallas kernels for 0%

profile of v1, /device:TPU:0, one launch (start us, length us, event | category | flops | bytes accessed | tf_op | source)
XLA Modules:
  0.0 124.4 jit_solution(14575793935206586189)
XLA Ops:
  0.6 2.2 %copy-done = bf16[1024,2048]{1,0:T(8,128)(2,1)S(1)} copy-done((bf16[1024,2048]{1,0:T(8,128)(2,1)S(1)}, bf16[1024,2048]{1,0:T(8,128)(2,1)}, u32[]{:S(2)}) %copy-start) | copy-done | bytes 4194328
  2.8 1.2 copy-done.1
  7.6 3.9 %collective-permute-start.3 = (bf16[256,256]{1,0:T(8,128)(2,1)S(1)}, bf16[256,256]{1,0:T(8,128)(2,1)S(1)}, u32[]{:S(2)}, u32[]{:S(2)}) collective-permute-start(bf16[256,256]{1,0:T(8,128)(2,1)S(1)} %add.60), channel_id=1, source_target_pairs={{0,6},{1,7},{2,4},{3,5},{4,2},{5,3},{6,0},{7,1},{8,14},{9,15},{10,... | collective-permute-start | bytes 393224 | tf_op jit(solution)/shard_map/ppermute | solution.py:215
  11.5 5.0 %collective-permute-start.2 = (bf16[256,256]{1,0:T(8,128)(2,1)S(1)}, bf16[256,256]{1,0:T(8,128)(2,1)S(1)}, u32[]{:S(2)}, u32[]{:S(2)}) collective-permute-start(bf16[256,256]{1,0:T(8,128)(2,1)S(1)} %add.60), channel_id=1, source_target_pairs={{0,4},{1,5},{2,6},{3,7},{4,0},{5,1},{6,2},{7,3},{8,12},{9,13},{10,... | collective-permute-start | bytes 393224 | tf_op jit(solution)/shard_map/ppermute | solution.py:215
  16.6 6.3 %collective-permute-done.2 = bf16[256,256]{1,0:T(8,128)(2,1)S(1)} collective-permute-done((bf16[256,256]{1,0:T(8,128)(2,1)S(1)}, bf16[256,256]{1,0:T(8,128)(2,1)S(1)}, u32[]{:S(2)}, u32[]{:S(2)}) %collective-permute-start.2) | collective-permute-done | bytes 131104 | tf_op jit(solution)/shard_map/ppermute | solution.py:215
  22.9 3.3 %collective-permute-start.4 = (bf16[256,256]{1,0:T(8,128)(2,1)S(1)}, bf16[256,256]{1,0:T(8,128)(2,1)S(1)}, u32[]{:S(2)}, u32[]{:S(2)}) collective-permute-start(bf16[256,256]{1,0:T(8,128)(2,1)S(1)} %add_add_fusion.3), channel_id=1, source_target_pairs={{0,8},{1,9},{2,10},{3,11},{4,12},{5,13},{6,14},{7,15},{8,0},{9,1},... | collective-permute-start | bytes 393224 | tf_op jit(solution)/shard_map/ppermute | solution.py:215
  26.3 6.4 %collective-permute-done.4 = bf16[256,256]{1,0:T(8,128)(2,1)S(1)} collective-permute-done((bf16[256,256]{1,0:T(8,128)(2,1)S(1)}, bf16[256,256]{1,0:T(8,128)(2,1)S(1)}, u32[]{:S(2)}, u32[]{:S(2)}) %collective-permute-start.4) | collective-permute-done | bytes 131104 | tf_op jit(solution)/shard_map/ppermute | solution.py:215
  32.8 1.3 %collective-permute-done.5.refs_1_ = bf16[256,256]{1,0:T(8,128)(2,1)S(1)} collective-permute-done((bf16[256,256]{1,0:T(8,128)(2,1)S(1)}, bf16[256,256]{1,0:T(8,128)(2,1)S(1)}, u32[]{:S(2)}, u32[]{:S(2)}) %collective-permute-start.5) | collective-permute-done | bytes 131104 | tf_op jit(solution)/shard_map/ppermute | solution.py:215
  35.0 1.2 collective-permute-done.6
  37.2 2.7 %collective-permute-start.8 = (bf16[256,256]{1,0:T(8,128)(2,1)S(1)}, bf16[256,256]{1,0:T(8,128)(2,1)S(1)}, u32[]{:S(2)}, u32[]{:S(2)}) collective-permute-start(bf16[256,256]{1,0:T(8,128)(2,1)S(1)} %add.65), channel_id=1, source_target_pairs={{0,4},{1,5},{2,6},{3,7},{4,0},{5,1},{6,2},{7,3},{8,12},{9,13},{10,... | collective-permute-start | bytes 393224 | tf_op jit(solution)/shard_map/ppermute | solution.py:215
  39.9 3.7 %collective-permute-done.9 = bf16[256,256]{1,0:T(8,128)(2,1)S(1)} collective-permute-done((bf16[256,256]{1,0:T(8,128)(2,1)S(1)}, bf16[256,256]{1,0:T(8,128)(2,1)S(1)}, u32[]{:S(2)}, u32[]{:S(2)}) %collective-permute-start.9) | collective-permute-done | bytes 131104 | tf_op jit(solution)/shard_map/ppermute | solution.py:215
  43.5 2.7 %collective-permute-done.8 = bf16[256,256]{1,0:T(8,128)(2,1)S(1)} collective-permute-done((bf16[256,256]{1,0:T(8,128)(2,1)S(1)}, bf16[256,256]{1,0:T(8,128)(2,1)S(1)}, u32[]{:S(2)}, u32[]{:S(2)}) %collective-permute-start.8) | collective-permute-done | bytes 131104 | tf_op jit(solution)/shard_map/ppermute | solution.py:215
  46.2 1.0 collective-permute-start.10
  47.3 7.4 %collective-permute-done.10 = bf16[256,256]{1,0:T(8,128)(2,1)S(1)} collective-permute-done((bf16[256,256]{1,0:T(8,128)(2,1)S(1)}, bf16[256,256]{1,0:T(8,128)(2,1)S(1)}, u32[]{:S(2)}, u32[]{:S(2)}) %collective-permute-start.10) | collective-permute-done | bytes 131104 | tf_op jit(solution)/shard_map/ppermute | solution.py:215
  54.8 1.3 %collective-permute-done.11.refs_3_ = bf16[256,256]{1,0:T(8,128)(2,1)S(1)} collective-permute-done((bf16[256,256]{1,0:T(8,128)(2,1)S(1)}, bf16[256,256]{1,0:T(8,128)(2,1)S(1)}, u32[]{:S(2)}, u32[]{:S(2)}) %collective-permute-start.11) | collective-permute-done | bytes 131104 | tf_op jit(solution)/shard_map/ppermute | solution.py:215
  57.0 1.2 collective-permute-done.12
  58.3 3.1 %collective-permute-start.14 = (bf16[256,256]{1,0:T(8,128)(2,1)S(1)}, bf16[256,256]{1,0:T(8,128)(2,1)S(1)}, u32[]{:S(2)}, u32[]{:S(2)}) collective-permute-start(bf16[256,256]{1,0:T(8,128)(2,1)S(1)} %add.70), channel_id=1, source_target_pairs={{0,4},{1,5},{2,6},{3,7},{4,0},{5,1},{6,2},{7,3},{8,12},{9,13},{10,... | collective-permute-start | bytes 393224 | tf_op jit(solution)/shard_map/ppermute | solution.py:215
  61.7 3.8 %collective-permute-done.15 = bf16[256,256]{1,0:T(8,128)(2,1)S(1)} collective-permute-done((bf16[256,256]{1,0:T(8,128)(2,1)S(1)}, bf16[256,256]{1,0:T(8,128)(2,1)S(1)}, u32[]{:S(2)}, u32[]{:S(2)}) %collective-permute-start.15) | collective-permute-done | bytes 131104 | tf_op jit(solution)/shard_map/ppermute | solution.py:215
  65.5 2.2 %collective-permute-done.14 = bf16[256,256]{1,0:T(8,128)(2,1)S(1)} collective-permute-done((bf16[256,256]{1,0:T(8,128)(2,1)S(1)}, bf16[256,256]{1,0:T(8,128)(2,1)S(1)}, u32[]{:S(2)}, u32[]{:S(2)}) %collective-permute-start.14) | collective-permute-done | bytes 131104 | tf_op jit(solution)/shard_map/ppermute | solution.py:215
  67.8 2.0 %collective-permute-start.16 = (bf16[256,256]{1,0:T(8,128)(2,1)S(1)}, bf16[256,256]{1,0:T(8,128)(2,1)S(1)}, u32[]{:S(2)}, u32[]{:S(2)}) collective-permute-start(bf16[256,256]{1,0:T(8,128)(2,1)S(1)} %add_add_fusion.1), channel_id=1, source_target_pairs={{0,8},{1,9},{2,10},{3,11},{4,12},{5,13},{6,14},{7,15},{8,0},{9,1},... | collective-permute-start | bytes 393224 | tf_op jit(solution)/shard_map/ppermute | solution.py:215
  69.8 6.6 %collective-permute-done.16 = bf16[256,256]{1,0:T(8,128)(2,1)S(1)} collective-permute-done((bf16[256,256]{1,0:T(8,128)(2,1)S(1)}, bf16[256,256]{1,0:T(8,128)(2,1)S(1)}, u32[]{:S(2)}, u32[]{:S(2)}) %collective-permute-start.16) | collective-permute-done | bytes 131104 | tf_op jit(solution)/shard_map/ppermute | solution.py:215
  76.4 1.3 %collective-permute-done.17.refs_5_ = bf16[256,256]{1,0:T(8,128)(2,1)S(1)} collective-permute-done((bf16[256,256]{1,0:T(8,128)(2,1)S(1)}, bf16[256,256]{1,0:T(8,128)(2,1)S(1)}, u32[]{:S(2)}, u32[]{:S(2)}) %collective-permute-start.17) | collective-permute-done | bytes 131104 | tf_op jit(solution)/shard_map/ppermute | solution.py:215
  78.6 1.2 collective-permute-done.18
  80.3 3.1 %collective-permute-start.20 = (bf16[256,256]{1,0:T(8,128)(2,1)S(1)}, bf16[256,256]{1,0:T(8,128)(2,1)S(1)}, u32[]{:S(2)}, u32[]{:S(2)}) collective-permute-start(bf16[256,256]{1,0:T(8,128)(2,1)S(1)} %add.75), channel_id=1, source_target_pairs={{0,4},{1,5},{2,6},{3,7},{4,0},{5,1},{6,2},{7,3},{8,12},{9,13},{10,... | collective-permute-start | bytes 393224 | tf_op jit(solution)/shard_map/ppermute | solution.py:215
  83.4 3.7 %collective-permute-done.21 = bf16[256,256]{1,0:T(8,128)(2,1)S(1)} collective-permute-done((bf16[256,256]{1,0:T(8,128)(2,1)S(1)}, bf16[256,256]{1,0:T(8,128)(2,1)S(1)}, u32[]{:S(2)}, u32[]{:S(2)}) %collective-permute-start.21) | collective-permute-done | bytes 131104 | tf_op jit(solution)/shard_map/ppermute | solution.py:215
  87.1 2.6 %collective-permute-done.20 = bf16[256,256]{1,0:T(8,128)(2,1)S(1)} collective-permute-done((bf16[256,256]{1,0:T(8,128)(2,1)S(1)}, bf16[256,256]{1,0:T(8,128)(2,1)S(1)}, u32[]{:S(2)}, u32[]{:S(2)}) %collective-permute-start.20) | collective-permute-done | bytes 131104 | tf_op jit(solution)/shard_map/ppermute | solution.py:215
  89.8 1.1 collective-permute-start.22
  90.9 7.4 %collective-permute-done.22 = bf16[256,256]{1,0:T(8,128)(2,1)S(1)} collective-permute-done((bf16[256,256]{1,0:T(8,128)(2,1)S(1)}, bf16[256,256]{1,0:T(8,128)(2,1)S(1)}, u32[]{:S(2)}, u32[]{:S(2)}) %collective-permute-start.22) | collective-permute-done | bytes 131104 | tf_op jit(solution)/shard_map/ppermute | solution.py:215
  98.4 1.3 %collective-permute-done.23.refs_7_ = bf16[256,256]{1,0:T(8,128)(2,1)S(1)} collective-permute-done((bf16[256,256]{1,0:T(8,128)(2,1)S(1)}, bf16[256,256]{1,0:T(8,128)(2,1)S(1)}, u32[]{:S(2)}, u32[]{:S(2)}) %collective-permute-start.23) | collective-permute-done | bytes 131104 | tf_op jit(solution)/shard_map/ppermute | solution.py:215
  99.7 3.3 %shard_map.63 = bf16[256,1024]{1,0:T(8,128)(2,1)S(1)} custom-call(s32[32]{0:T(128)S(1)} %copy-done.3, bf16[1024,2048]{1,0:T(8,128)(2,1)S(1)} %copy-done, f32[1024,256]{1,0:T(8,128)S(1)} %copy-done.2, bf16[256,256]{1,0:T(8,128)(2,1)S(1)} %add.64.refs_0_, bf16[256,256]{1,0:T(8,128)(2,1)S(1)} %collective-permute-done.5.refs_1_, ...), custom_call_target="tpu_custom_call" | custom-call | tf_op jit(solution)/shard_map/pallas_call | solution.py:248
  103.0 18.4 %all_to_all.11 = bf16[16,16,1024]{2,1,0:T(8,128)(2,1)S(1)} all-to-all(bf16[16,16,1024]{2,1,0:T(8,128)(2,1)S(1)} %bitcast.5), channel_id=1, replica_groups=mesh['groups'=2,'row'=16] {'row'}, dimensions={0} | all-to-all | bytes 1048576 | tf_op jit(solution)/shard_map/all_to_all | solution.py:253
  121.4 2.4 %shard_map.64 = (f32[16,16384]{1,0:T(8,128)}, f32[16,128]{1,0:T(8,128)S(1)}) custom-call(s32[32]{0:T(128)S(1)} %copy-done.3, bf16[256,1024]{1,0:T(8,128)(2,1)S(1)} %bitcast.4, bf16[256,256]{1,0:T(8,128)(2,1)S(1)} %add.64.refs_0_, bf16[256,256]{1,0:T(8,128)(2,1)S(1)} %collective-permute-done.5.refs_1_, bf16[256,256]{1,0:T(8,128)(2,1)S(1)} %add.69.refs_2_, ...), custom_call_target="tpu_custom_call" | custom-call | tf_op jit(solution)/shard_map/pallas_call | solution.py:254
  (46 shorter events, 9.2 us)
Async XLA Ops:
  0.6 2.2 %copy-start = (bf16[1024,2048]{1,0:T(8,128)(2,1)S(1)}, bf16[1024,2048]{1,0:T(8,128)(2,1)}, u32[]{:S(2)}) copy-start(bf16[1024,2048]{1,0:T(8,128)(2,1)} %factor.9) | copy-start | bytes 12582916
  2.8 1.2 copy-start.1
  4.0 0.7 copy-start.3
  4.7 0.7 copy-start.4
  5.4 28.8 %copy-start.2 = (f32[1024,256]{1,0:T(8,128)S(1)}, f32[1024,256]{1,0:T(8,128)}, u32[]{:S(2)}) copy-start(f32[1024,256]{1,0:T(8,128)} %rows.9) | copy-start | bytes 3145732
  6.0 1.5 %collective-permute-start = (bf16[256,256]{1,0:T(8,128)(2,1)S(1)}, bf16[256,256]{1,0:T(8,128)(2,1)S(1)}, u32[]{:S(2)}, u32[]{:S(2)}) collective-permute-start(bf16[256,256]{1,0:T(8,128)(2,1)S(1)} %get-tuple-element.15), channel_id=1, source_target_pairs={{0,1},{1,0},{2,3},{3,2},{4,5},{5,4},{6,7},{7,6},{8,9},{9,8},{10,11... | collective-permute-start | bytes 393224 | tf_op jit(solution)/shard_map/ppermute | solution.py:215
  7.6 9.0 %collective-permute-start.3 = (bf16[256,256]{1,0:T(8,128)(2,1)S(1)}, bf16[256,256]{1,0:T(8,128)(2,1)S(1)}, u32[]{:S(2)}, u32[]{:S(2)}) collective-permute-start(bf16[256,256]{1,0:T(8,128)(2,1)S(1)} %add.60), channel_id=1, source_target_pairs={{0,6},{1,7},{2,4},{3,5},{4,2},{5,3},{6,0},{7,1},{8,14},{9,15},{10,... | collective-permute-start | bytes 393224 | tf_op jit(solution)/shard_map/ppermute | solution.py:215
  11.5 11.4 %collective-permute-start.2 = (bf16[256,256]{1,0:T(8,128)(2,1)S(1)}, bf16[256,256]{1,0:T(8,128)(2,1)S(1)}, u32[]{:S(2)}, u32[]{:S(2)}) collective-permute-start(bf16[256,256]{1,0:T(8,128)(2,1)S(1)} %add.60), channel_id=1, source_target_pairs={{0,4},{1,5},{2,6},{3,7},{4,0},{5,1},{6,2},{7,3},{8,12},{9,13},{10,... | collective-permute-start | bytes 393224 | tf_op jit(solution)/shard_map/ppermute | solution.py:215
  16.5 6.4 %collective-permute-start.1 = (bf16[256,256]{1,0:T(8,128)(2,1)S(1)}, bf16[256,256]{1,0:T(8,128)(2,1)S(1)}, u32[]{:S(2)}, u32[]{:S(2)}) collective-permute-start(bf16[256,256]{1,0:T(8,128)(2,1)S(1)} %add.60), channel_id=1, source_target_pairs={{0,2},{1,3},{2,0},{3,1},{4,6},{5,7},{6,4},{7,5},{8,10},{9,11},{10,... | collective-permute-start | bytes 393224 | tf_op jit(solution)/shard_map/ppermute | solution.py:215
  22.9 9.8 %collective-permute-start.4 = (bf16[256,256]{1,0:T(8,128)(2,1)S(1)}, bf16[256,256]{1,0:T(8,128)(2,1)S(1)}, u32[]{:S(2)}, u32[]{:S(2)}) collective-permute-start(bf16[256,256]{1,0:T(8,128)(2,1)S(1)} %add_add_fusion.3), channel_id=1, source_target_pairs={{0,8},{1,9},{2,10},{3,11},{4,12},{5,13},{6,14},{7,15},{8,0},{9,1},... | collective-permute-start | bytes 393224 | tf_op jit(solution)/shard_map/ppermute | solution.py:215
  32.8 1.4 %collective-permute-start.5 = (bf16[256,256]{1,0:T(8,128)(2,1)S(1)}, bf16[256,256]{1,0:T(8,128)(2,1)S(1)}, u32[]{:S(2)}, u32[]{:S(2)}) collective-permute-start(bf16[256,256]{1,0:T(8,128)(2,1)S(1)} %add.64.refs_0_), channel_id=1, source_target_pairs={{0,1},{1,0},{2,3},{3,2},{4,5},{5,4},{6,7},{7,6},{8,9},{9,8},{10,11... | collective-permute-start | bytes 393224 | tf_op jit(solution)/shard_map/ppermute | solution.py:215
  34.8 1.4 %collective-permute-start.6 = (bf16[256,256]{1,0:T(8,128)(2,1)S(1)}, bf16[256,256]{1,0:T(8,128)(2,1)S(1)}, u32[]{:S(2)}, u32[]{:S(2)}) collective-permute-start(bf16[256,256]{1,0:T(8,128)(2,1)S(1)} %get-tuple-element.19), channel_id=1, source_target_pairs={{0,1},{1,0},{2,3},{3,2},{4,5},{5,4},{6,7},{7,6},{8,9},{9,8},{10,11... | collective-permute-start | bytes 393224 | tf_op jit(solution)/shard_map/ppermute | solution.py:215
  36.2 7.3 %collective-permute-start.9 = (bf16[256,256]{1,0:T(8,128)(2,1)S(1)}, bf16[256,256]{1,0:T(8,128)(2,1)S(1)}, u32[]{:S(2)}, u32[]{:S(2)}) collective-permute-start(bf16[256,256]{1,0:T(8,128)(2,1)S(1)} %add.65), channel_id=1, source_target_pairs={{0,6},{1,7},{2,4},{3,5},{4,2},{5,3},{6,0},{7,1},{8,14},{9,15},{10,... | collective-permute-start | bytes 393224 | tf_op jit(solution)/shard_map/ppermute | solution.py:215
  37.2 9.0 %collective-permute-start.8 = (bf16[256,256]{1,0:T(8,128)(2,1)S(1)}, bf16[256,256]{1,0:T(8,128)(2,1)S(1)}, u32[]{:S(2)}, u32[]{:S(2)}) collective-permute-start(bf16[256,256]{1,0:T(8,128)(2,1)S(1)} %add.65), channel_id=1, source_target_pairs={{0,4},{1,5},{2,6},{3,7},{4,0},{5,1},{6,2},{7,3},{8,12},{9,13},{10,... | collective-permute-start | bytes 393224 | tf_op jit(solution)/shard_map/ppermute | solution.py:215
  39.8 6.4 %collective-permute-start.7 = (bf16[256,256]{1,0:T(8,128)(2,1)S(1)}, bf16[256,256]{1,0:T(8,128)(2,1)S(1)}, u32[]{:S(2)}, u32[]{:S(2)}) collective-permute-start(bf16[256,256]{1,0:T(8,128)(2,1)S(1)} %add.65), channel_id=1, source_target_pairs={{0,2},{1,3},{2,0},{3,1},{4,6},{5,7},{6,4},{7,5},{8,10},{9,11},{10,... | collective-permute-start | bytes 393224 | tf_op jit(solution)/shard_map/ppermute | solution.py:215
  46.2 8.5 %collective-permute-start.10 = (bf16[256,256]{1,0:T(8,128)(2,1)S(1)}, bf16[256,256]{1,0:T(8,128)(2,1)S(1)}, u32[]{:S(2)}, u32[]{:S(2)}) collective-permute-start(bf16[256,256]{1,0:T(8,128)(2,1)S(1)} %add_add_fusion.2), channel_id=1, source_target_pairs={{0,8},{1,9},{2,10},{3,11},{4,12},{5,13},{6,14},{7,15},{8,0},{9,1},... | collective-permute-start | bytes 393224 | tf_op jit(solution)/shard_map/ppermute | solution.py:215
  54.7 1.4 %collective-permute-start.11 = (bf16[256,256]{1,0:T(8,128)(2,1)S(1)}, bf16[256,256]{1,0:T(8,128)(2,1)S(1)}, u32[]{:S(2)}, u32[]{:S(2)}) collective-permute-start(bf16[256,256]{1,0:T(8,128)(2,1)S(1)} %add.69.refs_2_), channel_id=1, source_target_pairs={{0,1},{1,0},{2,3},{3,2},{4,5},{5,4},{6,7},{7,6},{8,9},{9,8},{10,11... | collective-permute-start | bytes 393224 | tf_op jit(solution)/shard_map/ppermute | solution.py:215
  56.7 1.4 %collective-permute-start.12 = (bf16[256,256]{1,0:T(8,128)(2,1)S(1)}, bf16[256,256]{1,0:T(8,128)(2,1)S(1)}, u32[]{:S(2)}, u32[]{:S(2)}) collective-permute-start(bf16[256,256]{1,0:T(8,128)(2,1)S(1)} %get-tuple-element.21), channel_id=1, source_target_pairs={{0,1},{1,0},{2,3},{3,2},{4,5},{5,4},{6,7},{7,6},{8,9},{9,8},{10,11... | collective-permute-start | bytes 393224 | tf_op jit(solution)/shard_map/ppermute | solution.py:215
  58.2 7.3 %collective-permute-start.15 = (bf16[256,256]{1,0:T(8,128)(2,1)S(1)}, bf16[256,256]{1,0:T(8,128)(2,1)S(1)}, u32[]{:S(2)}, u32[]{:S(2)}) collective-permute-start(bf16[256,256]{1,0:T(8,128)(2,1)S(1)} %add.70), channel_id=1, source_target_pairs={{0,6},{1,7},{2,4},{3,5},{4,2},{5,3},{6,0},{7,1},{8,14},{9,15},{10,... | collective-permute-start | bytes 393224 | tf_op jit(solution)/shard_map/ppermute | solution.py:215
  58.3 9.4 %collective-permute-start.14 = (bf16[256,256]{1,0:T(8,128)(2,1)S(1)}, bf16[256,256]{1,0:T(8,128)(2,1)S(1)}, u32[]{:S(2)}, u32[]{:S(2)}) collective-permute-start(bf16[256,256]{1,0:T(8,128)(2,1)S(1)} %add.70), channel_id=1, source_target_pairs={{0,4},{1,5},{2,6},{3,7},{4,0},{5,1},{6,2},{7,3},{8,12},{9,13},{10,... | collective-permute-start | bytes 393224 | tf_op jit(solution)/shard_map/ppermute | solution.py:215
  61.4 6.4 %collective-permute-start.13 = (bf16[256,256]{1,0:T(8,128)(2,1)S(1)}, bf16[256,256]{1,0:T(8,128)(2,1)S(1)}, u32[]{:S(2)}, u32[]{:S(2)}) collective-permute-start(bf16[256,256]{1,0:T(8,128)(2,1)S(1)} %add.70), channel_id=1, source_target_pairs={{0,2},{1,3},{2,0},{3,1},{4,6},{5,7},{6,4},{7,5},{8,10},{9,11},{10,... | collective-permute-start | bytes 393224 | tf_op jit(solution)/shard_map/ppermute | solution.py:215
  67.8 8.5 %collective-permute-start.16 = (bf16[256,256]{1,0:T(8,128)(2,1)S(1)}, bf16[256,256]{1,0:T(8,128)(2,1)S(1)}, u32[]{:S(2)}, u32[]{:S(2)}) collective-permute-start(bf16[256,256]{1,0:T(8,128)(2,1)S(1)} %add_add_fusion.1), channel_id=1, source_target_pairs={{0,8},{1,9},{2,10},{3,11},{4,12},{5,13},{6,14},{7,15},{8,0},{9,1},... | collective-permute-start | bytes 393224 | tf_op jit(solution)/shard_map/ppermute | solution.py:215
  76.3 1.4 %collective-permute-start.17 = (bf16[256,256]{1,0:T(8,128)(2,1)S(1)}, bf16[256,256]{1,0:T(8,128)(2,1)S(1)}, u32[]{:S(2)}, u32[]{:S(2)}) collective-permute-start(bf16[256,256]{1,0:T(8,128)(2,1)S(1)} %add.74.refs_4_), channel_id=1, source_target_pairs={{0,1},{1,0},{2,3},{3,2},{4,5},{5,4},{6,7},{7,6},{8,9},{9,8},{10,11... | collective-permute-start | bytes 393224 | tf_op jit(solution)/shard_map/ppermute | solution.py:215
  78.3 1.4 %collective-permute-start.18 = (bf16[256,256]{1,0:T(8,128)(2,1)S(1)}, bf16[256,256]{1,0:T(8,128)(2,1)S(1)}, u32[]{:S(2)}, u32[]{:S(2)}) collective-permute-start(bf16[256,256]{1,0:T(8,128)(2,1)S(1)} %get-tuple-element.23), channel_id=1, source_target_pairs={{0,1},{1,0},{2,3},{3,2},{4,5},{5,4},{6,7},{7,6},{8,9},{9,8},{10,11... | collective-permute-start | bytes 393224 | tf_op jit(solution)/shard_map/ppermute | solution.py:215
  79.8 7.3 %collective-permute-start.21 = (bf16[256,256]{1,0:T(8,128)(2,1)S(1)}, bf16[256,256]{1,0:T(8,128)(2,1)S(1)}, u32[]{:S(2)}, u32[]{:S(2)}) collective-permute-start(bf16[256,256]{1,0:T(8,128)(2,1)S(1)} %add.75), channel_id=1, source_target_pairs={{0,6},{1,7},{2,4},{3,5},{4,2},{5,3},{6,0},{7,1},{8,14},{9,15},{10,... | collective-permute-start | bytes 393224 | tf_op jit(solution)/shard_map/ppermute | solution.py:215
  80.3 9.5 %collective-permute-start.20 = (bf16[256,256]{1,0:T(8,128)(2,1)S(1)}, bf16[256,256]{1,0:T(8,128)(2,1)S(1)}, u32[]{:S(2)}, u32[]{:S(2)}) collective-permute-start(bf16[256,256]{1,0:T(8,128)(2,1)S(1)} %add.75), channel_id=1, source_target_pairs={{0,4},{1,5},{2,6},{3,7},{4,0},{5,1},{6,2},{7,3},{8,12},{9,13},{10,... | collective-permute-start | bytes 393224 | tf_op jit(solution)/shard_map/ppermute | solution.py:215
  83.4 6.4 %collective-permute-start.19 = (bf16[256,256]{1,0:T(8,128)(2,1)S(1)}, bf16[256,256]{1,0:T(8,128)(2,1)S(1)}, u32[]{:S(2)}, u32[]{:S(2)}) collective-permute-start(bf16[256,256]{1,0:T(8,128)(2,1)S(1)} %add.75), channel_id=1, source_target_pairs={{0,2},{1,3},{2,0},{3,1},{4,6},{5,7},{6,4},{7,5},{8,10},{9,11},{10,... | collective-permute-start | bytes 393224 | tf_op jit(solution)/shard_map/ppermute | solution.py:215
  89.8 8.5 %collective-permute-start.22 = (bf16[256,256]{1,0:T(8,128)(2,1)S(1)}, bf16[256,256]{1,0:T(8,128)(2,1)S(1)}, u32[]{:S(2)}, u32[]{:S(2)}) collective-permute-start(bf16[256,256]{1,0:T(8,128)(2,1)S(1)} %add_add_fusion), channel_id=1, source_target_pairs={{0,8},{1,9},{2,10},{3,11},{4,12},{5,13},{6,14},{7,15},{8,0},{9,1},... | collective-permute-start | bytes 393224 | tf_op jit(solution)/shard_map/ppermute | solution.py:215
  98.3 1.4 %collective-permute-start.23 = (bf16[256,256]{1,0:T(8,128)(2,1)S(1)}, bf16[256,256]{1,0:T(8,128)(2,1)S(1)}, u32[]{:S(2)}, u32[]{:S(2)}) collective-permute-start(bf16[256,256]{1,0:T(8,128)(2,1)S(1)} %add.79.refs_6_), channel_id=1, source_target_pairs={{0,1},{1,0},{2,3},{3,2},{4,5},{5,4},{6,7},{7,6},{8,9},{9,8},{10,11... | collective-permute-start | bytes 393224 | tf_op jit(solution)/shard_map/ppermute | solution.py:215

commit v2 on v1

v2 whole, which is shorter than its diff:
```python
import functools

import jax
import jax.numpy as jnp
from jax import lax
from jax.experimental import pallas as pl
from jax.experimental.pallas import tpu as pltpu
from jax.sharding import PartitionSpec as P

BLOCK = 512
HALF = 256
STEPS = 4
PANEL = 2048
BF = jnp.bfloat16
F32 = jnp.float32
VMEM_LIMIT = 24 * 1024 * 1024


def mm(a, b):
    return jnp.dot(a, b, preferred_element_type=F32)


def mm_nt(a, b):
    return lax.dot_general(a, b, (((1,), (1,)), ((), ())), preferred_element_type=F32)


def parts(value):
    high = value.astype(BF)
    return high, (value - high.astype(F32)).astype(BF)


def mm3(a_high, a_low, b):
    b_high, b_low = parts(b)
    return mm(a_high, b_high) + (mm(a_high, b_low) + mm(a_low, b_high))


def odd_rows(value, size):
    picked = [value[at : at + size] for at in range(size, value.shape[0], 2 * size)]
    return picked[0] if len(picked) == 1 else jnp.concatenate(picked, axis=0)


def put_odd_rows(value, odd, size):
    pieces = []
    for at in range(0, value.shape[0], size):
        turn = at // size
        pieces.append(
            value[at : at + size] if turn % 2 == 0 else odd[turn // 2 * size : (turn // 2 + 1) * size]
        )
    return jnp.concatenate(pieces, axis=0)


def double(tile, inverse, halves, size, apart, lower):
    high, low = halves
    width = tile.shape[1]
    link = jnp.where((lax.shift_right_logical(apart, size.bit_length() - 1) == 1) & lower, tile, 0.0)
    link = link.astype(BF)
    packed = size >= 16
    if packed:
        link = odd_rows(link, size)
        left_high, left_low = odd_rows(high, size), odd_rows(low, size)
    else:
        left_high, left_low = high, low
    if width <= 128:
        both = mm(link, jnp.concatenate([high, low], axis=1))
        inner = both[:, :width] + both[:, width:]
    else:
        inner = mm(link, high) + mm(link, low)
    if packed:
        zero = jnp.zeros((size, width), F32)
        pieces = []
        for at in range(inner.shape[0] // size):
            pieces += [zero, inner[at * size : (at + 1) * size]]
        inner = jnp.concatenate(pieces, axis=0)
    inner_high, inner_low = parts(inner)
    if width <= 128:
        rows = left_high.shape[0]
        both = mm(
            jnp.concatenate([left_high, left_low], axis=0),
            jnp.concatenate([inner_high, inner_low], axis=1),
        )
        change = both[:rows, :width] + (both[:rows, width:] + both[rows:, :width])
    else:
        change = mm(left_high, inner_high) + (mm(left_high, inner_low) + mm(left_low, inner_high))
    if packed:
        inverse = put_odd_rows(inverse, odd_rows(inverse, size) - change, size)
    else:
        inverse = inverse - change
    return inverse, parts(inverse)


def index_maps(shape):
    row = lax.broadcasted_iota(jnp.int32, shape, 0)
    col = lax.broadcasted_iota(jnp.int32, shape, 1)
    return row == col, row ^ col, row > col


def invert(tiles, pivot_rows):
    quarter = HALF // 2
    on, apart, lower = index_maps((quarter, quarter))
    small, values = [], []
    for tile, pivot in zip(tiles, pivot_rows):
        for at in range(0, HALF, quarter):
            piece = tile[at : at + quarter, at : at + quarter].astype(F32)
            across = 1.0 / pivot[:, at : at + quarter]
            diag = jnp.where(on, across, 0.0)
            down = jnp.sum(diag, axis=1, keepdims=True)
            first = jnp.where((apart == 1) & lower, piece, 0.0)
            small.append(piece)
            values.append(diag - down * first * across)
    halves = [parts(value) for value in values]
    size = 2
    while size < quarter:
        for at, piece in enumerate(small):
            values[at], halves[at] = double(piece, values[at], halves[at], size, apart, lower)
        size *= 2
    zero = jnp.zeros((quarter, quarter), F32)
    _, apart, lower = index_maps((HALF, HALF))
    result = []
    for at, tile in enumerate(tiles):
        value = jnp.concatenate(
            [
                jnp.concatenate([values[2 * at], zero], axis=1),
                jnp.concatenate([zero, values[2 * at + 1]], axis=1),
            ],
            axis=0,
        )
        result.append(double(tile.astype(F32), value, parts(value), quarter, apart, lower)[1])
    return result


def solve(tile_cross, inv, rows):
    (a_high, a_low), (b_high, b_low) = inv
    top = mm3(a_high, a_low, rows[:HALF])
    top_high, top_low = parts(top)
    rest = rows[HALF:] - (mm(tile_cross, top_high) + mm(tile_cross, top_low))
    return top.astype(BF), mm3(b_high, b_low, rest).astype(BF)


def put_halves(core, top, bottom, keep_ref, send_ref):
    first = core == 0
    keep_ref[...] = jnp.where(first, top, bottom)
    send_ref[...] = jnp.where(first, bottom, top)


def first_kernel(slots, home_ref, factor, pivots, rows, inv_high, inv_low, keep, send,
                 home, tiles, pivot, value, sems):
    me = lax.axis_index("row")
    fetch_home = pltpu.make_async_copy(home_ref, home, sems.at[0])
    fetch_pivot = pltpu.make_async_copy(pivots, pivot, sems.at[1])
    fetch_home.start()
    fetch_pivot.start()
    fetch_home.wait()
    which = []
    for slot in range(slots):
        found = jnp.int32(-1)
        for k in range(STEPS):
            found = jnp.where(home[k] == me * slots + slot, k, found)
        which.append(found)
    mine = home[0] // slots == me
    first_slot = home[0] % slots
    fetch_rows = pltpu.make_async_copy(
        rows.at[pl.ds(pl.multiple_of(first_slot * BLOCK, BLOCK), BLOCK), :], value, sems.at[2]
    )

    def fetch_tile(slot):
        c0 = pl.multiple_of(jnp.maximum(which[slot], 0) * BLOCK, BLOCK)
        return pltpu.make_async_copy(
            factor.at[pl.ds(slot * BLOCK, BLOCK), pl.ds(c0, BLOCK)],
            tiles.at[pl.ds(slot * BLOCK, BLOCK), :],
            sems.at[3 + slot],
        )

    for slot in range(slots):

        @pl.when(which[slot] >= 0)
        def _(slot=slot):
            fetch_tile(slot).start()

    @pl.when(mine)
    def _():
        fetch_rows.start()

    fetch_pivot.wait()
    for slot in range(slots):

        @pl.when(which[slot] >= 0)
        def _(slot=slot):
            fetch_tile(slot).wait()

    def one_slot(slot, carry):
        at = which[0]
        for other in range(1, slots):
            at = jnp.where(slot == other, which[other], at)

        @pl.when(at >= 0)
        def _():
            r0 = pl.multiple_of(slot * BLOCK, BLOCK)
            c0 = pl.multiple_of(at * BLOCK, BLOCK)
            pieces = [
                tiles[pl.ds(r0 + h * HALF, HALF), h * HALF : (h + 1) * HALF] for h in range(2)
            ]
            pivot_rows = [pivot[:, pl.ds(c0 + h * HALF, HALF)] for h in range(2)]
            for h, (high, low) in enumerate(invert(pieces, pivot_rows)):
                inv_high[slot, h] = high
                inv_low[slot, h] = low

        return carry

    lax.fori_loop(0, slots, one_slot, 0)

    @pl.when(mine)
    def _():
        fetch_rows.wait()
        r0 = pl.multiple_of(first_slot * BLOCK + HALF, HALF)
        inv = [(inv_high[first_slot, h], inv_low[first_slot, h]) for h in range(2)]
        top, bottom = solve(tiles[pl.ds(r0, HALF), :HALF], inv, value[...])
        put_halves(me % 2, top, bottom, keep, send)

    @pl.when(jnp.logical_not(mine))
    def _():
        keep[...] = jnp.zeros_like(keep)
        send[...] = jnp.zeros_like(send)


def finish(k, slots, home, factor, rows, inv_high, inv_low, solved, keep, send):
    me = lax.axis_index("row")
    core = me % 2
    mine = home[k] // slots == me

    @pl.when(mine)
    def _():
        slot = home[k] % slots
        r0 = pl.multiple_of(slot * BLOCK, BLOCK)
        value = rows[pl.ds(r0, BLOCK), :]
        for j, pair in enumerate(solved):
            for turn, half in enumerate(pair):
                at = core if turn == 0 else 1 - core
                c0 = pl.multiple_of(j * BLOCK + at * HALF, HALF)
                value = value - mm(factor[pl.ds(r0, BLOCK), pl.ds(c0, HALF)], half[...])
        cross = factor[pl.ds(r0 + HALF, HALF), pl.ds(k * BLOCK, HALF)]
        inv = [(inv_high[slot, h], inv_low[slot, h]) for h in range(2)]
        top, bottom = solve(cross, inv, value)
        put_halves(core, top, bottom, keep, send)

    @pl.when(jnp.logical_not(mine))
    def _():
        keep[...] = jnp.zeros_like(keep)
        send[...] = jnp.zeros_like(send)


def step_kernel(k, slots, home, factor, rows, inv_high, inv_low, *refs):
    solved = [(refs[2 * j], refs[2 * j + 1]) for j in range(k)]
    keep, send = refs[2 * k :]
    finish(k, slots, home, factor, rows, inv_high, inv_low, solved, keep, send)


def turn(core, at, number):
    where = core if number == 0 else 1 - core
    return pl.multiple_of(at * BLOCK + where * HALF, HALF)


def columns_of(half, me, width):
    columns = half.shape[1]
    pick = (
        lax.broadcasted_iota(jnp.int32, (width, columns), 1)
        == lax.broadcasted_iota(jnp.int32, (width, columns), 0) + me * width
    ).astype(F32).astype(BF)
    return mm_nt(pick, half)


def row_of_squares(value):
    high, low = parts(value * value)
    ones = jnp.ones((8, value.shape[1]), BF)
    return (mm_nt(ones, high) + mm_nt(ones, low))[:1]


def early_kernel(width, factor, rows, after, *refs):
    me = lax.axis_index("row")
    core = me % 2
    count = STEPS - 1
    solved = [(refs[2 * j], refs[2 * j + 1]) for j in range(count)]
    rest, own, squares = refs[2 * count :]

    def chunk(at, carry):
        r0 = pl.multiple_of(at * HALF, HALF)
        value = rows[pl.ds(r0, HALF), :]
        for j, pair in enumerate(solved):
            for number, half in enumerate(pair):
                c0 = turn(core, j, number)
                value = value - mm(factor[pl.ds(r0, HALF), pl.ds(c0, HALF)], half[...])
        rest[pl.ds(r0, HALF), :] = value
        return carry

    lax.fori_loop(0, rows.shape[0] // HALF, chunk, 0)
    total = jnp.zeros((1, width), F32)
    for j, pair in enumerate(solved):
        for number, half in enumerate(pair):
            value = columns_of(half[...], me, width)
            own[:, pl.ds(turn(core, j, number), HALF)] = value
            total = total + row_of_squares(value)
    squares[...] = total


def last_kernel(factor, rest, *refs):
    core = lax.axis_index("row") % 2
    pair, out = refs[:2], refs[2]
    on, _, _ = index_maps((HALF, HALF))
    eye = on.astype(F32).astype(BF)
    columns = rest.shape[1]

    def chunk(at, carry):
        r0 = pl.multiple_of(at * HALF, HALF)
        value = rest[pl.ds(r0, HALF), :]
        for number, half in enumerate(pair):
            c0 = turn(core, STEPS - 1, number)
            value = value - mm(factor[pl.ds(r0, HALF), pl.ds(c0, HALF)], half[...])
        value = value.astype(BF)
        for c in range(0, columns, HALF):
            out[c : c + HALF, pl.ds(r0, HALF)] = mm_nt(eye, value[:, c : c + HALF]).astype(BF)
        return carry

    lax.fori_loop(0, rest.shape[0] // HALF, chunk, 0)


def order_kernel(slots, width, home, arrived, own, squares, mine, other, out, variance, held, sems):
    me = lax.axis_index("row")
    core = me % 2
    solved_rows = (STEPS - 1) * BLOCK
    blocks = held.shape[1] // BLOCK
    group = 4

    def put_out(at):
        span = pl.ds(pl.multiple_of(at * group * BLOCK, BLOCK), group * BLOCK)
        return pltpu.make_async_copy(held.at[:, span], out.at[:, span], sems.at[at])

    def place_group(at, carry):
        for turn_at in range(group):
            g = at * group + turn_at
            spot = home[g]
            r0 = pl.multiple_of((spot // slots) * width, width)
            c0 = pl.multiple_of((spot % slots) * BLOCK, BLOCK)
            o0 = pl.multiple_of(g * BLOCK, BLOCK)
            held[:, pl.ds(o0, BLOCK)] = arrived[pl.ds(r0, width), pl.ds(c0, BLOCK)].astype(F32)
        put_out(at).start()
        return carry

    held[:, :solved_rows] = own[...]
    total = squares[...]
    for number, half in enumerate((mine, other)):
        value = columns_of(half[...], me, width)
        held[:, pl.ds(turn(core, STEPS - 1, number), HALF)] = value
        total = total + row_of_squares(value)
    variance[...] = total * (1.0 / (STEPS * BLOCK))
    put_out(0).start()
    lax.fori_loop(1, blocks // group, place_group, 0)

    def drain(at, carry):
        put_out(at).wait()
        return carry

    lax.fori_loop(0, blocks // group, drain, 0)


def call(kernel, outs, in_specs, out_specs, scalars=0, scratch=(), flops=0):
    return pl.pallas_call(
        kernel,
        grid_spec=pltpu.PrefetchScalarGridSpec(
            num_scalar_prefetch=scalars,
            in_specs=in_specs,
            out_specs=out_specs,
            scratch_shapes=scratch,
        ),
        out_shape=outs,
        compiler_params=pltpu.CompilerParams(vmem_limit_bytes=VMEM_LIMIT),
        cost_estimate=pl.CostEstimate(flops=flops, bytes_accessed=0, transcendentals=0),
    )


def hop(value, count, mask):
    return lax.ppermute(value, "row", [(i, i ^ mask) for i in range(count)])


def spread(keep, send, count, beside=()):
    mine = keep + hop(send, count, 1)
    if count >= 8:
        mine = mine + hop(mine, count, 2) + hop(mine, count, 4) + hop(mine, count, 6)
        mask = 8
        if beside:
            mine, *beside = lax.optimization_barrier((mine, *beside))
    else:
        mask = 2
    while mask < count:
        mine = mine + hop(mine, count, mask)
        mask *= 2
    return [mine, hop(mine, count, 1), *beside]


def on_device(factor_panel, pivots, right_sides, block_home):
    slots = factor_panel.shape[0] // BLOCK
    held_rows, columns = right_sides.shape
    count = lax.axis_size("row")
    width = columns // count
    blocks = block_home.shape[0]
    total = blocks * BLOCK
    shape = jax.ShapeDtypeStruct
    half = shape((HALF, columns), BF)
    inverse = shape((slots, 2, HALF, HALF), BF)
    vmem = pl.BlockSpec(memory_space=pltpu.VMEM)
    hbm = pl.BlockSpec(memory_space=pltpu.HBM)
    inv_high, inv_low, keep, send = call(
        functools.partial(first_kernel, slots),
        [inverse, inverse, half, half],
        [hbm] * 4,
        [vmem] * 4,
        scratch=(
            pltpu.SMEM((blocks,), jnp.int32),
            pltpu.VMEM((slots * BLOCK, BLOCK), BF),
            pltpu.VMEM((1, PANEL), F32),
            pltpu.VMEM((BLOCK, columns), F32),
            pltpu.SemaphoreType.DMA((3 + slots,)),
        ),
    )(*(
        pltpu.with_memory_space_constraint(value, pltpu.HBM)
        for value in (block_home, factor_panel, pivots.reshape(1, PANEL), right_sides)
    ))
    solved = spread(keep, send, count)
    for k in range(1, STEPS):
        keep, send = call(
            functools.partial(step_kernel, k, slots),
            [half, half],
            [vmem] * (4 + 2 * k),
            [vmem] * 2,
            scalars=1,
        )(block_home, factor_panel, right_sides, inv_high, inv_low, *solved)
        beside = ()
        if k == STEPS - 1:
            beside = call(
                functools.partial(early_kernel, width),
                [shape((held_rows, columns), F32), shape((width, k * BLOCK), F32), shape((1, width), F32)],
                [vmem] * (3 + 2 * k),
                [vmem] * 3,
                flops=2 * held_rows * columns * k * BLOCK,
            )(factor_panel, right_sides, send, *solved)
        solved += spread(keep, send, count, beside)
    *solved, rest, own, squares = solved
    (turned,) = call(
        last_kernel, [shape((columns, held_rows), BF)], [vmem] * 4, [vmem]
    )(factor_panel, rest, *solved[-2:])
    arrived = lax.all_to_all(turned, "row", split_axis=0, concat_axis=0, tiled=True)
    out, variance = call(
        functools.partial(order_kernel, slots, width),
        [shape((width, total), F32), shape((1, width), F32)],
        [vmem] * 5,
        [hbm, vmem],
        scalars=1,
        scratch=(pltpu.VMEM((width, total), F32), pltpu.SemaphoreType.DMA((blocks // 4,))),
    )(block_home, arrived, own, squares, *solved[-2:])
    return out.T, variance[0]


def solution(mesh):
    in_specs = (P(("groups", "row"), None), P("groups"), P(("groups", "row"), None), P())
    out_specs = (P("groups", "row"), P(("groups", "row")))
    return jax.shard_map(
        on_device, mesh=mesh, in_specs=in_specs, out_specs=out_specs, check_vma=False
    )
```

time: 124 us -> 117 us (0.944)
  local copies, waits for them, and re-layouts: 5.38 us -> 0.01 us
  starting transfers between devices: 28.7 us -> 26.7 us
    unnamed x10 -> x6, local copies, waits for them, and re-layouts: 4.76 us -> 0.01 us
    ppermute x24, starting transfers between devices: 28.7 us -> 26.7 us  [hop(): return lax.ppermute(value, 'row', [(i, i ^ mask) for i in range(count)])]
    pallas_call x6 -> x7, Pallas kernels: 7.98 us -> 9.03 us  [the longest x1 2.45 us: on_device(): call(functools.partial(early_kernel, width), [shape((held_rows, columns),...]
  transfers between devices with their start and end apart: 24 -> 24, of which waited for: 19 -> 23; matrix products, arithmetic and copies ran while one was open for 0% -> 0% of each run, Pallas kernels for 0% -> 2%
where the time goes in v2:
time: 117 us
  waiting for transfers between devices  62.1 us (53%)
  starting transfers between devices  26.7 us (23%)
  blocking collectives  18.1 us (15%)
  Pallas kernels  9.03 us (8%)
    ppermute x24, waiting for transfers between devices, hop(): return lax.ppermute(value, 'row', [(i, i ^ mask) for i in range(count)])  62.1 us
    ppermute x24, starting transfers between devices, hop(): return lax.ppermute(value, 'row', [(i, i ^ mask) for i in range(count)])  26.7 us
    all_to_all x1, blocking collectives, on_device(): lax.all_to_all(turned, 'row', split_axis=0, concat_axis=0, tiled=True)  18.1 us
    pallas_call x1, Pallas kernels, on_device(): call(functools.partial(early_kernel, width), [shape((held_rows, columns),...  2.45 us
    pallas_call x1, Pallas kernels, on_device(): call(functools.partial(order_kernel, slots, width), [shape((width, total)...  2.37 us
  transfers between devices with their start and end apart: 24, of which 23 were waited for; matrix products, arithmetic and copies ran while one was open for 0% of the time, Pallas kernels for 2%

profile of v2, /device:TPU:0, one launch (start us, length us, event | category | flops | bytes accessed | tf_op | source)
XLA Modules:
  0.0 117.1 jit_solution(803582603855772514)
XLA Ops:
  2.1 1.0 collective-permute-done
  3.2 9.6 %collective-permute-start.3 = (bf16[256,256]{1,0:T(8,128)(2,1)S(1)}, bf16[256,256]{1,0:T(8,128)(2,1)S(1)}, u32[]{:S(2)}, u32[]{:S(2)}) collective-permute-start(bf16[256,256]{1,0:T(8,128)(2,1)S(1)} %add.60), channel_id=1, source_target_pairs={{0,6},{1,7},{2,4},{3,5},{4,2},{5,3},{6,0},{7,1},{8,14},{9,15},{10,... | collective-permute-start | bytes 393224 | tf_op jit(solution)/shard_map/ppermute | solution.py:380
  13.4 3.7 %collective-permute-done.3 = bf16[256,256]{1,0:T(8,128)(2,1)S(1)} collective-permute-done((bf16[256,256]{1,0:T(8,128)(2,1)S(1)}, bf16[256,256]{1,0:T(8,128)(2,1)S(1)}, u32[]{:S(2)}, u32[]{:S(2)}) %collective-permute-start.3) | collective-permute-done | bytes 131104 | tf_op jit(solution)/shard_map/ppermute | solution.py:380
  17.1 1.6 %collective-permute-done.2 = bf16[256,256]{1,0:T(8,128)(2,1)S(1)} collective-permute-done((bf16[256,256]{1,0:T(8,128)(2,1)S(1)}, bf16[256,256]{1,0:T(8,128)(2,1)S(1)}, u32[]{:S(2)}, u32[]{:S(2)}) %collective-permute-start.2) | collective-permute-done | bytes 131104 | tf_op jit(solution)/shard_map/ppermute | solution.py:380
  19.4 1.9 %collective-permute-start.4 = (bf16[256,256]{1,0:T(8,128)(2,1)S(1)}, bf16[256,256]{1,0:T(8,128)(2,1)S(1)}, u32[]{:S(2)}, u32[]{:S(2)}) collective-permute-start(bf16[256,256]{1,0:T(8,128)(2,1)S(1)} %add_add_fusion.3), channel_id=1, source_target_pairs={{0,8},{1,9},{2,10},{3,11},{4,12},{5,13},{6,14},{7,15},{8,0},{9,1},... | collective-permute-start | bytes 393224 | tf_op jit(solution)/shard_map/ppermute | solution.py:380
  21.3 7.2 %collective-permute-done.4 = bf16[256,256]{1,0:T(8,128)(2,1)S(1)} collective-permute-done((bf16[256,256]{1,0:T(8,128)(2,1)S(1)}, bf16[256,256]{1,0:T(8,128)(2,1)S(1)}, u32[]{:S(2)}, u32[]{:S(2)}) %collective-permute-start.4) | collective-permute-done | bytes 131104 | tf_op jit(solution)/shard_map/ppermute | solution.py:380
  28.6 1.3 %collective-permute-done.5.refs_1_ = bf16[256,256]{1,0:T(8,128)(2,1)S(1)} collective-permute-done((bf16[256,256]{1,0:T(8,128)(2,1)S(1)}, bf16[256,256]{1,0:T(8,128)(2,1)S(1)}, u32[]{:S(2)}, u32[]{:S(2)}) %collective-permute-start.5) | collective-permute-done | bytes 131104 | tf_op jit(solution)/shard_map/ppermute | solution.py:380
  30.8 1.2 %collective-permute-done.6 = bf16[256,256]{1,0:T(8,128)(2,1)S(1)} collective-permute-done((bf16[256,256]{1,0:T(8,128)(2,1)S(1)}, bf16[256,256]{1,0:T(8,128)(2,1)S(1)}, u32[]{:S(2)}, u32[]{:S(2)}) %collective-permute-start.6) | collective-permute-done | bytes 131104 | tf_op jit(solution)/shard_map/ppermute | solution.py:380
  32.1 1.9 %collective-permute-start.8 = (bf16[256,256]{1,0:T(8,128)(2,1)S(1)}, bf16[256,256]{1,0:T(8,128)(2,1)S(1)}, u32[]{:S(2)}, u32[]{:S(2)}) collective-permute-start(bf16[256,256]{1,0:T(8,128)(2,1)S(1)} %add.65), channel_id=1, source_target_pairs={{0,4},{1,5},{2,6},{3,7},{4,0},{5,1},{6,2},{7,3},{8,12},{9,13},{10,... | collective-permute-start | bytes 393224 | tf_op jit(solution)/shard_map/ppermute | solution.py:380
  34.0 1.6 %collective-permute-start.7 = (bf16[256,256]{1,0:T(8,128)(2,1)S(1)}, bf16[256,256]{1,0:T(8,128)(2,1)S(1)}, u32[]{:S(2)}, u32[]{:S(2)}) collective-permute-start(bf16[256,256]{1,0:T(8,128)(2,1)S(1)} %add.65), channel_id=1, source_target_pairs={{0,2},{1,3},{2,0},{3,1},{4,6},{5,7},{6,4},{7,5},{8,10},{9,11},{10,... | collective-permute-start | bytes 393224 | tf_op jit(solution)/shard_map/ppermute | solution.py:380
  35.6 3.8 %collective-permute-done.9 = bf16[256,256]{1,0:T(8,128)(2,1)S(1)} collective-permute-done((bf16[256,256]{1,0:T(8,128)(2,1)S(1)}, bf16[256,256]{1,0:T(8,128)(2,1)S(1)}, u32[]{:S(2)}, u32[]{:S(2)}) %collective-permute-start.9) | collective-permute-done | bytes 131104 | tf_op jit(solution)/shard_map/ppermute | solution.py:380
  40.3 1.0 collective-permute-done.7
  42.2 7.9 %collective-permute-done.10 = bf16[256,256]{1,0:T(8,128)(2,1)S(1)} collective-permute-done((bf16[256,256]{1,0:T(8,128)(2,1)S(1)}, bf16[256,256]{1,0:T(8,128)(2,1)S(1)}, u32[]{:S(2)}, u32[]{:S(2)}) %collective-permute-start.10) | collective-permute-done | bytes 131104 | tf_op jit(solution)/shard_map/ppermute | solution.py:380
  50.2 1.3 %collective-permute-done.11.refs_3_ = bf16[256,256]{1,0:T(8,128)(2,1)S(1)} collective-permute-done((bf16[256,256]{1,0:T(8,128)(2,1)S(1)}, bf16[256,256]{1,0:T(8,128)(2,1)S(1)}, u32[]{:S(2)}, u32[]{:S(2)}) %collective-permute-start.11) | collective-permute-done | bytes 131104 | tf_op jit(solution)/shard_map/ppermute | solution.py:380
  52.3 1.2 %collective-permute-done.12 = bf16[256,256]{1,0:T(8,128)(2,1)S(1)} collective-permute-done((bf16[256,256]{1,0:T(8,128)(2,1)S(1)}, bf16[256,256]{1,0:T(8,128)(2,1)S(1)}, u32[]{:S(2)}, u32[]{:S(2)}) %collective-permute-start.12) | collective-permute-done | bytes 131104 | tf_op jit(solution)/shard_map/ppermute | solution.py:380
  53.6 3.1 %collective-permute-start.14 = (bf16[256,256]{1,0:T(8,128)(2,1)S(1)}, bf16[256,256]{1,0:T(8,128)(2,1)S(1)}, u32[]{:S(2)}, u32[]{:S(2)}) collective-permute-start(bf16[256,256]{1,0:T(8,128)(2,1)S(1)} %add.70), channel_id=1, source_target_pairs={{0,4},{1,5},{2,6},{3,7},{4,0},{5,1},{6,2},{7,3},{8,12},{9,13},{10,... | collective-permute-start | bytes 393224 | tf_op jit(solution)/shard_map/ppermute | solution.py:380
  57.1 3.8 %collective-permute-done.15 = bf16[256,256]{1,0:T(8,128)(2,1)S(1)} collective-permute-done((bf16[256,256]{1,0:T(8,128)(2,1)S(1)}, bf16[256,256]{1,0:T(8,128)(2,1)S(1)}, u32[]{:S(2)}, u32[]{:S(2)}) %collective-permute-start.15) | collective-permute-done | bytes 131104 | tf_op jit(solution)/shard_map/ppermute | solution.py:380
  60.9 2.5 %collective-permute-done.14 = bf16[256,256]{1,0:T(8,128)(2,1)S(1)} collective-permute-done((bf16[256,256]{1,0:T(8,128)(2,1)S(1)}, bf16[256,256]{1,0:T(8,128)(2,1)S(1)}, u32[]{:S(2)}, u32[]{:S(2)}) %collective-permute-start.14) | collective-permute-done | bytes 131104 | tf_op jit(solution)/shard_map/ppermute | solution.py:380
  63.5 8.6 %collective-permute-done.16 = bf16[256,256]{1,0:T(8,128)(2,1)S(1)} collective-permute-done((bf16[256,256]{1,0:T(8,128)(2,1)S(1)}, bf16[256,256]{1,0:T(8,128)(2,1)S(1)}, u32[]{:S(2)}, u32[]{:S(2)}) %collective-permute-start.16) | collective-permute-done | bytes 131104 | tf_op jit(solution)/shard_map/ppermute | solution.py:380
  72.2 1.3 %collective-permute-done.17.refs_5_ = bf16[256,256]{1,0:T(8,128)(2,1)S(1)} collective-permute-done((bf16[256,256]{1,0:T(8,128)(2,1)S(1)}, bf16[256,256]{1,0:T(8,128)(2,1)S(1)}, u32[]{:S(2)}, u32[]{:S(2)}) %collective-permute-start.17) | collective-permute-done | bytes 131104 | tf_op jit(solution)/shard_map/ppermute | solution.py:380
  74.3 1.2 %collective-permute-done.18 = bf16[256,256]{1,0:T(8,128)(2,1)S(1)} collective-permute-done((bf16[256,256]{1,0:T(8,128)(2,1)S(1)}, bf16[256,256]{1,0:T(8,128)(2,1)S(1)}, u32[]{:S(2)}, u32[]{:S(2)}) %collective-permute-start.18) | collective-permute-done | bytes 131104 | tf_op jit(solution)/shard_map/ppermute | solution.py:380
  75.6 2.0 %collective-permute-start.20 = (bf16[256,256]{1,0:T(8,128)(2,1)S(1)}, bf16[256,256]{1,0:T(8,128)(2,1)S(1)}, u32[]{:S(2)}, u32[]{:S(2)}) collective-permute-start(bf16[256,256]{1,0:T(8,128)(2,1)S(1)} %add.75), channel_id=1, source_target_pairs={{0,4},{1,5},{2,6},{3,7},{4,0},{5,1},{6,2},{7,3},{8,12},{9,13},{10,... | collective-permute-start | bytes 393224 | tf_op jit(solution)/shard_map/ppermute | solution.py:380
  77.6 1.5 %collective-permute-start.19 = (bf16[256,256]{1,0:T(8,128)(2,1)S(1)}, bf16[256,256]{1,0:T(8,128)(2,1)S(1)}, u32[]{:S(2)}, u32[]{:S(2)}) collective-permute-start(bf16[256,256]{1,0:T(8,128)(2,1)S(1)} %add.75), channel_id=1, source_target_pairs={{0,2},{1,3},{2,0},{3,1},{4,6},{5,7},{6,4},{7,5},{8,10},{9,11},{10,... | collective-permute-start | bytes 393224 | tf_op jit(solution)/shard_map/ppermute | solution.py:380
  79.1 2.4 %shard_map.63 = (f32[1024,256]{1,0:T(8,128)S(1)}, f32[16,1536]{1,0:T(8,128)S(1)}, f32[1,16]{1,0:T(1,128)S(1)}) custom-call(bf16[1024,2048]{1,0:T(8,128)(2,1)S(1)} %copy-done, f32[1024,256]{1,0:T(8,128)S(1)} %copy-done.1, bf16[256,256]{1,0:T(8,128)(2,1)S(1)} %get-tuple-element.30.after, bf16[256,256]{1,0:T(8,128)(2,1)S(1)} %add.64.refs_0_, ...), custom_call_target="tpu_custom_call" | custom-call | flops 805306368 | tf_op jit(solution)/shard_map/pallas_call | solution.py:437
  81.6 1.3 %collective-permute-done.21 = bf16[256,256]{1,0:T(8,128)(2,1)S(1)} collective-permute-done((bf16[256,256]{1,0:T(8,128)(2,1)S(1)}, bf16[256,256]{1,0:T(8,128)(2,1)S(1)}, u32[]{:S(2)}, u32[]{:S(2)}) %collective-permute-start.21) | collective-permute-done | bytes 131104 | tf_op jit(solution)/shard_map/ppermute | solution.py:380
  82.9 1.1 collective-permute-done.20
  84.9 1.5 %collective-permute-start.22 = (bf16[256,256]{1,0:T(8,128)(2,1)S(1)}, bf16[256,256]{1,0:T(8,128)(2,1)S(1)}, u32[]{:S(2)}, u32[]{:S(2)}) collective-permute-start(bf16[256,256]{1,0:T(8,128)(2,1)S(1)} %add_add_fusion), channel_id=1, source_target_pairs={{0,8},{1,9},{2,10},{3,11},{4,12},{5,13},{6,14},{7,15},{8,0},{9,1},... | collective-permute-start | bytes 393224 | tf_op jit(solution)/shard_map/ppermute | solution.py:380
  86.4 7.2 %collective-permute-done.22 = bf16[256,256]{1,0:T(8,128)(2,1)S(1)} collective-permute-done((bf16[256,256]{1,0:T(8,128)(2,1)S(1)}, bf16[256,256]{1,0:T(8,128)(2,1)S(1)}, u32[]{:S(2)}, u32[]{:S(2)}) %collective-permute-start.22) | collective-permute-done | bytes 131104 | tf_op jit(solution)/shard_map/ppermute | solution.py:380
  93.7 1.3 %collective-permute-done.23.refs_1_.other = bf16[256,256]{1,0:T(8,128)(2,1)S(1)} collective-permute-done((bf16[256,256]{1,0:T(8,128)(2,1)S(1)}, bf16[256,256]{1,0:T(8,128)(2,1)S(1)}, u32[]{:S(2)}, u32[]{:S(2)}) %collective-permute-start.23) | collective-permute-done | bytes 131104 | tf_op jit(solution)/shard_map/ppermute | solution.py:380
  95.0 1.6 %shard_map.64 = bf16[256,1024]{1,0:T(8,128)(2,1)S(1)} custom-call(bf16[1024,2048]{1,0:T(8,128)(2,1)S(1)} %copy-done, f32[1024,256]{1,0:T(8,128)S(1)} %get-tuple-element.34.rest, bf16[256,256]{1,0:T(8,128)(2,1)S(1)} %add.79.refs_0_.mine, bf16[256,256]{1,0:T(8,128)(2,1)S(1)} %collective-permute-done.23.refs_1_.other), custom_call_target="tpu_custom_call" | custom-call | tf_op jit(solution)/shard_map/pallas_call | solution.py:446
  96.6 18.1 %all_to_all.11 = bf16[16,16,1024]{2,1,0:T(8,128)(2,1)S(1)} all-to-all(bf16[16,16,1024]{2,1,0:T(8,128)(2,1)S(1)} %bitcast.5), channel_id=1, replica_groups=mesh['groups'=2,'row'=16] {'row'}, dimensions={0} | all-to-all | bytes 1048576 | tf_op jit(solution)/shard_map/all_to_all | solution.py:449
  114.7 2.4 %shard_map.65 = (f32[16,16384]{1,0:T(8,128)}, f32[1,16]{1,0:T(1,128)}) custom-call(s32[32]{0:T(128)S(1)} %copy-done.2, bf16[256,1024]{1,0:T(8,128)(2,1)S(1)} %bitcast.6, f32[16,1536]{1,0:T(8,128)S(1)} %get-tuple-element.36.own, f32[1,16]{1,0:T(1,128)S(1)} %get-tuple-element.37.squares, bf16[256,256]{1,0:T(8,128)(2,1)S(1)} %add.79.refs_0_.mine, ...), custom_call_target="tpu_custom_call" | custom-call | tf_op jit(solution)/shard_map/pallas_call | solution.py:450
  (42 shorter events, 9.3 us)
Async XLA Ops:
  0.6 29.3 %copy-start = (bf16[1024,2048]{1,0:T(8,128)(2,1)S(1)}, bf16[1024,2048]{1,0:T(8,128)(2,1)}, u32[]{:S(2)}) copy-start(bf16[1024,2048]{1,0:T(8,128)(2,1)} %factor.11) | copy-start | bytes 12582916
  0.6 29.3 %copy-start.2 = (s32[32]{0:T(128)S(1)}, s32[32]{0:T(128)}, u32[]{:S(2)}) copy-start(s32[32]{0:T(128)} %home.7) | copy-start | bytes 388
  0.7 29.3 %copy-start.1 = (f32[1024,256]{1,0:T(8,128)S(1)}, f32[1024,256]{1,0:T(8,128)}, u32[]{:S(2)}) copy-start(f32[1024,256]{1,0:T(8,128)} %rows.9) | copy-start | bytes 3145732
  1.6 1.5 %collective-permute-start = (bf16[256,256]{1,0:T(8,128)(2,1)S(1)}, bf16[256,256]{1,0:T(8,128)(2,1)S(1)}, u32[]{:S(2)}, u32[]{:S(2)}) collective-permute-start(bf16[256,256]{1,0:T(8,128)(2,1)S(1)} %get-tuple-element.24), channel_id=1, source_target_pairs={{0,1},{1,0},{2,3},{3,2},{4,5},{5,4},{6,7},{7,6},{8,9},{9,8},{10,11... | collective-permute-start | bytes 393224 | tf_op jit(solution)/shard_map/ppermute | solution.py:380
  3.2 13.9 %collective-permute-start.3 = (bf16[256,256]{1,0:T(8,128)(2,1)S(1)}, bf16[256,256]{1,0:T(8,128)(2,1)S(1)}, u32[]{:S(2)}, u32[]{:S(2)}) collective-permute-start(bf16[256,256]{1,0:T(8,128)(2,1)S(1)} %add.60), channel_id=1, source_target_pairs={{0,6},{1,7},{2,4},{3,5},{4,2},{5,3},{6,0},{7,1},{8,14},{9,15},{10,... | collective-permute-start | bytes 393224 | tf_op jit(solution)/shard_map/ppermute | solution.py:380
  12.7 5.9 %collective-permute-start.2 = (bf16[256,256]{1,0:T(8,128)(2,1)S(1)}, bf16[256,256]{1,0:T(8,128)(2,1)S(1)}, u32[]{:S(2)}, u32[]{:S(2)}) collective-permute-start(bf16[256,256]{1,0:T(8,128)(2,1)S(1)} %add.60), channel_id=1, source_target_pairs={{0,4},{1,5},{2,6},{3,7},{4,0},{5,1},{6,2},{7,3},{8,12},{9,13},{10,... | collective-permute-start | bytes 393224 | tf_op jit(solution)/shard_map/ppermute | solution.py:380
  12.7 6.6 %collective-permute-start.1 = (bf16[256,256]{1,0:T(8,128)(2,1)S(1)}, bf16[256,256]{1,0:T(8,128)(2,1)S(1)}, u32[]{:S(2)}, u32[]{:S(2)}) collective-permute-start(bf16[256,256]{1,0:T(8,128)(2,1)S(1)} %add.60), channel_id=1, source_target_pairs={{0,2},{1,3},{2,0},{3,1},{4,6},{5,7},{6,4},{7,5},{8,10},{9,11},{10,... | collective-permute-start | bytes 393224 | tf_op jit(solution)/shard_map/ppermute | solution.py:380
  19.4 9.1 %collective-permute-start.4 = (bf16[256,256]{1,0:T(8,128)(2,1)S(1)}, bf16[256,256]{1,0:T(8,128)(2,1)S(1)}, u32[]{:S(2)}, u32[]{:S(2)}) collective-permute-start(bf16[256,256]{1,0:T(8,128)(2,1)S(1)} %add_add_fusion.3), channel_id=1, source_target_pairs={{0,8},{1,9},{2,10},{3,11},{4,12},{5,13},{6,14},{7,15},{8,0},{9,1},... | collective-permute-start | bytes 393224 | tf_op jit(solution)/shard_map/ppermute | solution.py:380
  28.5 1.4 %collective-permute-start.5 = (bf16[256,256]{1,0:T(8,128)(2,1)S(1)}, bf16[256,256]{1,0:T(8,128)(2,1)S(1)}, u32[]{:S(2)}, u32[]{:S(2)}) collective-permute-start(bf16[256,256]{1,0:T(8,128)(2,1)S(1)} %add.64.refs_0_), channel_id=1, source_target_pairs={{0,1},{1,0},{2,3},{3,2},{4,5},{5,4},{6,7},{7,6},{8,9},{9,8},{10,11... | collective-permute-start | bytes 393224 | tf_op jit(solution)/shard_map/ppermute | solution.py:380
  30.6 1.4 %collective-permute-start.6 = (bf16[256,256]{1,0:T(8,128)(2,1)S(1)}, bf16[256,256]{1,0:T(8,128)(2,1)S(1)}, u32[]{:S(2)}, u32[]{:S(2)}) collective-permute-start(bf16[256,256]{1,0:T(8,128)(2,1)S(1)} %get-tuple-element.26), channel_id=1, source_target_pairs={{0,1},{1,0},{2,3},{3,2},{4,5},{5,4},{6,7},{7,6},{8,9},{9,8},{10,11... | collective-permute-start | bytes 393224 | tf_op jit(solution)/shard_map/ppermute | solution.py:380
  32.0 7.3 %collective-permute-start.9 = (bf16[256,256]{1,0:T(8,128)(2,1)S(1)}, bf16[256,256]{1,0:T(8,128)(2,1)S(1)}, u32[]{:S(2)}, u32[]{:S(2)}) collective-permute-start(bf16[256,256]{1,0:T(8,128)(2,1)S(1)} %add.65), channel_id=1, source_target_pairs={{0,6},{1,7},{2,4},{3,5},{4,2},{5,3},{6,0},{7,1},{8,14},{9,15},{10,... | collective-permute-start | bytes 393224 | tf_op jit(solution)/shard_map/ppermute | solution.py:380
  32.1 8.2 %collective-permute-start.8 = (bf16[256,256]{1,0:T(8,128)(2,1)S(1)}, bf16[256,256]{1,0:T(8,128)(2,1)S(1)}, u32[]{:S(2)}, u32[]{:S(2)}) collective-permute-start(bf16[256,256]{1,0:T(8,128)(2,1)S(1)} %add.65), channel_id=1, source_target_pairs={{0,4},{1,5},{2,6},{3,7},{4,0},{5,1},{6,2},{7,3},{8,12},{9,13},{10,... | collective-permute-start | bytes 393224 | tf_op jit(solution)/shard_map/ppermute | solution.py:380
  34.0 7.3 %collective-permute-start.7 = (bf16[256,256]{1,0:T(8,128)(2,1)S(1)}, bf16[256,256]{1,0:T(8,128)(2,1)S(1)}, u32[]{:S(2)}, u32[]{:S(2)}) collective-permute-start(bf16[256,256]{1,0:T(8,128)(2,1)S(1)} %add.65), channel_id=1, source_target_pairs={{0,2},{1,3},{2,0},{3,1},{4,6},{5,7},{6,4},{7,5},{8,10},{9,11},{10,... | collective-permute-start | bytes 393224 | tf_op jit(solution)/shard_map/ppermute | solution.py:380
  41.4 8.7 %collective-permute-start.10 = (bf16[256,256]{1,0:T(8,128)(2,1)S(1)}, bf16[256,256]{1,0:T(8,128)(2,1)S(1)}, u32[]{:S(2)}, u32[]{:S(2)}) collective-permute-start(bf16[256,256]{1,0:T(8,128)(2,1)S(1)} %add_add_fusion.2), channel_id=1, source_target_pairs={{0,8},{1,9},{2,10},{3,11},{4,12},{5,13},{6,14},{7,15},{8,0},{9,1},... | collective-permute-start | bytes 393224 | tf_op jit(solution)/shard_map/ppermute | solution.py:380
  50.1 1.4 %collective-permute-start.11 = (bf16[256,256]{1,0:T(8,128)(2,1)S(1)}, bf16[256,256]{1,0:T(8,128)(2,1)S(1)}, u32[]{:S(2)}, u32[]{:S(2)}) collective-permute-start(bf16[256,256]{1,0:T(8,128)(2,1)S(1)} %add.69.refs_2_), channel_id=1, source_target_pairs={{0,1},{1,0},{2,3},{3,2},{4,5},{5,4},{6,7},{7,6},{8,9},{9,8},{10,11... | collective-permute-start | bytes 393224 | tf_op jit(solution)/shard_map/ppermute | solution.py:380
  52.1 1.4 %collective-permute-start.12 = (bf16[256,256]{1,0:T(8,128)(2,1)S(1)}, bf16[256,256]{1,0:T(8,128)(2,1)S(1)}, u32[]{:S(2)}, u32[]{:S(2)}) collective-permute-start(bf16[256,256]{1,0:T(8,128)(2,1)S(1)} %get-tuple-element.28), channel_id=1, source_target_pairs={{0,1},{1,0},{2,3},{3,2},{4,5},{5,4},{6,7},{7,6},{8,9},{9,8},{10,11... | collective-permute-start | bytes 393224 | tf_op jit(solution)/shard_map/ppermute | solution.py:380
  53.6 7.3 %collective-permute-start.15 = (bf16[256,256]{1,0:T(8,128)(2,1)S(1)}, bf16[256,256]{1,0:T(8,128)(2,1)S(1)}, u32[]{:S(2)}, u32[]{:S(2)}) collective-permute-start(bf16[256,256]{1,0:T(8,128)(2,1)S(1)} %add.70), channel_id=1, source_target_pairs={{0,6},{1,7},{2,4},{3,5},{4,2},{5,3},{6,0},{7,1},{8,14},{9,15},{10,... | collective-permute-start | bytes 393224 | tf_op jit(solution)/shard_map/ppermute | solution.py:380
  53.6 9.7 %collective-permute-start.14 = (bf16[256,256]{1,0:T(8,128)(2,1)S(1)}, bf16[256,256]{1,0:T(8,128)(2,1)S(1)}, u32[]{:S(2)}, u32[]{:S(2)}) collective-permute-start(bf16[256,256]{1,0:T(8,128)(2,1)S(1)} %add.70), channel_id=1, source_target_pairs={{0,4},{1,5},{2,6},{3,7},{4,0},{5,1},{6,2},{7,3},{8,12},{9,13},{10,... | collective-permute-start | bytes 393224 | tf_op jit(solution)/shard_map/ppermute | solution.py:380
  56.8 6.6 %collective-permute-start.13 = (bf16[256,256]{1,0:T(8,128)(2,1)S(1)}, bf16[256,256]{1,0:T(8,128)(2,1)S(1)}, u32[]{:S(2)}, u32[]{:S(2)}) collective-permute-start(bf16[256,256]{1,0:T(8,128)(2,1)S(1)} %add.70), channel_id=1, source_target_pairs={{0,2},{1,3},{2,0},{3,1},{4,6},{5,7},{6,4},{7,5},{8,10},{9,11},{10,... | collective-permute-start | bytes 393224 | tf_op jit(solution)/shard_map/ppermute | solution.py:380
  63.4 8.7 %collective-permute-start.16 = (bf16[256,256]{1,0:T(8,128)(2,1)S(1)}, bf16[256,256]{1,0:T(8,128)(2,1)S(1)}, u32[]{:S(2)}, u32[]{:S(2)}) collective-permute-start(bf16[256,256]{1,0:T(8,128)(2,1)S(1)} %add_add_fusion.1), channel_id=1, source_target_pairs={{0,8},{1,9},{2,10},{3,11},{4,12},{5,13},{6,14},{7,15},{8,0},{9,1},... | collective-permute-start | bytes 393224 | tf_op jit(solution)/shard_map/ppermute | solution.py:380
  72.1 1.4 %collective-permute-start.17 = (bf16[256,256]{1,0:T(8,128)(2,1)S(1)}, bf16[256,256]{1,0:T(8,128)(2,1)S(1)}, u32[]{:S(2)}, u32[]{:S(2)}) collective-permute-start(bf16[256,256]{1,0:T(8,128)(2,1)S(1)} %add.74.refs_4_), channel_id=1, source_target_pairs={{0,1},{1,0},{2,3},{3,2},{4,5},{5,4},{6,7},{7,6},{8,9},{9,8},{10,11... | collective-permute-start | bytes 393224 | tf_op jit(solution)/shard_map/ppermute | solution.py:380
  74.1 1.4 %collective-permute-start.18 = (bf16[256,256]{1,0:T(8,128)(2,1)S(1)}, bf16[256,256]{1,0:T(8,128)(2,1)S(1)}, u32[]{:S(2)}, u32[]{:S(2)}) collective-permute-start(bf16[256,256]{1,0:T(8,128)(2,1)S(1)} %get-tuple-element.30.after), channel_id=1, source_target_pairs={{0,1},{1,0},{2,3},{3,2},{4,5},{5,4},{6,7},{7,6},{8,9},{9,8},{10,11... | collective-permute-start | bytes 393224 | tf_op jit(solution)/shard_map/ppermute | solution.py:380
  75.5 7.3 %collective-permute-start.21 = (bf16[256,256]{1,0:T(8,128)(2,1)S(1)}, bf16[256,256]{1,0:T(8,128)(2,1)S(1)}, u32[]{:S(2)}, u32[]{:S(2)}) collective-permute-start(bf16[256,256]{1,0:T(8,128)(2,1)S(1)} %add.75), channel_id=1, source_target_pairs={{0,6},{1,7},{2,4},{3,5},{4,2},{5,3},{6,0},{7,1},{8,14},{9,15},{10,... | collective-permute-start | bytes 393224 | tf_op jit(solution)/shard_map/ppermute | solution.py:380
  75.6 8.3 %collective-permute-start.20 = (bf16[256,256]{1,0:T(8,128)(2,1)S(1)}, bf16[256,256]{1,0:T(8,128)(2,1)S(1)}, u32[]{:S(2)}, u32[]{:S(2)}) collective-permute-start(bf16[256,256]{1,0:T(8,128)(2,1)S(1)} %add.75), channel_id=1, source_target_pairs={{0,4},{1,5},{2,6},{3,7},{4,0},{5,1},{6,2},{7,3},{8,12},{9,13},{10,... | collective-permute-start | bytes 393224 | tf_op jit(solution)/shard_map/ppermute | solution.py:380
  77.6 7.3 %collective-permute-start.19 = (bf16[256,256]{1,0:T(8,128)(2,1)S(1)}, bf16[256,256]{1,0:T(8,128)(2,1)S(1)}, u32[]{:S(2)}, u32[]{:S(2)}) collective-permute-start(bf16[256,256]{1,0:T(8,128)(2,1)S(1)} %add.75), channel_id=1, source_target_pairs={{0,2},{1,3},{2,0},{3,1},{4,6},{5,7},{6,4},{7,5},{8,10},{9,11},{10,... | collective-permute-start | bytes 393224 | tf_op jit(solution)/shard_map/ppermute | solution.py:380
  84.9 8.7 %collective-permute-start.22 = (bf16[256,256]{1,0:T(8,128)(2,1)S(1)}, bf16[256,256]{1,0:T(8,128)(2,1)S(1)}, u32[]{:S(2)}, u32[]{:S(2)}) collective-permute-start(bf16[256,256]{1,0:T(8,128)(2,1)S(1)} %add_add_fusion), channel_id=1, source_target_pairs={{0,8},{1,9},{2,10},{3,11},{4,12},{5,13},{6,14},{7,15},{8,0},{9,1},... | collective-permute-start | bytes 393224 | tf_op jit(solution)/shard_map/ppermute | solution.py:380
  93.6 1.4 %collective-permute-start.23 = (bf16[256,256]{1,0:T(8,128)(2,1)S(1)}, bf16[256,256]{1,0:T(8,128)(2,1)S(1)}, u32[]{:S(2)}, u32[]{:S(2)}) collective-permute-start(bf16[256,256]{1,0:T(8,128)(2,1)S(1)} %add.79.refs_0_.mine), channel_id=1, source_target_pairs={{0,1},{1,0},{2,3},{3,2},{4,5},{5,4},{6,7},{7,6},{8,9},{9,8},{10,11... | collective-permute-start | bytes 393224 | tf_op jit(solution)/shard_map/ppermute | solution.py:380

commit v3 on v2

--- a/solution.py
+++ b/solution.py
@@ -222,36 +222,28 @@
         send[...] = jnp.zeros_like(send)
 
 
-def finish(k, slots, home, factor, rows, inv_high, inv_low, solved, keep, send):
+def step_kernel(k, slots, home, factor, rest, inv_high, inv_low, mine, other, keep, send):
     me = lax.axis_index("row")
     core = me % 2
-    mine = home[k] // slots == me
-
-    @pl.when(mine)
+    owner = home[k] // slots == me
+
+    @pl.when(owner)
     def _():
         slot = home[k] % slots
         r0 = pl.multiple_of(slot * BLOCK, BLOCK)
-        value = rows[pl.ds(r0, BLOCK), :]
-        for j, pair in enumerate(solved):
-            for turn, half in enumerate(pair):
-                at = core if turn == 0 else 1 - core
-                c0 = pl.multiple_of(j * BLOCK + at * HALF, HALF)
-                value = value - mm(factor[pl.ds(r0, BLOCK), pl.ds(c0, HALF)], half[...])
+        value = rest[pl.ds(r0, BLOCK), :]
+        for number, half in enumerate((mine, other)):
+            c0 = turn(core, k - 1, number)
+            value = value - mm(factor[pl.ds(r0, BLOCK), pl.ds(c0, HALF)], half[...])
         cross = factor[pl.ds(r0 + HALF, HALF), pl.ds(k * BLOCK, HALF)]
         inv = [(inv_high[slot, h], inv_low[slot, h]) for h in range(2)]
         top, bottom = solve(cross, inv, value)
         put_halves(core, top, bottom, keep, send)
 
-    @pl.when(jnp.logical_not(mine))
+    @pl.when(jnp.logical_not(owner))
     def _():
         keep[...] = jnp.zeros_like(keep)
         send[...] = jnp.zeros_like(send)
-
-
-def step_kernel(k, slots, home, factor, rows, inv_high, inv_low, *refs):
-    solved = [(refs[2 * j], refs[2 * j + 1]) for j in range(k)]
-    keep, send = refs[2 * k :]
-    finish(k, slots, home, factor, rows, inv_high, inv_low, solved, keep, send)
 
 
 def turn(core, at, number):
@@ -274,30 +266,29 @@
     return (mm_nt(ones, high) + mm_nt(ones, low))[:1]
 
 
-def early_kernel(width, factor, rows, after, *refs):
+def early_kernel(k, width, factor, before, after, mine, other, rest, own, squares):
     me = lax.axis_index("row")
     core = me % 2
-    count = STEPS - 1
-    solved = [(refs[2 * j], refs[2 * j + 1]) for j in range(count)]
-    rest, own, squares = refs[2 * count :]
 
     def chunk(at, carry):
         r0 = pl.multiple_of(at * HALF, HALF)
-        value = rows[pl.ds(r0, HALF), :]
-        for j, pair in enumerate(solved):
-            for number, half in enumerate(pair):
-                c0 = turn(core, j, number)
-                value = value - mm(factor[pl.ds(r0, HALF), pl.ds(c0, HALF)], half[...])
+        value = before[pl.ds(r0, HALF), :]
+        for number, half in enumerate((mine, other)):
+            c0 = turn(core, k, number)
+            value = value - mm(factor[pl.ds(r0, HALF), pl.ds(c0, HALF)], half[...])
         rest[pl.ds(r0, HALF), :] = value
         return carry
 
-    lax.fori_loop(0, rows.shape[0] // HALF, chunk, 0)
+    lax.fori_loop(0, before.shape[0] // HALF, chunk, 0)
+    own_columns(core, me, width, mine, other, own, squares)
+
+
+def own_columns(core, me, width, mine, other, own, squares):
     total = jnp.zeros((1, width), F32)
-    for j, pair in enumerate(solved):
-        for number, half in enumerate(pair):
-            value = columns_of(half[...], me, width)
-            own[:, pl.ds(turn(core, j, number), HALF)] = value
-            total = total + row_of_squares(value)
+    for number, half in enumerate((mine, other)):
+        value = columns_of(half[...], me, width)
+        own[:, pl.ds(turn(core, 0, number), HALF)] = value
+        total = total + row_of_squares(value)
     squares[...] = total
 
 
@@ -322,12 +313,13 @@
     lax.fori_loop(0, rest.shape[0] // HALF, chunk, 0)
 
 
-def order_kernel(slots, width, home, arrived, own, squares, mine, other, out, variance, held, sems):
+def order_kernel(slots, width, home, arrived, mine, other, *refs):
+    owns, squares = refs[: STEPS - 1], refs[STEPS - 1 : 2 * (STEPS - 1)]
+    out, variance, held, sems = refs[2 * (STEPS - 1) :]
     me = lax.axis_index("row")
     core = me % 2
-    solved_rows = (STEPS - 1) * BLOCK
     blocks = held.shape[1] // BLOCK
-    group = 4
+    group = STEPS
 
     def put_out(at):
         span = pl.ds(pl.multiple_of(at * group * BLOCK, BLOCK), group * BLOCK)
@@ -344,8 +336,10 @@
         put_out(at).start()
         return carry
 
-    held[:, :solved_rows] = own[...]
-    total = squares[...]
+    total = jnp.zeros((1, width), F32)
+    for j in range(STEPS - 1):
+        held[:, j * BLOCK : (j + 1) * BLOCK] = owns[j][...]
+        total = total + squares[j][...]
     for number, half in enumerate((mine, other)):
         value = columns_of(half[...], me, width)
         held[:, pl.ds(turn(core, STEPS - 1, number), HALF)] = value
@@ -376,23 +370,20 @@
     )
 
 
-def hop(value, count, mask):
-    return lax.ppermute(value, "row", [(i, i ^ mask) for i in range(count)])
+def hop(value, count, even, odd):
+    return lax.ppermute(
+        value, "row", [(i, i ^ (odd if i % 2 else even)) for i in range(count)]
+    )
 
 
 def spread(keep, send, count, beside=()):
-    mine = keep + hop(send, count, 1)
-    if count >= 8:
-        mine = mine + hop(mine, count, 2) + hop(mine, count, 4) + hop(mine, count, 6)
-        mask = 8
-        if beside:
+    mine = keep + hop(send, count, 1, 1)
+    masks = [1 << bit for bit in range(1, count.bit_length() - 1)]
+    for at, mask in enumerate(masks):
+        mine = mine + hop(mine, count, mask, masks[at - 1])
+        if beside and at == 0:
             mine, *beside = lax.optimization_barrier((mine, *beside))
-    else:
-        mask = 2
-    while mask < count:
-        mine = mine + hop(mine, count, mask)
-        mask *= 2
-    return [mine, hop(mine, count, 1), *beside]
+    return [mine, hop(mine, count, 1, 1)], beside
 
 
 def on_device(factor_panel, pivots, right_sides, block_home):
@@ -423,38 +414,39 @@
         pltpu.with_memory_space_constraint(value, pltpu.HBM)
         for value in (block_home, factor_panel, pivots.reshape(1, PANEL), right_sides)
     ))
-    solved = spread(keep, send, count)
+    (mine, other), _ = spread(keep, send, count)
+    rest = right_sides
+    owns, squares = [], []
     for k in range(1, STEPS):
         keep, send = call(
             functools.partial(step_kernel, k, slots),
             [half, half],
-            [vmem] * (4 + 2 * k),
+            [vmem] * 6,
             [vmem] * 2,
             scalars=1,
-        )(block_home, factor_panel, right_sides, inv_high, inv_low, *solved)
-        beside = ()
-        if k == STEPS - 1:
-            beside = call(
-                functools.partial(early_kernel, width),
-                [shape((held_rows, columns), F32), shape((width, k * BLOCK), F32), shape((1, width), F32)],
-                [vmem] * (3 + 2 * k),
-                [vmem] * 3,
-                flops=2 * held_rows * columns * k * BLOCK,
-            )(factor_panel, right_sides, send, *solved)
-        solved += spread(keep, send, count, beside)
-    *solved, rest, own, squares = solved
+        )(block_home, factor_panel, rest, inv_high, inv_low, mine, other)
+        beside = call(
+            functools.partial(early_kernel, k - 1, width),
+            [shape((held_rows, columns), F32), shape((width, BLOCK), F32), shape((1, width), F32)],
+            [vmem] * 5,
+            [vmem] * 3,
+            flops=2 * held_rows * columns * BLOCK,
+        )(factor_panel, rest, send, mine, other)
+        (mine, other), (rest, own, square) = spread(keep, send, count, beside)
+        owns.append(own)
+        squares.append(square)
     (turned,) = call(
         last_kernel, [shape((columns, held_rows), BF)], [vmem] * 4, [vmem]
-    )(factor_panel, rest, *solved[-2:])
+    )(factor_panel, rest, mine, other)
     arrived = lax.all_to_all(turned, "row", split_axis=0, concat_axis=0, tiled=True)
     out, variance = call(
         functools.partial(order_kernel, slots, width),
         [shape((width, total), F32), shape((1, width), F32)],
-        [vmem] * 5,
+        [vmem] * (3 + 2 * (STEPS - 1)),
         [hbm, vmem],
         scalars=1,
-        scratch=(pltpu.VMEM((width, total), F32), pltpu.SemaphoreType.DMA((blocks // 4,))),
-    )(block_home, arrived, own, squares, *solved[-2:])
+        scratch=(pltpu.VMEM((width, total), F32), pltpu.SemaphoreType.DMA((blocks // STEPS,))),
+    )(block_home, arrived, mine, other, *owns, *squares)
     return out.T, variance[0]
 
 

time: 117 us -> 114 us (0.974)
  waiting for transfers between devices: 62.1 us -> 47.9 us
  starting transfers between devices: 26.7 us -> 34.5 us
  blocking collectives: 18.1 us -> 20.7 us
  Pallas kernels: 9.03 us -> 10.2 us
    ppermute x24 -> x20, waiting for transfers between devices: 62.1 us -> 47.9 us  [hop(): lax.ppermute(value, 'row', [(i, i ^ (odd if i % 2 else even)) for i in ra...]
    ppermute x24 -> x20, starting transfers between devices: 26.7 us -> 34.5 us  [hop(): lax.ppermute(value, 'row', [(i, i ^ (odd if i % 2 else even)) for i in ra...]
    all_to_all x1, blocking collectives: 18.1 us -> 20.7 us  [on_device(): lax.all_to_all(turned, 'row', split_axis=0, concat_axis=0, tiled=True)]
    pallas_call x4 -> x6, Pallas kernels: 4.18 us -> 5.37 us  [the longest x3 3.64 us: on_device(): call(functools.partial(early_kernel, k - 1, width), [shape((held_rows, co...]
  transfers between devices with their start and end apart: 24 -> 20, of which waited for: 23 -> 20; matrix products, arithmetic and copies ran while one was open for 0% -> 0% of each run, Pallas kernels for 2% -> 3%
where the time goes in v3:
time: 114 us; the launch traced here: 115 us
  waiting for transfers between devices  47.9 us (42%)
  starting transfers between devices  34.5 us (30%)
  blocking collectives  20.7 us (18%)
  Pallas kernels  10.2 us (9%)
    ppermute x20, waiting for transfers between devices, hop(): lax.ppermute(value, 'row', [(i, i ^ (odd if i % 2 else even)) for i in ra...  47.9 us
    ppermute x20, starting transfers between devices, hop(): lax.ppermute(value, 'row', [(i, i ^ (odd if i % 2 else even)) for i in ra...  34.5 us
    all_to_all x1, blocking collectives, on_device(): lax.all_to_all(turned, 'row', split_axis=0, concat_axis=0, tiled=True)  20.7 us
    pallas_call x3, Pallas kernels, on_device(): call(functools.partial(early_kernel, k - 1, width), [shape((held_rows, co...  3.64 us
    pallas_call x1, Pallas kernels, on_device(): call(functools.partial(order_kernel, slots, width), [shape((width, total)...  2.36 us
  transfers between devices with their start and end apart: 20, of which 20 were waited for; matrix products, arithmetic and copies ran while one was open for 0% of the time, Pallas kernels for 3%

profile of v3, /device:TPU:0, one launch (start us, length us, event | category | flops | bytes accessed | tf_op | source)
XLA Modules:
  0.0 114.7 jit_solution(12641648163157876777)
XLA Ops:
  3.2 2.9 %collective-permute-start.1 = (bf16[256,256]{1,0:T(8,128)(2,1)S(1)}, bf16[256,256]{1,0:T(8,128)(2,1)S(1)}, u32[]{:S(2)}, u32[]{:S(2)}) collective-permute-start(bf16[256,256]{1,0:T(8,128)(2,1)S(1)} %add.48), channel_id=1, source_target_pairs={{0,2},{1,9},{2,0},{3,11},{4,6},{5,13},{6,4},{7,15},{8,10},{9,1},{1... | collective-permute-start | bytes 393224 | tf_op jit(solution)/shard_map/ppermute | solution.py:374
  6.1 2.9 %collective-permute-done.1 = bf16[256,256]{1,0:T(8,128)(2,1)S(1)} collective-permute-done((bf16[256,256]{1,0:T(8,128)(2,1)S(1)}, bf16[256,256]{1,0:T(8,128)(2,1)S(1)}, u32[]{:S(2)}, u32[]{:S(2)}) %collective-permute-start.1) | collective-permute-done | bytes 131104 | tf_op jit(solution)/shard_map/ppermute | solution.py:374
  9.1 2.1 %collective-permute-start.2 = (bf16[256,256]{1,0:T(8,128)(2,1)S(1)}, bf16[256,256]{1,0:T(8,128)(2,1)S(1)}, u32[]{:S(2)}, u32[]{:S(2)}) collective-permute-start(bf16[256,256]{1,0:T(8,128)(2,1)S(1)} %add.49), channel_id=1, source_target_pairs={{0,4},{1,3},{2,6},{3,1},{4,0},{5,7},{6,2},{7,5},{8,12},{9,11},{10,... | collective-permute-start | bytes 393224 | tf_op jit(solution)/shard_map/ppermute | solution.py:374
  11.2 3.5 %collective-permute-done.2 = bf16[256,256]{1,0:T(8,128)(2,1)S(1)} collective-permute-done((bf16[256,256]{1,0:T(8,128)(2,1)S(1)}, bf16[256,256]{1,0:T(8,128)(2,1)S(1)}, u32[]{:S(2)}, u32[]{:S(2)}) %collective-permute-start.2) | collective-permute-done | bytes 131104 | tf_op jit(solution)/shard_map/ppermute | solution.py:374
  14.8 7.6 %collective-permute-start.3 = (bf16[256,256]{1,0:T(8,128)(2,1)S(1)}, bf16[256,256]{1,0:T(8,128)(2,1)S(1)}, u32[]{:S(2)}, u32[]{:S(2)}) collective-permute-start(bf16[256,256]{1,0:T(8,128)(2,1)S(1)} %add.50), channel_id=1, source_target_pairs={{0,8},{1,5},{2,10},{3,7},{4,12},{5,1},{6,14},{7,3},{8,0},{9,13},{1... | collective-permute-start | bytes 393224 | tf_op jit(solution)/shard_map/ppermute | solution.py:374
  22.4 3.7 %collective-permute-done.3 = bf16[256,256]{1,0:T(8,128)(2,1)S(1)} collective-permute-done((bf16[256,256]{1,0:T(8,128)(2,1)S(1)}, bf16[256,256]{1,0:T(8,128)(2,1)S(1)}, u32[]{:S(2)}, u32[]{:S(2)}) %collective-permute-start.3) | collective-permute-done | bytes 131104 | tf_op jit(solution)/shard_map/ppermute | solution.py:374
  26.2 1.3 %collective-permute-done.4.other = bf16[256,256]{1,0:T(8,128)(2,1)S(1)} collective-permute-done((bf16[256,256]{1,0:T(8,128)(2,1)S(1)}, bf16[256,256]{1,0:T(8,128)(2,1)S(1)}, u32[]{:S(2)}, u32[]{:S(2)}) %collective-permute-start.4) | collective-permute-done | bytes 131104 | tf_op jit(solution)/shard_map/ppermute | solution.py:374
  29.6 1.2 %shard_map.61 = (f32[1024,256]{1,0:T(8,128)S(1)}, f32[16,512]{1,0:T(8,128)S(1)}, f32[1,16]{1,0:T(1,128)S(1)}) custom-call(bf16[1024,2048]{1,0:T(8,128)(2,1)S(1)} %copy-done, f32[1024,256]{1,0:T(8,128)S(1)} %copy-done.1, bf16[256,256]{1,0:T(8,128)(2,1)S(1)} %get-tuple-element.40.after, bf16[256,256]{1,0:T(8,128)(2,1)S(1)} %add.51.mine, ...), custom_call_target="tpu_custom_call" | custom-call | flops 268435456 | tf_op jit(solution)/shard_map/pallas_call | solution.py:428
  30.9 3.7 %collective-permute-done.6 = bf16[256,256]{1,0:T(8,128)(2,1)S(1)} collective-permute-done((bf16[256,256]{1,0:T(8,128)(2,1)S(1)}, bf16[256,256]{1,0:T(8,128)(2,1)S(1)}, u32[]{:S(2)}, u32[]{:S(2)}) %collective-permute-start.6) | collective-permute-done | bytes 131104 | tf_op jit(solution)/shard_map/ppermute | solution.py:374
  34.6 1.9 %collective-permute-start.7 = (bf16[256,256]{1,0:T(8,128)(2,1)S(1)}, bf16[256,256]{1,0:T(8,128)(2,1)S(1)}, u32[]{:S(2)}, u32[]{:S(2)}) collective-permute-start(bf16[256,256]{1,0:T(8,128)(2,1)S(1)} %add.53), channel_id=1, source_target_pairs={{0,4},{1,3},{2,6},{3,1},{4,0},{5,7},{6,2},{7,5},{8,12},{9,11},{10,... | collective-permute-start | bytes 393224 | tf_op jit(solution)/shard_map/ppermute | solution.py:374
  36.5 3.1 %collective-permute-done.7 = bf16[256,256]{1,0:T(8,128)(2,1)S(1)} collective-permute-done((bf16[256,256]{1,0:T(8,128)(2,1)S(1)}, bf16[256,256]{1,0:T(8,128)(2,1)S(1)}, u32[]{:S(2)}, u32[]{:S(2)}) %collective-permute-start.7) | collective-permute-done | bytes 131104 | tf_op jit(solution)/shard_map/ppermute | solution.py:374
  39.7 4.1 %collective-permute-start.8 = (bf16[256,256]{1,0:T(8,128)(2,1)S(1)}, bf16[256,256]{1,0:T(8,128)(2,1)S(1)}, u32[]{:S(2)}, u32[]{:S(2)}) collective-permute-start(bf16[256,256]{1,0:T(8,128)(2,1)S(1)} %add.54), channel_id=1, source_target_pairs={{0,8},{1,5},{2,10},{3,7},{4,12},{5,1},{6,14},{7,3},{8,0},{9,13},{1... | collective-permute-start | bytes 393224 | tf_op jit(solution)/shard_map/ppermute | solution.py:374
  43.8 2.9 %collective-permute-done.8 = bf16[256,256]{1,0:T(8,128)(2,1)S(1)} collective-permute-done((bf16[256,256]{1,0:T(8,128)(2,1)S(1)}, bf16[256,256]{1,0:T(8,128)(2,1)S(1)}, u32[]{:S(2)}, u32[]{:S(2)}) %collective-permute-start.8) | collective-permute-done | bytes 131104 | tf_op jit(solution)/shard_map/ppermute | solution.py:374
  46.9 1.3 %collective-permute-done.9.other = bf16[256,256]{1,0:T(8,128)(2,1)S(1)} collective-permute-done((bf16[256,256]{1,0:T(8,128)(2,1)S(1)}, bf16[256,256]{1,0:T(8,128)(2,1)S(1)}, u32[]{:S(2)}, u32[]{:S(2)}) %collective-permute-start.9) | collective-permute-done | bytes 131104 | tf_op jit(solution)/shard_map/ppermute | solution.py:374
  50.3 1.2 %shard_map.63 = (f32[1024,256]{1,0:T(8,128)S(1)}, f32[16,512]{1,0:T(8,128)S(1)}, f32[1,16]{1,0:T(1,128)S(1)}) custom-call(bf16[1024,2048]{1,0:T(8,128)(2,1)S(1)} %copy-done, f32[1024,256]{1,0:T(8,128)S(1)} %get-tuple-element.44.rest.before, bf16[256,256]{1,0:T(8,128)(2,1)S(1)} %get-tuple-element.47.after, bf16[256,256]{1,0:T(8,128)(2,1)S(1)} %add.55.mine, ...), custom_call_target="tpu_custom_call" | custom-call | flops 268435456 | tf_op jit(solution)/shard_map/pallas_call | solution.py:428
  51.5 3.7 %collective-permute-done.11 = bf16[256,256]{1,0:T(8,128)(2,1)S(1)} collective-permute-done((bf16[256,256]{1,0:T(8,128)(2,1)S(1)}, bf16[256,256]{1,0:T(8,128)(2,1)S(1)}, u32[]{:S(2)}, u32[]{:S(2)}) %collective-permute-start.11) | collective-permute-done | bytes 131104 | tf_op jit(solution)/shard_map/ppermute | solution.py:374
  55.3 2.5 %collective-permute-start.12 = (bf16[256,256]{1,0:T(8,128)(2,1)S(1)}, bf16[256,256]{1,0:T(8,128)(2,1)S(1)}, u32[]{:S(2)}, u32[]{:S(2)}) collective-permute-start(bf16[256,256]{1,0:T(8,128)(2,1)S(1)} %add.57), channel_id=1, source_target_pairs={{0,4},{1,3},{2,6},{3,1},{4,0},{5,7},{6,2},{7,5},{8,12},{9,11},{10,... | collective-permute-start | bytes 393224 | tf_op jit(solution)/shard_map/ppermute | solution.py:374
  57.8 2.9 %collective-permute-done.12 = bf16[256,256]{1,0:T(8,128)(2,1)S(1)} collective-permute-done((bf16[256,256]{1,0:T(8,128)(2,1)S(1)}, bf16[256,256]{1,0:T(8,128)(2,1)S(1)}, u32[]{:S(2)}, u32[]{:S(2)}) %collective-permute-start.12) | collective-permute-done | bytes 131104 | tf_op jit(solution)/shard_map/ppermute | solution.py:374
  60.8 3.4 %collective-permute-start.13 = (bf16[256,256]{1,0:T(8,128)(2,1)S(1)}, bf16[256,256]{1,0:T(8,128)(2,1)S(1)}, u32[]{:S(2)}, u32[]{:S(2)}) collective-permute-start(bf16[256,256]{1,0:T(8,128)(2,1)S(1)} %add.58), channel_id=1, source_target_pairs={{0,8},{1,5},{2,10},{3,7},{4,12},{5,1},{6,14},{7,3},{8,0},{9,13},{1... | collective-permute-start | bytes 393224 | tf_op jit(solution)/shard_map/ppermute | solution.py:374
  64.2 2.9 %collective-permute-done.13 = bf16[256,256]{1,0:T(8,128)(2,1)S(1)} collective-permute-done((bf16[256,256]{1,0:T(8,128)(2,1)S(1)}, bf16[256,256]{1,0:T(8,128)(2,1)S(1)}, u32[]{:S(2)}, u32[]{:S(2)}) %collective-permute-start.13) | collective-permute-done | bytes 131104 | tf_op jit(solution)/shard_map/ppermute | solution.py:374
  67.3 1.3 %collective-permute-done.14.other = bf16[256,256]{1,0:T(8,128)(2,1)S(1)} collective-permute-done((bf16[256,256]{1,0:T(8,128)(2,1)S(1)}, bf16[256,256]{1,0:T(8,128)(2,1)S(1)}, u32[]{:S(2)}, u32[]{:S(2)}) %collective-permute-start.14) | collective-permute-done | bytes 131104 | tf_op jit(solution)/shard_map/ppermute | solution.py:374
  70.6 1.3 %collective-permute-start.16 = (bf16[256,256]{1,0:T(8,128)(2,1)S(1)}, bf16[256,256]{1,0:T(8,128)(2,1)S(1)}, u32[]{:S(2)}, u32[]{:S(2)}) collective-permute-start(bf16[256,256]{1,0:T(8,128)(2,1)S(1)} %add.60), channel_id=1, source_target_pairs={{0,2},{1,9},{2,0},{3,11},{4,6},{5,13},{6,4},{7,15},{8,10},{9,1},{1... | collective-permute-start | bytes 393224 | tf_op jit(solution)/shard_map/ppermute | solution.py:374
  72.0 1.2 %shard_map.65 = (f32[1024,256]{1,0:T(8,128)S(1)}, f32[16,512]{1,0:T(8,128)S(1)}, f32[1,16]{1,0:T(1,128)S(1)}) custom-call(bf16[1024,2048]{1,0:T(8,128)(2,1)S(1)} %copy-done, f32[1024,256]{1,0:T(8,128)S(1)} %get-tuple-element.51.rest.before, bf16[256,256]{1,0:T(8,128)(2,1)S(1)} %get-tuple-element.54.after, bf16[256,256]{1,0:T(8,128)(2,1)S(1)} %add.59.mine, ...), custom_call_target="tpu_custom_call" | custom-call | flops 268435456 | tf_op jit(solution)/shard_map/pallas_call | solution.py:428
  73.2 2.5 %collective-permute-done.16 = bf16[256,256]{1,0:T(8,128)(2,1)S(1)} collective-permute-done((bf16[256,256]{1,0:T(8,128)(2,1)S(1)}, bf16[256,256]{1,0:T(8,128)(2,1)S(1)}, u32[]{:S(2)}, u32[]{:S(2)}) %collective-permute-start.16) | collective-permute-done | bytes 131104 | tf_op jit(solution)/shard_map/ppermute | solution.py:374
  75.7 2.5 %collective-permute-start.17 = (bf16[256,256]{1,0:T(8,128)(2,1)S(1)}, bf16[256,256]{1,0:T(8,128)(2,1)S(1)}, u32[]{:S(2)}, u32[]{:S(2)}) collective-permute-start(bf16[256,256]{1,0:T(8,128)(2,1)S(1)} %add.61), channel_id=1, source_target_pairs={{0,4},{1,3},{2,6},{3,1},{4,0},{5,7},{6,2},{7,5},{8,12},{9,11},{10,... | collective-permute-start | bytes 393224 | tf_op jit(solution)/shard_map/ppermute | solution.py:374
  78.2 2.9 %collective-permute-done.17 = bf16[256,256]{1,0:T(8,128)(2,1)S(1)} collective-permute-done((bf16[256,256]{1,0:T(8,128)(2,1)S(1)}, bf16[256,256]{1,0:T(8,128)(2,1)S(1)}, u32[]{:S(2)}, u32[]{:S(2)}) %collective-permute-start.17) | collective-permute-done | bytes 131104 | tf_op jit(solution)/shard_map/ppermute | solution.py:374
  81.2 4.5 %collective-permute-start.18 = (bf16[256,256]{1,0:T(8,128)(2,1)S(1)}, bf16[256,256]{1,0:T(8,128)(2,1)S(1)}, u32[]{:S(2)}, u32[]{:S(2)}) collective-permute-start(bf16[256,256]{1,0:T(8,128)(2,1)S(1)} %add.62), channel_id=1, source_target_pairs={{0,8},{1,5},{2,10},{3,7},{4,12},{5,1},{6,14},{7,3},{8,0},{9,13},{1... | collective-permute-start | bytes 393224 | tf_op jit(solution)/shard_map/ppermute | solution.py:374
  85.7 2.9 %collective-permute-done.18 = bf16[256,256]{1,0:T(8,128)(2,1)S(1)} collective-permute-done((bf16[256,256]{1,0:T(8,128)(2,1)S(1)}, bf16[256,256]{1,0:T(8,128)(2,1)S(1)}, u32[]{:S(2)}, u32[]{:S(2)}) %collective-permute-start.18) | collective-permute-done | bytes 131104 | tf_op jit(solution)/shard_map/ppermute | solution.py:374
  88.7 1.3 %collective-permute-done.19.refs_1_.other = bf16[256,256]{1,0:T(8,128)(2,1)S(1)} collective-permute-done((bf16[256,256]{1,0:T(8,128)(2,1)S(1)}, bf16[256,256]{1,0:T(8,128)(2,1)S(1)}, u32[]{:S(2)}, u32[]{:S(2)}) %collective-permute-start.19) | collective-permute-done | bytes 131104 | tf_op jit(solution)/shard_map/ppermute | solution.py:374
  90.1 1.6 %shard_map.66 = bf16[256,1024]{1,0:T(8,128)(2,1)S(1)} custom-call(bf16[1024,2048]{1,0:T(8,128)(2,1)S(1)} %copy-done, f32[1024,256]{1,0:T(8,128)S(1)} %get-tuple-element.58.rest, bf16[256,256]{1,0:T(8,128)(2,1)S(1)} %add.63.refs_0_.mine, bf16[256,256]{1,0:T(8,128)(2,1)S(1)} %collective-permute-done.19.refs_1_.other), custom_call_target="tpu_custom_call" | custom-call | tf_op jit(solution)/shard_map/pallas_call | solution.py:438
  91.6 20.7 %all_to_all.11 = bf16[16,16,1024]{2,1,0:T(8,128)(2,1)S(1)} all-to-all(bf16[16,16,1024]{2,1,0:T(8,128)(2,1)S(1)} %bitcast.5), channel_id=1, replica_groups=mesh['groups'=2,'row'=16] {'row'}, dimensions={0} | all-to-all | bytes 1048576 | tf_op jit(solution)/shard_map/all_to_all | solution.py:441
  112.3 2.4 %shard_map.67 = (f32[16,16384]{1,0:T(8,128)}, f32[1,16]{1,0:T(1,128)}) custom-call(s32[32]{0:T(128)S(1)} %copy-done.2, bf16[256,1024]{1,0:T(8,128)(2,1)S(1)} %bitcast.6, bf16[256,256]{1,0:T(8,128)(2,1)S(1)} %add.63.refs_0_.mine, bf16[256,256]{1,0:T(8,128)(2,1)S(1)} %collective-permute-done.19.refs_1_.other, f32[16,512]{1,0:T(8,128)S(1)} %get-tuple-element.60.refs_0_, ...), custom_call_target="tpu_custom_call" | custom-call | tf_op jit(solution)/shard_map/pallas_call | solution.py:442
  (40 shorter events, 9.4 us)
Async XLA Ops:
  0.6 26.9 %copy-start = (bf16[1024,2048]{1,0:T(8,128)(2,1)S(1)}, bf16[1024,2048]{1,0:T(8,128)(2,1)}, u32[]{:S(2)}) copy-start(bf16[1024,2048]{1,0:T(8,128)(2,1)} %factor.15) | copy-start | bytes 12582916
  0.6 26.9 %copy-start.2 = (s32[32]{0:T(128)S(1)}, s32[32]{0:T(128)}, u32[]{:S(2)}) copy-start(s32[32]{0:T(128)} %home.7) | copy-start | bytes 388
  0.7 26.9 %copy-start.1 = (f32[1024,256]{1,0:T(8,128)S(1)}, f32[1024,256]{1,0:T(8,128)}, u32[]{:S(2)}) copy-start(f32[1024,256]{1,0:T(8,128)} %before.1) | copy-start | bytes 3145732
  1.6 1.5 %collective-permute-start = (bf16[256,256]{1,0:T(8,128)(2,1)S(1)}, bf16[256,256]{1,0:T(8,128)(2,1)S(1)}, u32[]{:S(2)}, u32[]{:S(2)}) collective-permute-start(bf16[256,256]{1,0:T(8,128)(2,1)S(1)} %get-tuple-element.38), channel_id=1, source_target_pairs={{0,1},{1,0},{2,3},{3,2},{4,5},{5,4},{6,7},{7,6},{8,9},{9,8},{10,11... | collective-permute-start | bytes 393224 | tf_op jit(solution)/shard_map/ppermute | solution.py:374
  3.2 5.9 %collective-permute-start.1 = (bf16[256,256]{1,0:T(8,128)(2,1)S(1)}, bf16[256,256]{1,0:T(8,128)(2,1)S(1)}, u32[]{:S(2)}, u32[]{:S(2)}) collective-permute-start(bf16[256,256]{1,0:T(8,128)(2,1)S(1)} %add.48), channel_id=1, source_target_pairs={{0,2},{1,9},{2,0},{3,11},{4,6},{5,13},{6,4},{7,15},{8,10},{9,1},{1... | collective-permute-start | bytes 393224 | tf_op jit(solution)/shard_map/ppermute | solution.py:374
  9.1 5.6 %collective-permute-start.2 = (bf16[256,256]{1,0:T(8,128)(2,1)S(1)}, bf16[256,256]{1,0:T(8,128)(2,1)S(1)}, u32[]{:S(2)}, u32[]{:S(2)}) collective-permute-start(bf16[256,256]{1,0:T(8,128)(2,1)S(1)} %add.49), channel_id=1, source_target_pairs={{0,4},{1,3},{2,6},{3,1},{4,0},{5,7},{6,2},{7,5},{8,12},{9,11},{10,... | collective-permute-start | bytes 393224 | tf_op jit(solution)/shard_map/ppermute | solution.py:374
  14.8 11.3 %collective-permute-start.3 = (bf16[256,256]{1,0:T(8,128)(2,1)S(1)}, bf16[256,256]{1,0:T(8,128)(2,1)S(1)}, u32[]{:S(2)}, u32[]{:S(2)}) collective-permute-start(bf16[256,256]{1,0:T(8,128)(2,1)S(1)} %add.50), channel_id=1, source_target_pairs={{0,8},{1,5},{2,10},{3,7},{4,12},{5,1},{6,14},{7,3},{8,0},{9,13},{1... | collective-permute-start | bytes 393224 | tf_op jit(solution)/shard_map/ppermute | solution.py:374
  26.1 1.4 %collective-permute-start.4 = (bf16[256,256]{1,0:T(8,128)(2,1)S(1)}, bf16[256,256]{1,0:T(8,128)(2,1)S(1)}, u32[]{:S(2)}, u32[]{:S(2)}) collective-permute-start(bf16[256,256]{1,0:T(8,128)(2,1)S(1)} %add.51.mine), channel_id=1, source_target_pairs={{0,1},{1,0},{2,3},{3,2},{4,5},{5,4},{6,7},{7,6},{8,9},{9,8},{10,11... | collective-permute-start | bytes 393224 | tf_op jit(solution)/shard_map/ppermute | solution.py:374
  28.1 1.4 %collective-permute-start.5 = (bf16[256,256]{1,0:T(8,128)(2,1)S(1)}, bf16[256,256]{1,0:T(8,128)(2,1)S(1)}, u32[]{:S(2)}, u32[]{:S(2)}) collective-permute-start(bf16[256,256]{1,0:T(8,128)(2,1)S(1)} %get-tuple-element.40.after), channel_id=1, source_target_pairs={{0,1},{1,0},{2,3},{3,2},{4,5},{5,4},{6,7},{7,6},{8,9},{9,8},{10,11... | collective-permute-start | bytes 393224 | tf_op jit(solution)/shard_map/ppermute | solution.py:374
  29.6 5.0 %collective-permute-start.6 = (bf16[256,256]{1,0:T(8,128)(2,1)S(1)}, bf16[256,256]{1,0:T(8,128)(2,1)S(1)}, u32[]{:S(2)}, u32[]{:S(2)}) collective-permute-start(bf16[256,256]{1,0:T(8,128)(2,1)S(1)} %add.52), channel_id=1, source_target_pairs={{0,2},{1,9},{2,0},{3,11},{4,6},{5,13},{6,4},{7,15},{8,10},{9,1},{1... | collective-permute-start | bytes 393224 | tf_op jit(solution)/shard_map/ppermute | solution.py:374
  34.6 5.0 %collective-permute-start.7 = (bf16[256,256]{1,0:T(8,128)(2,1)S(1)}, bf16[256,256]{1,0:T(8,128)(2,1)S(1)}, u32[]{:S(2)}, u32[]{:S(2)}) collective-permute-start(bf16[256,256]{1,0:T(8,128)(2,1)S(1)} %add.53), channel_id=1, source_target_pairs={{0,4},{1,3},{2,6},{3,1},{4,0},{5,7},{6,2},{7,5},{8,12},{9,11},{10,... | collective-permute-start | bytes 393224 | tf_op jit(solution)/shard_map/ppermute | solution.py:374
  39.7 7.1 %collective-permute-start.8 = (bf16[256,256]{1,0:T(8,128)(2,1)S(1)}, bf16[256,256]{1,0:T(8,128)(2,1)S(1)}, u32[]{:S(2)}, u32[]{:S(2)}) collective-permute-start(bf16[256,256]{1,0:T(8,128)(2,1)S(1)} %add.54), channel_id=1, source_target_pairs={{0,8},{1,5},{2,10},{3,7},{4,12},{5,1},{6,14},{7,3},{8,0},{9,13},{1... | collective-permute-start | bytes 393224 | tf_op jit(solution)/shard_map/ppermute | solution.py:374
  46.8 1.4 %collective-permute-start.9 = (bf16[256,256]{1,0:T(8,128)(2,1)S(1)}, bf16[256,256]{1,0:T(8,128)(2,1)S(1)}, u32[]{:S(2)}, u32[]{:S(2)}) collective-permute-start(bf16[256,256]{1,0:T(8,128)(2,1)S(1)} %add.55.mine), channel_id=1, source_target_pairs={{0,1},{1,0},{2,3},{3,2},{4,5},{5,4},{6,7},{7,6},{8,9},{9,8},{10,11... | collective-permute-start | bytes 393224 | tf_op jit(solution)/shard_map/ppermute | solution.py:374
  48.8 1.4 %collective-permute-start.10 = (bf16[256,256]{1,0:T(8,128)(2,1)S(1)}, bf16[256,256]{1,0:T(8,128)(2,1)S(1)}, u32[]{:S(2)}, u32[]{:S(2)}) collective-permute-start(bf16[256,256]{1,0:T(8,128)(2,1)S(1)} %get-tuple-element.47.after), channel_id=1, source_target_pairs={{0,1},{1,0},{2,3},{3,2},{4,5},{5,4},{6,7},{7,6},{8,9},{9,8},{10,11... | collective-permute-start | bytes 393224 | tf_op jit(solution)/shard_map/ppermute | solution.py:374
  50.2 5.0 %collective-permute-start.11 = (bf16[256,256]{1,0:T(8,128)(2,1)S(1)}, bf16[256,256]{1,0:T(8,128)(2,1)S(1)}, u32[]{:S(2)}, u32[]{:S(2)}) collective-permute-start(bf16[256,256]{1,0:T(8,128)(2,1)S(1)} %add.56), channel_id=1, source_target_pairs={{0,2},{1,9},{2,0},{3,11},{4,6},{5,13},{6,4},{7,15},{8,10},{9,1},{1... | collective-permute-start | bytes 393224 | tf_op jit(solution)/shard_map/ppermute | solution.py:374
  55.3 5.4 %collective-permute-start.12 = (bf16[256,256]{1,0:T(8,128)(2,1)S(1)}, bf16[256,256]{1,0:T(8,128)(2,1)S(1)}, u32[]{:S(2)}, u32[]{:S(2)}) collective-permute-start(bf16[256,256]{1,0:T(8,128)(2,1)S(1)} %add.57), channel_id=1, source_target_pairs={{0,4},{1,3},{2,6},{3,1},{4,0},{5,7},{6,2},{7,5},{8,12},{9,11},{10,... | collective-permute-start | bytes 393224 | tf_op jit(solution)/shard_map/ppermute | solution.py:374
  60.8 6.4 %collective-permute-start.13 = (bf16[256,256]{1,0:T(8,128)(2,1)S(1)}, bf16[256,256]{1,0:T(8,128)(2,1)S(1)}, u32[]{:S(2)}, u32[]{:S(2)}) collective-permute-start(bf16[256,256]{1,0:T(8,128)(2,1)S(1)} %add.58), channel_id=1, source_target_pairs={{0,8},{1,5},{2,10},{3,7},{4,12},{5,1},{6,14},{7,3},{8,0},{9,13},{1... | collective-permute-start | bytes 393224 | tf_op jit(solution)/shard_map/ppermute | solution.py:374
  67.2 1.4 %collective-permute-start.14 = (bf16[256,256]{1,0:T(8,128)(2,1)S(1)}, bf16[256,256]{1,0:T(8,128)(2,1)S(1)}, u32[]{:S(2)}, u32[]{:S(2)}) collective-permute-start(bf16[256,256]{1,0:T(8,128)(2,1)S(1)} %add.59.mine), channel_id=1, source_target_pairs={{0,1},{1,0},{2,3},{3,2},{4,5},{5,4},{6,7},{7,6},{8,9},{9,8},{10,11... | collective-permute-start | bytes 393224 | tf_op jit(solution)/shard_map/ppermute | solution.py:374
  69.2 1.4 %collective-permute-start.15 = (bf16[256,256]{1,0:T(8,128)(2,1)S(1)}, bf16[256,256]{1,0:T(8,128)(2,1)S(1)}, u32[]{:S(2)}, u32[]{:S(2)}) collective-permute-start(bf16[256,256]{1,0:T(8,128)(2,1)S(1)} %get-tuple-element.54.after), channel_id=1, source_target_pairs={{0,1},{1,0},{2,3},{3,2},{4,5},{5,4},{6,7},{7,6},{8,9},{9,8},{10,11... | collective-permute-start | bytes 393224 | tf_op jit(solution)/shard_map/ppermute | solution.py:374
  70.6 5.0 %collective-permute-start.16 = (bf16[256,256]{1,0:T(8,128)(2,1)S(1)}, bf16[256,256]{1,0:T(8,128)(2,1)S(1)}, u32[]{:S(2)}, u32[]{:S(2)}) collective-permute-start(bf16[256,256]{1,0:T(8,128)(2,1)S(1)} %add.60), channel_id=1, source_target_pairs={{0,2},{1,9},{2,0},{3,11},{4,6},{5,13},{6,4},{7,15},{8,10},{9,1},{1... | collective-permute-start | bytes 393224 | tf_op jit(solution)/shard_map/ppermute | solution.py:374
  75.7 5.4 %collective-permute-start.17 = (bf16[256,256]{1,0:T(8,128)(2,1)S(1)}, bf16[256,256]{1,0:T(8,128)(2,1)S(1)}, u32[]{:S(2)}, u32[]{:S(2)}) collective-permute-start(bf16[256,256]{1,0:T(8,128)(2,1)S(1)} %add.61), channel_id=1, source_target_pairs={{0,4},{1,3},{2,6},{3,1},{4,0},{5,7},{6,2},{7,5},{8,12},{9,11},{10,... | collective-permute-start | bytes 393224 | tf_op jit(solution)/shard_map/ppermute | solution.py:374
  81.2 7.4 %collective-permute-start.18 = (bf16[256,256]{1,0:T(8,128)(2,1)S(1)}, bf16[256,256]{1,0:T(8,128)(2,1)S(1)}, u32[]{:S(2)}, u32[]{:S(2)}) collective-permute-start(bf16[256,256]{1,0:T(8,128)(2,1)S(1)} %add.62), channel_id=1, source_target_pairs={{0,8},{1,5},{2,10},{3,7},{4,12},{5,1},{6,14},{7,3},{8,0},{9,13},{1... | collective-permute-start | bytes 393224 | tf_op jit(solution)/shard_map/ppermute | solution.py:374
  88.6 1.4 %collective-permute-start.19 = (bf16[256,256]{1,0:T(8,128)(2,1)S(1)}, bf16[256,256]{1,0:T(8,128)(2,1)S(1)}, u32[]{:S(2)}, u32[]{:S(2)}) collective-permute-start(bf16[256,256]{1,0:T(8,128)(2,1)S(1)} %add.63.refs_0_.mine), channel_id=1, source_target_pairs={{0,1},{1,0},{2,3},{3,2},{4,5},{5,4},{6,7},{7,6},{8,9},{9,8},{10,11... | collective-permute-start | bytes 393224 | tf_op jit(solution)/shard_map/ppermute | solution.py:374

commit v4 on v3

v4 whole, which is shorter than its diff:
```python
import functools

import jax
import jax.numpy as jnp
from jax import lax
from jax.experimental import pallas as pl
from jax.experimental.pallas import tpu as pltpu
from jax.sharding import PartitionSpec as P

BLOCK = 512
HALF = 256
STEPS = 4
PANEL = 2048
BF = jnp.bfloat16
F32 = jnp.float32
VMEM_LIMIT = 24 * 1024 * 1024


def mm(a, b):
    return jnp.dot(a, b, preferred_element_type=F32)


def mm_nt(a, b):
    return lax.dot_general(a, b, (((1,), (1,)), ((), ())), preferred_element_type=F32)


def parts(value):
    high = value.astype(BF)
    return high, (value - high.astype(F32)).astype(BF)


def mm3(a_high, a_low, b):
    b_high, b_low = parts(b)
    return mm(a_high, b_high) + (mm(a_high, b_low) + mm(a_low, b_high))


def odd_rows(value, size):
    picked = [value[at : at + size] for at in range(size, value.shape[0], 2 * size)]
    return picked[0] if len(picked) == 1 else jnp.concatenate(picked, axis=0)


def put_odd_rows(value, odd, size):
    pieces = []
    for at in range(0, value.shape[0], size):
        turn = at // size
        pieces.append(
            value[at : at + size] if turn % 2 == 0 else odd[turn // 2 * size : (turn // 2 + 1) * size]
        )
    return jnp.concatenate(pieces, axis=0)


def double(tile, inverse, halves, size, apart, lower):
    high, low = halves
    width = tile.shape[1]
    link = jnp.where((lax.shift_right_logical(apart, size.bit_length() - 1) == 1) & lower, tile, 0.0)
    link = link.astype(BF)
    packed = size >= 16
    if packed:
        link = odd_rows(link, size)
        left_high, left_low = odd_rows(high, size), odd_rows(low, size)
    else:
        left_high, left_low = high, low
    if width <= 128:
        both = mm(link, jnp.concatenate([high, low], axis=1))
        inner = both[:, :width] + both[:, width:]
    else:
        inner = mm(link, high) + mm(link, low)
    if packed:
        zero = jnp.zeros((size, width), F32)
        pieces = []
        for at in range(inner.shape[0] // size):
            pieces += [zero, inner[at * size : (at + 1) * size]]
        inner = jnp.concatenate(pieces, axis=0)
    inner_high, inner_low = parts(inner)
    if width <= 128:
        rows = left_high.shape[0]
        both = mm(
            jnp.concatenate([left_high, left_low], axis=0),
            jnp.concatenate([inner_high, inner_low], axis=1),
        )
        change = both[:rows, :width] + (both[:rows, width:] + both[rows:, :width])
    else:
        change = mm(left_high, inner_high) + (mm(left_high, inner_low) + mm(left_low, inner_high))
    if packed:
        inverse = put_odd_rows(inverse, odd_rows(inverse, size) - change, size)
    else:
        inverse = inverse - change
    return inverse, parts(inverse)


def index_maps(shape):
    row = lax.broadcasted_iota(jnp.int32, shape, 0)
    col = lax.broadcasted_iota(jnp.int32, shape, 1)
    return row == col, row ^ col, row > col


def invert(tiles, pivot_rows):
    quarter = HALF // 2
    on, apart, lower = index_maps((quarter, quarter))
    small, values = [], []
    for tile, pivot in zip(tiles, pivot_rows):
        for at in range(0, HALF, quarter):
            piece = tile[at : at + quarter, at : at + quarter].astype(F32)
            across = 1.0 / pivot[:, at : at + quarter]
            diag = jnp.where(on, across, 0.0)
            down = jnp.sum(diag, axis=1, keepdims=True)
            first = jnp.where((apart == 1) & lower, piece, 0.0)
            small.append(piece)
            values.append(diag - down * first * across)
    halves = [parts(value) for value in values]
    size = 2
    while size < quarter:
        for at, piece in enumerate(small):
            values[at], halves[at] = double(piece, values[at], halves[at], size, apart, lower)
        size *= 2
    zero = jnp.zeros((quarter, quarter), F32)
    _, apart, lower = index_maps((HALF, HALF))
    result = []
    for at, tile in enumerate(tiles):
        value = jnp.concatenate(
            [
                jnp.concatenate([values[2 * at], zero], axis=1),
                jnp.concatenate([zero, values[2 * at + 1]], axis=1),
            ],
            axis=0,
        )
        result.append(double(tile.astype(F32), value, parts(value), quarter, apart, lower)[1])
    return result


def solve(tile_cross, inv, rows):
    (a_high, a_low), (b_high, b_low) = inv
    top = mm3(a_high, a_low, rows[:HALF])
    top_high, top_low = parts(top)
    rest = rows[HALF:] - (mm(tile_cross, top_high) + mm(tile_cross, top_low))
    return top.astype(BF), mm3(b_high, b_low, rest).astype(BF)


def first_kernel(slots, home_ref, factor, pivots, rows, keep, send, home, tile, pivot, value, sems):
    me = lax.axis_index("row")
    fetch_home = pltpu.make_async_copy(home_ref, home, sems.at[0])
    fetch_pivot = pltpu.make_async_copy(pivots, pivot, sems.at[1])
    fetch_home.start()
    fetch_pivot.start()
    fetch_home.wait()
    owner = home[0] // slots == me
    r0 = pl.multiple_of(home[0] % slots * BLOCK, BLOCK)
    fetch_tile = pltpu.make_async_copy(
        factor.at[pl.ds(r0, BLOCK), pl.ds(0, BLOCK)], tile, sems.at[2]
    )
    fetch_rows = pltpu.make_async_copy(rows.at[pl.ds(r0, BLOCK), :], value, sems.at[3])

    @pl.when(owner)
    def _():
        fetch_tile.start()
        fetch_rows.start()

    fetch_pivot.wait()

    @pl.when(owner)
    def _():
        fetch_tile.wait()
        pieces = [tile[h * HALF : (h + 1) * HALF, h * HALF : (h + 1) * HALF] for h in range(2)]
        inv = invert(pieces, [pivot[:, h * HALF : (h + 1) * HALF] for h in range(2)])
        fetch_rows.wait()
        top, bottom = solve(tile[HALF:, :HALF], inv, value[...])
        half = keep.shape[1]
        first = me % 2 == 0
        for at, part in enumerate((top, bottom)):
            span = slice(at * HALF, (at + 1) * HALF)
            keep[span, :] = jnp.where(first, part[:, :half], part[:, half:])
            send[span, :] = jnp.where(first, part[:, half:], part[:, :half])

    @pl.when(jnp.logical_not(owner))
    def _():
        keep[...] = jnp.zeros_like(keep)
        send[...] = jnp.zeros_like(send)


def invert_kernel(slots, home, factor, factor_there, pivots, inv_high, inv_low):
    me = lax.axis_index("row")

    def one_block(k, carry):
        r0 = pl.multiple_of(home[k] % slots * BLOCK, BLOCK)
        c0 = pl.multiple_of(k * BLOCK, BLOCK)
        for there, held in enumerate((factor, factor_there)):

            @pl.when(home[k] // slots == (me ^ there))
            def _(held=held):
                pieces = [
                    held[pl.ds(r0 + h * HALF, HALF), pl.ds(c0 + h * HALF, HALF)] for h in range(2)
                ]
                pivot_rows = [pivots[:, pl.ds(c0 + h * HALF, HALF)] for h in range(2)]
                for h, (high, low) in enumerate(invert(pieces, pivot_rows)):
                    inv_high[k - 1, h] = high
                    inv_low[k - 1, h] = low

        return carry

    lax.fori_loop(1, STEPS, one_block, 0)


def step_kernel(k, slots, home, factor, factor_there, rows, rows_there, inv_high, inv_low, *refs):
    me = lax.axis_index("row")
    solved, piece = refs[:k], refs[k]
    half = piece.shape[1]
    r0 = pl.multiple_of(home[k] % slots * BLOCK, BLOCK)
    q0 = pl.multiple_of(me % 2 * half, half)
    inv = [(inv_high.at[k - 1, h], inv_low.at[k - 1, h]) for h in range(2)]
    for there, (held, right) in enumerate(((factor, rows), (factor_there, rows_there))):

        @pl.when(home[k] // slots == (me ^ there))
        def _(held=held, right=right):
            value = right[pl.ds(r0, BLOCK), pl.ds(q0, half)]
            for j in range(k):
                value = value - mm(
                    held[pl.ds(r0, BLOCK), j * BLOCK : (j + 1) * BLOCK], solved[j][...]
                )
            cross = held[pl.ds(r0 + HALF, HALF), k * BLOCK : k * BLOCK + HALF]
            top, bottom = solve(cross, [(high[...], low[...]) for high, low in inv], value)
            piece[:HALF, :] = top
            piece[HALF:, :] = bottom

    @pl.when(home[k] // (2 * slots) != me // 2)
    def _():
        piece[...] = jnp.zeros_like(piece)


def in_order(me, mine, other):
    first = me % 2 == 0
    here, there = mine[...], other[...]
    return jnp.concatenate([jnp.where(first, here, there), jnp.where(first, there, here)], axis=1)


def columns_of(half, me, width):
    columns = half.shape[1]
    pick = (
        lax.broadcasted_iota(jnp.int32, (width, columns), 1)
        == lax.broadcasted_iota(jnp.int32, (width, columns), 0) + me * width
    ).astype(F32).astype(BF)
    return mm_nt(pick, half)


def row_of_squares(value):
    high, low = parts(value * value)
    ones = jnp.ones((8, value.shape[1]), BF)
    return (mm_nt(ones, high) + mm_nt(ones, low))[:1]


def early_kernel(k, width, factor, before, mine, other, rest, own, squares):
    me = lax.axis_index("row")
    full = in_order(me, mine, other)

    for r0 in range(0, before.shape[0], HALF):
        span = slice(r0, r0 + HALF)
        rest[span, :] = before[span, :] - mm(factor[span, k * BLOCK : (k + 1) * BLOCK], full)
    own_columns(me, width, full, own, squares)


def own_columns(me, width, full, own, squares):
    value = columns_of(full, me, width)
    own[...] = value
    squares[...] = row_of_squares(value)


def last_kernel(width, factor, rest, mine, other, out, own, squares):
    me = lax.axis_index("row")
    full = in_order(me, mine, other)
    on, _, _ = index_maps((HALF, HALF))
    eye = on.astype(F32).astype(BF)
    columns = rest.shape[1]
    for r0 in range(0, rest.shape[0], HALF):
        span = slice(r0, r0 + HALF)
        value = rest[span, :] - mm(factor[span, (STEPS - 1) * BLOCK :], full)
        value = value.astype(BF)
        for c in range(0, columns, HALF):
            out[c : c + HALF, span] = mm_nt(eye, value[:, c : c + HALF]).astype(BF)
    own_columns(me, width, full, own, squares)


def order_kernel(slots, width, home, arrived, *refs):
    owns, squares = refs[:STEPS], refs[STEPS : 2 * STEPS]
    out, variance, held, sems = refs[2 * STEPS :]
    blocks = held.shape[1] // BLOCK
    group = STEPS

    def put_out(at):
        span = pl.ds(pl.multiple_of(at * group * BLOCK, BLOCK), group * BLOCK)
        return pltpu.make_async_copy(held.at[:, span], out.at[:, span], sems.at[at])

    def place_group(at, carry):
        for turn_at in range(group):
            g = at * group + turn_at
            spot = home[g]
            r0 = pl.multiple_of((spot // slots) * width, width)
            c0 = pl.multiple_of((spot % slots) * BLOCK, BLOCK)
            o0 = pl.multiple_of(g * BLOCK, BLOCK)
            held[:, pl.ds(o0, BLOCK)] = arrived[pl.ds(r0, width), pl.ds(c0, BLOCK)].astype(F32)
        put_out(at).start()
        return carry

    total = jnp.zeros((1, width), F32)
    for j in range(STEPS):
        held[:, j * BLOCK : (j + 1) * BLOCK] = owns[j][...]
        total = total + squares[j][...]
    variance[...] = total * (1.0 / (STEPS * BLOCK))
    put_out(0).start()
    lax.fori_loop(1, blocks // group, place_group, 0)

    def drain(at, carry):
        put_out(at).wait()
        return carry

    lax.fori_loop(0, blocks // group, drain, 0)


def call(kernel, outs, in_specs, out_specs, scalars=0, scratch=(), flops=0):
    return pl.pallas_call(
        kernel,
        grid_spec=pltpu.PrefetchScalarGridSpec(
            num_scalar_prefetch=scalars,
            in_specs=in_specs,
            out_specs=out_specs,
            scratch_shapes=scratch,
        ),
        out_shape=outs,
        compiler_params=pltpu.CompilerParams(vmem_limit_bytes=VMEM_LIMIT),
        cost_estimate=pl.CostEstimate(flops=flops, bytes_accessed=0, transcendentals=0),
    )


def hop(value, count, even, odd):
    return lax.ppermute(
        value, "row", [(i, i ^ (odd if i % 2 else even)) for i in range(count)]
    )


def spread(value, count, needed, beside):
    masks = [1 << bit for bit in range(1, count.bit_length() - 1)]
    for at, mask in enumerate(masks):
        value = value + hop(value, count, mask, masks[at - 1])
        if at == 0:
            value, needed = lax.optimization_barrier((value, needed))
            done = beside(needed)
        elif at == 1:
            value, *done = lax.optimization_barrier((value, *done))
    return value, done


def on_device(factor_panel, pivots, right_sides, block_home):
    slots = factor_panel.shape[0] // BLOCK
    held_rows, columns = right_sides.shape
    count = lax.axis_size("row")
    width = columns // count
    blocks = block_home.shape[0]
    total = blocks * BLOCK
    shape = jax.ShapeDtypeStruct
    half = shape((BLOCK, columns // 2), BF)
    inverse = shape((STEPS - 1, 2, HALF, HALF), BF)
    vmem = pl.BlockSpec(memory_space=pltpu.VMEM)
    hbm = pl.BlockSpec(memory_space=pltpu.HBM)
    pivot_row = pivots.reshape(1, PANEL)
    factor_there = hop(factor_panel, count, 1, 1)
    rows_there = hop(right_sides, count, 1, 1)
    keep, send = call(
        functools.partial(first_kernel, slots),
        [half, half],
        [hbm] * 4,
        [vmem] * 2,
        scratch=(
            pltpu.SMEM((blocks,), jnp.int32),
            pltpu.VMEM((BLOCK, BLOCK), BF),
            pltpu.VMEM((1, PANEL), F32),
            pltpu.VMEM((BLOCK, columns), F32),
            pltpu.SemaphoreType.DMA((4,)),
        ),
    )(*(
        pltpu.with_memory_space_constraint(value, pltpu.HBM)
        for value in (block_home, factor_panel, pivot_row, right_sides)
    ))
    mine = keep + hop(send, count, 1, 1)
    invert_rest = call(
        functools.partial(invert_kernel, slots),
        [inverse, inverse],
        [vmem] * 3,
        [vmem] * 2,
        scalars=1,
        flops=10**9,
    )
    mine, (inv_high, inv_low) = spread(
        keep + hop(send, count, 1, 1),
        count,
        factor_there,
        lambda there: invert_rest(block_home, factor_panel, there, pivot_row),
    )
    solved = [mine]
    rest = right_sides
    owns, squares = [], []
    own_shapes = [shape((width, BLOCK), F32), shape((1, width), F32)]
    for k in range(1, STEPS):
        (piece,) = call(
            functools.partial(step_kernel, k, slots), [half], [vmem] * (6 + k), [vmem], scalars=1
        )(
            block_home, factor_panel, factor_there, right_sides, rows_there, inv_high, inv_low, *solved
        )
        piece, shared = lax.optimization_barrier((piece, solved[-1]))
        update = call(
            functools.partial(early_kernel, k - 1, width),
            [shape((held_rows, columns), F32), *own_shapes],
            [vmem] * 4,
            [vmem] * 3,
            flops=2 * held_rows * columns * BLOCK,
        )
        mine, (rest, own, square) = spread(
            piece,
            count,
            hop(shared, count, 1, 1),
            lambda other: update(factor_panel, rest, shared, other),
        )
        solved.append(mine)
        owns.append(own)
        squares.append(square)
    turned, own, square = call(
        functools.partial(last_kernel, width),
        [shape((columns, held_rows), BF), *own_shapes],
        [vmem] * 4,
        [vmem] * 3,
    )(factor_panel, rest, mine, hop(mine, count, 1, 1))
    owns.append(own)
    squares.append(square)
    arrived = lax.all_to_all(turned, "row", split_axis=0, concat_axis=0, tiled=True)
    out, variance = call(
        functools.partial(order_kernel, slots, width),
        [shape((width, total), F32), shape((1, width), F32)],
        [vmem] * (1 + 2 * STEPS),
        [hbm, vmem],
        scalars=1,
        scratch=(pltpu.VMEM((width, total), F32), pltpu.SemaphoreType.DMA((blocks // STEPS,))),
    )(block_home, arrived, *owns, *squares)
    return out.T, variance[0]


def solution(mesh):
    in_specs = (P(("groups", "row"), None), P("groups"), P(("groups", "row"), None), P())
    out_specs = (P("groups", "row"), P(("groups", "row")))
    return jax.shard_map(
        on_device, mesh=mesh, in_specs=in_specs, out_specs=out_specs, check_vma=False
    )
```

time: 114 us -> 116 us (1.018)
  waiting for transfers between devices: 47.9 us -> 54.7 us
  starting transfers between devices: 34.5 us -> 30.8 us
    ppermute x20 -> x19, waiting for transfers between devices: 47.9 us -> 54.7 us  [hop(): lax.ppermute(value, 'row', [(i, i ^ (odd if i % 2 else even)) for i in ra...]
    ppermute x20 -> x19, starting transfers between devices: 34.5 us -> 30.8 us  [hop(): lax.ppermute(value, 'row', [(i, i ^ (odd if i % 2 else even)) for i in ra...]
    pallas_call x8 -> x9, Pallas kernels: 7.86 us -> 7.03 us  [the longest x3 1.99 us: on_device(): call(functools.partial(step_kernel, k, slots), [half], [vmem] * (6 + k),...]
  transfers between devices with their start and end apart: 20 -> 19, of which waited for: 20 -> 14; matrix products, arithmetic and copies ran while one was open for 0% -> 0% of each run, Pallas kernels for 3% -> 3%
where the time goes in v4:
time: 116 us; the launch traced here: 117 us
  waiting for transfers between devices  54.7 us (47%)
  starting transfers between devices  30.8 us (27%)
  blocking collectives  21.4 us (18%)
  Pallas kernels  9.12 us (8%)
    ppermute x19, waiting for transfers between devices, hop(): lax.ppermute(value, 'row', [(i, i ^ (odd if i % 2 else even)) for i in ra...  54.7 us
    ppermute x19, starting transfers between devices, hop(): lax.ppermute(value, 'row', [(i, i ^ (odd if i % 2 else even)) for i in ra...  30.8 us
    all_to_all x1, blocking collectives, on_device(): lax.all_to_all(turned, 'row', split_axis=0, concat_axis=0, tiled=True)  21.4 us
  transfers between devices with their start and end apart: 19, of which 14 were waited for; matrix products, arithmetic and copies ran while one was open for 0% of the time, Pallas kernels for 3%

profile of v4, /device:TPU:0, one launch (start us, length us, event | category | flops | bytes accessed | tf_op | source)
XLA Modules:
  0.0 117.5 jit_solution(17711538055888566863)
XLA Ops:
  1.3 1.1 shard_map.59
  2.9 7.0 %collective-permute-done.2 = bf16[512,128]{1,0:T(8,128)(2,1)S(1)} collective-permute-done((bf16[512,128]{1,0:T(8,128)(2,1)S(1)}, bf16[512,128]{1,0:T(8,128)(2,1)S(1)}, u32[]{:S(2)}, u32[]{:S(2)}) %collective-permute-start.2) | collective-permute-done | bytes 131104 | tf_op jit(solution)/shard_map/ppermute | solution.py:333
  9.9 2.9 %collective-permute-start.3 = (bf16[512,128]{1,0:T(8,128)(2,1)S(1)}, bf16[512,128]{1,0:T(8,128)(2,1)S(1)}, u32[]{:S(2)}, u32[]{:S(2)}) collective-permute-start(bf16[512,128]{1,0:T(8,128)(2,1)S(1)} %add.39), channel_id=1, source_target_pairs={{0,2},{1,9},{2,0},{3,11},{4,6},{5,13},{6,4},{7,15},{8,10},{9,1},{1... | collective-permute-start | bytes 393224 | tf_op jit(solution)/shard_map/ppermute | solution.py:333
  12.9 2.9 %collective-permute-done.3 = bf16[512,128]{1,0:T(8,128)(2,1)S(1)} collective-permute-done((bf16[512,128]{1,0:T(8,128)(2,1)S(1)}, bf16[512,128]{1,0:T(8,128)(2,1)S(1)}, u32[]{:S(2)}, u32[]{:S(2)}) %collective-permute-start.3) | collective-permute-done | bytes 131104 | tf_op jit(solution)/shard_map/ppermute | solution.py:333
  15.9 2.1 %collective-permute-start.4 = (bf16[512,128]{1,0:T(8,128)(2,1)S(1)}, bf16[512,128]{1,0:T(8,128)(2,1)S(1)}, u32[]{:S(2)}, u32[]{:S(2)}) collective-permute-start(bf16[512,128]{1,0:T(8,128)(2,1)S(1)} %add.40), channel_id=1, source_target_pairs={{0,4},{1,3},{2,6},{3,1},{4,0},{5,7},{6,2},{7,5},{8,12},{9,11},{10,... | collective-permute-start | bytes 393224 | tf_op jit(solution)/shard_map/ppermute | solution.py:333
  18.0 0.6 shard_map.60
  18.7 2.3 %collective-permute-done.4 = bf16[512,128]{1,0:T(8,128)(2,1)S(1)} collective-permute-done((bf16[512,128]{1,0:T(8,128)(2,1)S(1)}, bf16[512,128]{1,0:T(8,128)(2,1)S(1)}, u32[]{:S(2)}, u32[]{:S(2)}) %collective-permute-start.4) | collective-permute-done | bytes 131104 | tf_op jit(solution)/shard_map/ppermute | solution.py:333
  21.0 3.1 %collective-permute-start.5 = (bf16[512,128]{1,0:T(8,128)(2,1)S(1)}, bf16[512,128]{1,0:T(8,128)(2,1)S(1)}, u32[]{:S(2)}, u32[]{:S(2)}) collective-permute-start(bf16[512,128]{1,0:T(8,128)(2,1)S(1)} %add.41), channel_id=1, source_target_pairs={{0,8},{1,5},{2,10},{3,7},{4,12},{5,1},{6,14},{7,3},{8,0},{9,13},{1... | collective-permute-start | bytes 393224 | tf_op jit(solution)/shard_map/ppermute | solution.py:333
  24.1 3.0 %collective-permute-done.5 = bf16[512,128]{1,0:T(8,128)(2,1)S(1)} collective-permute-done((bf16[512,128]{1,0:T(8,128)(2,1)S(1)}, bf16[512,128]{1,0:T(8,128)(2,1)S(1)}, u32[]{:S(2)}, u32[]{:S(2)}) %collective-permute-start.5) | collective-permute-done | bytes 131104 | tf_op jit(solution)/shard_map/ppermute | solution.py:333
  27.2 0.6 shard_map.61
  27.8 2.8 %collective-permute-start.6 = (bf16[512,128]{1,0:T(8,128)(2,1)S(1)}, bf16[512,128]{1,0:T(8,128)(2,1)S(1)}, u32[]{:S(2)}, u32[]{:S(2)}) collective-permute-start(bf16[512,128]{1,0:T(8,128)(2,1)S(1)} %shard_map.61), channel_id=1, source_target_pairs={{0,2},{1,9},{2,0},{3,11},{4,6},{5,13},{6,4},{7,15},{8,10},{9,1},{1... | collective-permute-start | bytes 393224 | tf_op jit(solution)/shard_map/ppermute | solution.py:333
  30.6 2.9 %collective-permute-done.6 = bf16[512,128]{1,0:T(8,128)(2,1)S(1)} collective-permute-done((bf16[512,128]{1,0:T(8,128)(2,1)S(1)}, bf16[512,128]{1,0:T(8,128)(2,1)S(1)}, u32[]{:S(2)}, u32[]{:S(2)}) %collective-permute-start.6) | collective-permute-done | bytes 131104 | tf_op jit(solution)/shard_map/ppermute | solution.py:333
  33.6 2.7 %collective-permute-start.8 = (bf16[512,128]{1,0:T(8,128)(2,1)S(1)}, bf16[512,128]{1,0:T(8,128)(2,1)S(1)}, u32[]{:S(2)}, u32[]{:S(2)}) collective-permute-start(bf16[512,128]{1,0:T(8,128)(2,1)S(1)} %add.43), channel_id=1, source_target_pairs={{0,4},{1,3},{2,6},{3,1},{4,0},{5,7},{6,2},{7,5},{8,12},{9,11},{10,... | collective-permute-start | bytes 393224 | tf_op jit(solution)/shard_map/ppermute | solution.py:333
  36.9 2.4 %collective-permute-done.8 = bf16[512,128]{1,0:T(8,128)(2,1)S(1)} collective-permute-done((bf16[512,128]{1,0:T(8,128)(2,1)S(1)}, bf16[512,128]{1,0:T(8,128)(2,1)S(1)}, u32[]{:S(2)}, u32[]{:S(2)}) %collective-permute-start.8) | collective-permute-done | bytes 131104 | tf_op jit(solution)/shard_map/ppermute | solution.py:333
  39.3 2.6 %collective-permute-start.9 = (bf16[512,128]{1,0:T(8,128)(2,1)S(1)}, bf16[512,128]{1,0:T(8,128)(2,1)S(1)}, u32[]{:S(2)}, u32[]{:S(2)}) collective-permute-start(bf16[512,128]{1,0:T(8,128)(2,1)S(1)} %add.44), channel_id=1, source_target_pairs={{0,8},{1,5},{2,10},{3,7},{4,12},{5,1},{6,14},{7,3},{8,0},{9,13},{1... | collective-permute-start | bytes 393224 | tf_op jit(solution)/shard_map/ppermute | solution.py:333
  41.9 3.3 %collective-permute-done.9 = bf16[512,128]{1,0:T(8,128)(2,1)S(1)} collective-permute-done((bf16[512,128]{1,0:T(8,128)(2,1)S(1)}, bf16[512,128]{1,0:T(8,128)(2,1)S(1)}, u32[]{:S(2)}, u32[]{:S(2)}) %collective-permute-start.9) | collective-permute-done | bytes 131104 | tf_op jit(solution)/shard_map/ppermute | solution.py:333
  45.2 0.8 shard_map.63
  46.0 7.1 %collective-permute-start.10 = (bf16[512,128]{1,0:T(8,128)(2,1)S(1)}, bf16[512,128]{1,0:T(8,128)(2,1)S(1)}, u32[]{:S(2)}, u32[]{:S(2)}) collective-permute-start(bf16[512,128]{1,0:T(8,128)(2,1)S(1)} %shard_map.63), channel_id=1, source_target_pairs={{0,2},{1,9},{2,0},{3,11},{4,6},{5,13},{6,4},{7,15},{8,10},{9,1},{1... | collective-permute-start | bytes 393224 | tf_op jit(solution)/shard_map/ppermute | solution.py:333
  53.1 3.1 %collective-permute-done.10 = bf16[512,128]{1,0:T(8,128)(2,1)S(1)} collective-permute-done((bf16[512,128]{1,0:T(8,128)(2,1)S(1)}, bf16[512,128]{1,0:T(8,128)(2,1)S(1)}, u32[]{:S(2)}, u32[]{:S(2)}) %collective-permute-start.10) | collective-permute-done | bytes 131104 | tf_op jit(solution)/shard_map/ppermute | solution.py:333
  57.0 4.5 %collective-permute-done.12 = bf16[512,128]{1,0:T(8,128)(2,1)S(1)} collective-permute-done((bf16[512,128]{1,0:T(8,128)(2,1)S(1)}, bf16[512,128]{1,0:T(8,128)(2,1)S(1)}, u32[]{:S(2)}, u32[]{:S(2)}) %collective-permute-start.12) | collective-permute-done | bytes 131104 | tf_op jit(solution)/shard_map/ppermute | solution.py:333
  61.5 1.2 %collective-permute-start.13 = (bf16[512,128]{1,0:T(8,128)(2,1)S(1)}, bf16[512,128]{1,0:T(8,128)(2,1)S(1)}, u32[]{:S(2)}, u32[]{:S(2)}) collective-permute-start(bf16[512,128]{1,0:T(8,128)(2,1)S(1)} %add.47), channel_id=1, source_target_pairs={{0,8},{1,5},{2,10},{3,7},{4,12},{5,1},{6,14},{7,3},{8,0},{9,13},{1... | collective-permute-start | bytes 393224 | tf_op jit(solution)/shard_map/ppermute | solution.py:333
  62.7 8.8 %collective-permute-done.13 = bf16[512,128]{1,0:T(8,128)(2,1)S(1)} collective-permute-done((bf16[512,128]{1,0:T(8,128)(2,1)S(1)}, bf16[512,128]{1,0:T(8,128)(2,1)S(1)}, u32[]{:S(2)}, u32[]{:S(2)}) %collective-permute-start.13) | collective-permute-done | bytes 131104 | tf_op jit(solution)/shard_map/ppermute | solution.py:333
  71.5 0.6 shard_map.65
  72.2 3.0 %collective-permute-start.14 = (bf16[512,128]{1,0:T(8,128)(2,1)S(1)}, bf16[512,128]{1,0:T(8,128)(2,1)S(1)}, u32[]{:S(2)}, u32[]{:S(2)}) collective-permute-start(bf16[512,128]{1,0:T(8,128)(2,1)S(1)} %shard_map.65), channel_id=1, source_target_pairs={{0,2},{1,9},{2,0},{3,11},{4,6},{5,13},{6,4},{7,15},{8,10},{9,1},{1... | collective-permute-start | bytes 393224 | tf_op jit(solution)/shard_map/ppermute | solution.py:333
  75.2 3.1 %collective-permute-done.14 = bf16[512,128]{1,0:T(8,128)(2,1)S(1)} collective-permute-done((bf16[512,128]{1,0:T(8,128)(2,1)S(1)}, bf16[512,128]{1,0:T(8,128)(2,1)S(1)}, u32[]{:S(2)}, u32[]{:S(2)}) %collective-permute-start.14) | collective-permute-done | bytes 131104 | tf_op jit(solution)/shard_map/ppermute | solution.py:333
  78.9 4.5 %collective-permute-done.16 = bf16[512,128]{1,0:T(8,128)(2,1)S(1)} collective-permute-done((bf16[512,128]{1,0:T(8,128)(2,1)S(1)}, bf16[512,128]{1,0:T(8,128)(2,1)S(1)}, u32[]{:S(2)}, u32[]{:S(2)}) %collective-permute-start.16) | collective-permute-done | bytes 131104 | tf_op jit(solution)/shard_map/ppermute | solution.py:333
  83.5 1.8 %collective-permute-start.17 = (bf16[512,128]{1,0:T(8,128)(2,1)S(1)}, bf16[512,128]{1,0:T(8,128)(2,1)S(1)}, u32[]{:S(2)}, u32[]{:S(2)}) collective-permute-start(bf16[512,128]{1,0:T(8,128)(2,1)S(1)} %add.50), channel_id=1, source_target_pairs={{0,8},{1,5},{2,10},{3,7},{4,12},{5,1},{6,14},{7,3},{8,0},{9,13},{1... | collective-permute-start | bytes 393224 | tf_op jit(solution)/shard_map/ppermute | solution.py:333
  85.3 5.5 %collective-permute-done.17 = bf16[512,128]{1,0:T(8,128)(2,1)S(1)} collective-permute-done((bf16[512,128]{1,0:T(8,128)(2,1)S(1)}, bf16[512,128]{1,0:T(8,128)(2,1)S(1)}, u32[]{:S(2)}, u32[]{:S(2)}) %collective-permute-start.17) | collective-permute-done | bytes 131104 | tf_op jit(solution)/shard_map/ppermute | solution.py:333
  91.0 1.3 %collective-permute-done.18.other = bf16[512,128]{1,0:T(8,128)(2,1)S(1)} collective-permute-done((bf16[512,128]{1,0:T(8,128)(2,1)S(1)}, bf16[512,128]{1,0:T(8,128)(2,1)S(1)}, u32[]{:S(2)}, u32[]{:S(2)}) %collective-permute-start.18) | collective-permute-done | bytes 131104 | tf_op jit(solution)/shard_map/ppermute | solution.py:333
  92.3 1.6 %shard_map.67 = (bf16[256,1024]{1,0:T(8,128)(2,1)S(1)}, f32[16,512]{1,0:T(8,128)S(1)}, f32[1,16]{1,0:T(1,128)S(1)}) custom-call(bf16[1024,2048]{1,0:T(8,128)(2,1)S(1)} %copy-done, f32[1024,256]{1,0:T(8,128)S(1)} %get-tuple-element.83.rest, bf16[512,128]{1,0:T(8,128)(2,1)S(1)} %add.51.mine, bf16[512,128]{1,0:T(8,128)(2,1)S(1)} %collective-permute-done.18.other), custom_call_target="tpu_custom_call" | custom-call | tf_op jit(solution)/shard_map/pallas_call | solution.py:423
  93.9 21.4 %all_to_all.11 = bf16[16,16,1024]{2,1,0:T(8,128)(2,1)S(1)} all-to-all(bf16[16,16,1024]{2,1,0:T(8,128)(2,1)S(1)} %bitcast.6), channel_id=1, replica_groups=mesh['groups'=2,'row'=16] {'row'}, dimensions={0} | all-to-all | bytes 1048576 | tf_op jit(solution)/shard_map/all_to_all | solution.py:431
  115.3 2.1 %shard_map.68 = (f32[16,16384]{1,0:T(8,128)}, f32[1,16]{1,0:T(1,128)}) custom-call(s32[32]{0:T(128)S(1)} %copy-done.3, bf16[256,1024]{1,0:T(8,128)(2,1)S(1)} %bitcast.5, f32[16,512]{1,0:T(8,128)S(1)} %get-tuple-element.86.refs_0_, f32[16,512]{1,0:T(8,128)S(1)} %get-tuple-element.87.refs_1_, f32[16,512]{1,0:T(8,128)S(1)} %get-tuple-element.88.refs_2_, ...), custom_call_target="tpu_custom_call" | custom-call | tf_op jit(solution)/shard_map/pallas_call | solution.py:432
  (38 shorter events, 3.6 us)
Async XLA Ops:
  0.6 17.4 %copy-start = (bf16[1024,2048]{1,0:T(8,128)(2,1)S(1)}, bf16[1024,2048]{1,0:T(8,128)(2,1)}, u32[]{:S(2)}) copy-start(bf16[1024,2048]{1,0:T(8,128)(2,1)} %factor.17) | copy-start | bytes 12582916
  0.6 17.4 %copy-start.3 = (s32[32]{0:T(128)S(1)}, s32[32]{0:T(128)}, u32[]{:S(2)}) copy-start(s32[32]{0:T(128)} %home.9) | copy-start | bytes 388
  0.6 17.4 %copy-start.2 = (f32[2048]{0:T(1024)S(1)}, f32[2048]{0:T(1024)}, u32[]{:S(2)}) copy-start(f32[2048]{0:T(1024)} %param.5) | copy-start | bytes 24580
  0.7 15.2 %collective-permute-start = (bf16[1024,2048]{1,0:T(8,128)(2,1)}, bf16[1024,2048]{1,0:T(8,128)(2,1)S(1)}, u32[]{:S(2)}, u32[]{:S(2)}) collective-permute-start(bf16[1024,2048]{1,0:T(8,128)(2,1)} %factor.17), channel_id=1, source_target_pairs={{0,1},{1,0},{2,3},{3,2},{4,5},{5,4},{6,7},{7,6},{8,9},{9,8},{10,11... | collective-permute-start | bytes 12582920 | tf_op jit(solution)/shard_map/ppermute | solution.py:333
  1.2 26.0 %collective-permute-start.1 = (f32[1024,256]{1,0:T(8,128)}, f32[1024,256]{1,0:T(8,128)S(1)}, u32[]{:S(2)}, u32[]{:S(2)}) collective-permute-start(f32[1024,256]{1,0:T(8,128)} %rows.7), channel_id=1, source_target_pairs={{0,1},{1,0},{2,3},{3,2},{4,5},{5,4},{6,7},{7,6},{8,9},{9,8},{10,11... | collective-permute-start | bytes 3145736 | tf_op jit(solution)/shard_map/ppermute | solution.py:333
  2.4 7.5 %collective-permute-start.2 = (bf16[512,128]{1,0:T(8,128)(2,1)S(1)}, bf16[512,128]{1,0:T(8,128)(2,1)S(1)}, u32[]{:S(2)}, u32[]{:S(2)}) collective-permute-start(bf16[512,128]{1,0:T(8,128)(2,1)S(1)} %get-tuple-element.50), channel_id=1, source_target_pairs={{0,1},{1,0},{2,3},{3,2},{4,5},{5,4},{6,7},{7,6},{8,9},{9,8},{10,11... | collective-permute-start | bytes 393224 | tf_op jit(solution)/shard_map/ppermute | solution.py:333
  9.9 5.9 %collective-permute-start.3 = (bf16[512,128]{1,0:T(8,128)(2,1)S(1)}, bf16[512,128]{1,0:T(8,128)(2,1)S(1)}, u32[]{:S(2)}, u32[]{:S(2)}) collective-permute-start(bf16[512,128]{1,0:T(8,128)(2,1)S(1)} %add.39), channel_id=1, source_target_pairs={{0,2},{1,9},{2,0},{3,11},{4,6},{5,13},{6,4},{7,15},{8,10},{9,1},{1... | collective-permute-start | bytes 393224 | tf_op jit(solution)/shard_map/ppermute | solution.py:333
  15.9 11.3 %copy-start.1 = (f32[1024,256]{1,0:T(8,128)S(1)}, f32[1024,256]{1,0:T(8,128)}, u32[]{:S(2)}) copy-start(f32[1024,256]{1,0:T(8,128)} %rows.7) | copy-start | bytes 3145732
  15.9 5.1 %collective-permute-start.4 = (bf16[512,128]{1,0:T(8,128)(2,1)S(1)}, bf16[512,128]{1,0:T(8,128)(2,1)S(1)}, u32[]{:S(2)}, u32[]{:S(2)}) collective-permute-start(bf16[512,128]{1,0:T(8,128)(2,1)S(1)} %add.40), channel_id=1, source_target_pairs={{0,4},{1,3},{2,6},{3,1},{4,0},{5,7},{6,2},{7,5},{8,12},{9,11},{10,... | collective-permute-start | bytes 393224 | tf_op jit(solution)/shard_map/ppermute | solution.py:333
  21.0 6.1 %collective-permute-start.5 = (bf16[512,128]{1,0:T(8,128)(2,1)S(1)}, bf16[512,128]{1,0:T(8,128)(2,1)S(1)}, u32[]{:S(2)}, u32[]{:S(2)}) collective-permute-start(bf16[512,128]{1,0:T(8,128)(2,1)S(1)} %add.41), channel_id=1, source_target_pairs={{0,8},{1,5},{2,10},{3,7},{4,12},{5,1},{6,14},{7,3},{8,0},{9,13},{1... | collective-permute-start | bytes 393224 | tf_op jit(solution)/shard_map/ppermute | solution.py:333
  27.8 5.7 %collective-permute-start.6 = (bf16[512,128]{1,0:T(8,128)(2,1)S(1)}, bf16[512,128]{1,0:T(8,128)(2,1)S(1)}, u32[]{:S(2)}, u32[]{:S(2)}) collective-permute-start(bf16[512,128]{1,0:T(8,128)(2,1)S(1)} %shard_map.61), channel_id=1, source_target_pairs={{0,2},{1,9},{2,0},{3,11},{4,6},{5,13},{6,4},{7,15},{8,10},{9,1},{1... | collective-permute-start | bytes 393224 | tf_op jit(solution)/shard_map/ppermute | solution.py:333
  30.6 3.0 %collective-permute-start.7 = (bf16[512,128]{1,0:T(8,128)(2,1)S(1)}, bf16[512,128]{1,0:T(8,128)(2,1)S(1)}, u32[]{:S(2)}, u32[]{:S(2)}) collective-permute-start(bf16[512,128]{1,0:T(8,128)(2,1)S(1)} %add.42.refs_0_.mine), channel_id=1, source_target_pairs={{0,1},{1,0},{2,3},{3,2},{4,5},{5,4},{6,7},{7,6},{8,9},{9,8},{10,11... | collective-permute-start | bytes 393224 | tf_op jit(solution)/shard_map/ppermute | solution.py:333
  33.6 5.6 %collective-permute-start.8 = (bf16[512,128]{1,0:T(8,128)(2,1)S(1)}, bf16[512,128]{1,0:T(8,128)(2,1)S(1)}, u32[]{:S(2)}, u32[]{:S(2)}) collective-permute-start(bf16[512,128]{1,0:T(8,128)(2,1)S(1)} %add.43), channel_id=1, source_target_pairs={{0,4},{1,3},{2,6},{3,1},{4,0},{5,7},{6,2},{7,5},{8,12},{9,11},{10,... | collective-permute-start | bytes 393224 | tf_op jit(solution)/shard_map/ppermute | solution.py:333
  39.3 5.9 %collective-permute-start.9 = (bf16[512,128]{1,0:T(8,128)(2,1)S(1)}, bf16[512,128]{1,0:T(8,128)(2,1)S(1)}, u32[]{:S(2)}, u32[]{:S(2)}) collective-permute-start(bf16[512,128]{1,0:T(8,128)(2,1)S(1)} %add.44), channel_id=1, source_target_pairs={{0,8},{1,5},{2,10},{3,7},{4,12},{5,1},{6,14},{7,3},{8,0},{9,13},{1... | collective-permute-start | bytes 393224 | tf_op jit(solution)/shard_map/ppermute | solution.py:333
  46.0 10.2 %collective-permute-start.10 = (bf16[512,128]{1,0:T(8,128)(2,1)S(1)}, bf16[512,128]{1,0:T(8,128)(2,1)S(1)}, u32[]{:S(2)}, u32[]{:S(2)}) collective-permute-start(bf16[512,128]{1,0:T(8,128)(2,1)S(1)} %shard_map.63), channel_id=1, source_target_pairs={{0,2},{1,9},{2,0},{3,11},{4,6},{5,13},{6,4},{7,15},{8,10},{9,1},{1... | collective-permute-start | bytes 393224 | tf_op jit(solution)/shard_map/ppermute | solution.py:333
  53.1 3.1 %collective-permute-start.11 = (bf16[512,128]{1,0:T(8,128)(2,1)S(1)}, bf16[512,128]{1,0:T(8,128)(2,1)S(1)}, u32[]{:S(2)}, u32[]{:S(2)}) collective-permute-start(bf16[512,128]{1,0:T(8,128)(2,1)S(1)} %add.45.refs_1_.mine), channel_id=1, source_target_pairs={{0,1},{1,0},{2,3},{3,2},{4,5},{5,4},{6,7},{7,6},{8,9},{9,8},{10,11... | collective-permute-start | bytes 393224 | tf_op jit(solution)/shard_map/ppermute | solution.py:333
  56.3 5.2 %collective-permute-start.12 = (bf16[512,128]{1,0:T(8,128)(2,1)S(1)}, bf16[512,128]{1,0:T(8,128)(2,1)S(1)}, u32[]{:S(2)}, u32[]{:S(2)}) collective-permute-start(bf16[512,128]{1,0:T(8,128)(2,1)S(1)} %add.46), channel_id=1, source_target_pairs={{0,4},{1,3},{2,6},{3,1},{4,0},{5,7},{6,2},{7,5},{8,12},{9,11},{10,... | collective-permute-start | bytes 393224 | tf_op jit(solution)/shard_map/ppermute | solution.py:333
  61.5 10.0 %collective-permute-start.13 = (bf16[512,128]{1,0:T(8,128)(2,1)S(1)}, bf16[512,128]{1,0:T(8,128)(2,1)S(1)}, u32[]{:S(2)}, u32[]{:S(2)}) collective-permute-start(bf16[512,128]{1,0:T(8,128)(2,1)S(1)} %add.47), channel_id=1, source_target_pairs={{0,8},{1,5},{2,10},{3,7},{4,12},{5,1},{6,14},{7,3},{8,0},{9,13},{1... | collective-permute-start | bytes 393224 | tf_op jit(solution)/shard_map/ppermute | solution.py:333
  72.2 6.1 %collective-permute-start.14 = (bf16[512,128]{1,0:T(8,128)(2,1)S(1)}, bf16[512,128]{1,0:T(8,128)(2,1)S(1)}, u32[]{:S(2)}, u32[]{:S(2)}) collective-permute-start(bf16[512,128]{1,0:T(8,128)(2,1)S(1)} %shard_map.65), channel_id=1, source_target_pairs={{0,2},{1,9},{2,0},{3,11},{4,6},{5,13},{6,4},{7,15},{8,10},{9,1},{1... | collective-permute-start | bytes 393224 | tf_op jit(solution)/shard_map/ppermute | solution.py:333
  75.1 3.1 %collective-permute-start.15 = (bf16[512,128]{1,0:T(8,128)(2,1)S(1)}, bf16[512,128]{1,0:T(8,128)(2,1)S(1)}, u32[]{:S(2)}, u32[]{:S(2)}) collective-permute-start(bf16[512,128]{1,0:T(8,128)(2,1)S(1)} %add.48.refs_2_.mine), channel_id=1, source_target_pairs={{0,1},{1,0},{2,3},{3,2},{4,5},{5,4},{6,7},{7,6},{8,9},{9,8},{10,11... | collective-permute-start | bytes 393224 | tf_op jit(solution)/shard_map/ppermute | solution.py:333
  78.3 5.2 %collective-permute-start.16 = (bf16[512,128]{1,0:T(8,128)(2,1)S(1)}, bf16[512,128]{1,0:T(8,128)(2,1)S(1)}, u32[]{:S(2)}, u32[]{:S(2)}) collective-permute-start(bf16[512,128]{1,0:T(8,128)(2,1)S(1)} %add.49), channel_id=1, source_target_pairs={{0,4},{1,3},{2,6},{3,1},{4,0},{5,7},{6,2},{7,5},{8,12},{9,11},{10,... | collective-permute-start | bytes 393224 | tf_op jit(solution)/shard_map/ppermute | solution.py:333
  83.5 7.3 %collective-permute-start.17 = (bf16[512,128]{1,0:T(8,128)(2,1)S(1)}, bf16[512,128]{1,0:T(8,128)(2,1)S(1)}, u32[]{:S(2)}, u32[]{:S(2)}) collective-permute-start(bf16[512,128]{1,0:T(8,128)(2,1)S(1)} %add.50), channel_id=1, source_target_pairs={{0,8},{1,5},{2,10},{3,7},{4,12},{5,1},{6,14},{7,3},{8,0},{9,13},{1... | collective-permute-start | bytes 393224 | tf_op jit(solution)/shard_map/ppermute | solution.py:333
  90.9 1.4 %collective-permute-start.18 = (bf16[512,128]{1,0:T(8,128)(2,1)S(1)}, bf16[512,128]{1,0:T(8,128)(2,1)S(1)}, u32[]{:S(2)}, u32[]{:S(2)}) collective-permute-start(bf16[512,128]{1,0:T(8,128)(2,1)S(1)} %add.51.mine), channel_id=1, source_target_pairs={{0,1},{1,0},{2,3},{3,2},{4,5},{5,4},{6,7},{7,6},{8,9},{9,8},{10,11... | collective-permute-start | bytes 393224 | tf_op jit(solution)/shard_map/ppermute | solution.py:333
